TPU v7x, 256 devices: a whole 4x4x8 slice. The times are simulated.
256 devices in a mesh: ent: 64 (over x, z, core), rel: 4 (over y).
Axes of the slice: x: 4, y: 4, z: 8, core: 2. Of those that a mesh axis runs over, the one named last changes fastest.
Arguments:
- state_zero: bfloat16 [65536, 256], P('ent'), may hold values from -6 to 6
- state_one: bfloat16 [65536, 256], P('ent'), may hold values from -6 to 6
- aggregate_one: bfloat16 [65536, 256], P('ent'), may hold values from -6 to 6
- aggregate_two: bfloat16 [65536, 256], P('ent'), may hold values from -6 to 6
- cotangent: bfloat16 [65536, 256], P('ent'), may hold values from -6 to 6
- relation_table: bfloat16 [1312, 256], P('rel'), may hold values from -6 to 6
- update_in: bfloat16 [2, 64, 256], replicated, may hold values from -0.75 to 0.75
- update_bias: float32 [2, 256], replicated, may hold values from -3 to 3
- update_out: bfloat16 [2, 256, 32], replicated, may hold values from -0.375 to 0.375
- frontier_tiles: int32 [2, 128], P(None, 'ent'), may hold values from 0 to 7, as said below
- frontier_count: int32 [2, 64], P(None, 'ent'), may hold values from 1 to 2, as said below
- edge_source: int32 [262144], P(('ent', 'rel')), may hold values from 0 to 1023
- edge_relation: int32 [262144], P(('ent', 'rel')), may hold values from 0 to 327
- edge_target: int32 [262144], P(('ent', 'rel')), may hold values from 0 to 1023
- edge_owner: int32 [262144, 1], P(('ent', 'rel')), may hold values from 0 to 63; in each aligned block of 1024 rows (0 to 1023, 1024 to 2047, ...) at most 24 rows name the same one
Outputs:
- grad_state_zero: bfloat16 [65536, 256], P(('ent', 'rel'))
- grad_relation: float32 [1312, 256], P('rel')
- grad_update_in: float32 [2, 64, 256], replicated
- grad_update_bias: float32 [2, 256], replicated
- grad_update_out: float32 [2, 256, 32], replicated
Inputs may be any that keep to these rules, and one draw needn't show every extreme that they name: `frontier_tiles`: within one owner's 2 slots of a hop the tile numbers are distinct, padded slots included. The first frontier_count entries of an owner's list are its live tiles; in each hop some owner has all 2 live. `edge_owner`: among the 1024 edges of one device at most 24 name the same owner, and in some device some owner is named by exactly 24.
All inputs are finite; a program needn't handle non-finite values.
Results may differ from a plain program's by a relative error of at most 0.009.
Values may be sent and summed in bfloat16 or wider, within the bound.
No kernel may reach another device: no remote copies, remote signals or barrier semaphores. Data moves between devices by JAX's collectives and lax.ppermute only.
A program may use at most 64 MiB of HBM per device.

v0:
```python
import math

import jax
import jax.numpy as jnp
from jax import lax
from jax.sharding import PartitionSpec as P

QUERIES = 8
DIM = 32
TILE = 128


def frontier_rows(tile_ids, live_count, tile_total):
    slot_valid = jnp.arange(tile_ids.shape[0], dtype=jnp.int32) < live_count
    tile_range = jnp.arange(tile_total, dtype=jnp.int32)
    matched = (tile_ids[None, :] == tile_range[:, None]) & slot_valid[None, :]
    return jnp.repeat(jnp.any(matched, axis=1).astype(jnp.float32), TILE)


def exact_pick_sum(selector, values, contract_dim):
    high_part = values.astype(jnp.bfloat16)
    low_part = (values - high_part.astype(jnp.float32)).astype(jnp.bfloat16)
    numbers = (((contract_dim,), (0,)), ((), ()))
    first = lax.dot_general(selector, high_part, numbers, preferred_element_type=jnp.float32)
    second = lax.dot_general(selector, low_part, numbers, preferred_element_type=jnp.float32)
    return first + second


def update_backward(aggregate, state, upstream, update_in, update_bias, update_out):
    row_count = aggregate.shape[0]
    inputs = jnp.concatenate(
        [aggregate.reshape(row_count, QUERIES, DIM), state.reshape(row_count, QUERIES, DIM)], axis=2
    )
    pre_act = (
        jnp.einsum("nqd,de->nqe", inputs, update_in, preferred_element_type=jnp.float32)
        + update_bias
    )
    gate_value = jax.nn.sigmoid(pre_act)
    activated = (pre_act * gate_value).astype(jnp.bfloat16)
    slope = gate_value * (1.0 + pre_act * (1.0 - gate_value))
    upstream_low = upstream.astype(jnp.bfloat16).reshape(row_count, QUERIES, DIM)
    grad_act = jnp.einsum(
        "nqd,ed->nqe", upstream_low, update_out, preferred_element_type=jnp.float32
    )
    grad_pre = grad_act * slope
    grad_pre_low = grad_pre.astype(jnp.bfloat16)
    grad_out = jnp.einsum(
        "nqe,nqd->ed", activated, upstream_low, preferred_element_type=jnp.float32
    )
    grad_bias = jnp.sum(grad_pre, axis=(0, 1))
    grad_in = jnp.einsum("nqd,nqe->de", inputs, grad_pre_low, preferred_element_type=jnp.float32)
    grad_inputs = jnp.einsum(
        "nqe,de->nqd", grad_pre_low, update_in, preferred_element_type=jnp.float32
    )
    grad_agg = grad_inputs[:, :, :DIM].reshape(row_count, QUERIES * DIM).astype(jnp.bfloat16)
    grad_state = grad_inputs[:, :, DIM:].reshape(row_count, QUERIES * DIM)
    return (grad_agg, grad_state, grad_in, grad_bias, grad_out)


def mlp_blocks(aggregate, state, upstream, update_in, update_bias, update_out):
    row_count = aggregate.shape[0]
    feature_width = aggregate.shape[1]
    block_rows = math.gcd(row_count, 512)
    block_count = row_count // block_rows

    def step(carry, pieces):
        grad_agg, grad_state, grad_in, grad_bias, grad_out = update_backward(
            pieces[0], pieces[1], pieces[2], update_in, update_bias, update_out
        )
        return (
            (carry[0] + grad_in, carry[1] + grad_bias, carry[2] + grad_out),
            (grad_agg, grad_state),
        )

    initial = (
        jnp.zeros(update_in.shape, jnp.float32),
        jnp.zeros(update_bias.shape, jnp.float32),
        jnp.zeros(update_out.shape, jnp.float32),
    )
    stacked = tuple(
        (
            source_array.reshape(block_count, block_rows, feature_width)
            for source_array in (aggregate, state, upstream)
        )
    )
    sums, (grad_agg, grad_state) = lax.scan(step, initial, stacked)
    return (
        grad_agg.reshape(row_count, feature_width),
        grad_state.reshape(row_count, feature_width),
        sums,
    )


def shards(
    state_zero,
    state_one,
    aggregate_one,
    aggregate_two,
    cotangent,
    relation_table,
    update_in,
    update_bias,
    update_out,
    frontier_tiles,
    frontier_count,
    edge_source,
    edge_relation,
    edge_target,
    edge_owner,
):
    block_rows = state_zero.shape[0]
    feature_width = state_zero.shape[1]
    group_size = lax.axis_size("rel")
    peer_count = lax.axis_size("ent")
    quarter = block_rows // group_size
    quarter_start = lax.axis_index("rel") * quarter
    edge_count = edge_source.shape[0]
    capacity = 3 * edge_count // (2 * peer_count)
    tile_total = block_rows // TILE
    group_width = relation_table.shape[0]
    edge_peer = edge_owner[:, 0]
    onehot = (edge_peer[:, None] == jnp.arange(peer_count, dtype=jnp.int32)[None, :]).astype(
        jnp.int32
    )
    earlier = jnp.sum((jnp.cumsum(onehot, axis=0) - onehot) * onehot, axis=1)
    edge_slot = edge_peer * capacity + earlier
    request = jnp.zeros((peer_count * capacity,), jnp.int32).at[edge_slot].set(edge_target)
    asked = lax.all_to_all(
        request.reshape(peer_count, capacity), "ent", split_axis=0, concat_axis=0, tiled=True
    )
    source_select = (
        jnp.arange(block_rows, dtype=jnp.int32)[:, None] == edge_source[None, :]
    ).astype(jnp.bfloat16)
    relation_select = (
        edge_relation[:, None] == jnp.arange(group_width, dtype=jnp.int32)[None, :]
    ).astype(jnp.bfloat16)
    edge_table = jnp.dot(relation_select, relation_table, preferred_element_type=jnp.float32)
    upstream = cotangent.astype(jnp.float32)
    relation_grad = jnp.zeros((group_width, feature_width), jnp.float32)
    layer_sums = [None, None]
    for aggregate, state, layer in ((aggregate_two, state_one, 1), (aggregate_one, state_zero, 0)):
        grad_agg, grad_state, sums = mlp_blocks(
            aggregate, state, upstream, update_in[layer], update_bias[layer], update_out[layer]
        )
        picked = grad_agg[asked]
        answered = lax.all_to_all(picked, "ent", split_axis=0, concat_axis=0, tiled=True)
        served = answered.reshape(peer_count * capacity, feature_width)[edge_slot]
        tile_ids = frontier_tiles[layer]
        row_mask = frontier_rows(tile_ids, frontier_count[layer, 0], tile_total)
        weighted = served.astype(jnp.float32) * row_mask[edge_source][:, None]
        contrib = exact_pick_sum(source_select, weighted * edge_table, 1)
        relation_grad = relation_grad + exact_pick_sum(
            relation_select, weighted * state[edge_source].astype(jnp.float32), 0
        )
        source_grad = lax.psum(contrib.astype(jnp.bfloat16), "rel").astype(jnp.float32)
        upstream = upstream + grad_state + source_grad
        layer_sums[layer] = sums
    stacked_in = jnp.stack([layer_sums[0][0], layer_sums[1][0]])
    stacked_bias = jnp.stack([layer_sums[0][1], layer_sums[1][1]])
    stacked_out = jnp.stack([layer_sums[0][2], layer_sums[1][2]])
    grad_in_all, grad_bias_all, grad_out_all, relation_total = lax.psum(
        (stacked_in, stacked_bias, stacked_out, relation_grad), "ent"
    )
    scale_weights = 1.0 / math.sqrt(block_rows * peer_count * QUERIES)
    scale_relations = math.sqrt(group_width * group_size / (edge_count * peer_count * group_size))
    return (
        lax.dynamic_slice_in_dim(upstream, quarter_start, quarter, 0).astype(jnp.bfloat16),
        relation_total * scale_relations,
        grad_in_all * scale_weights,
        grad_bias_all * scale_weights,
        grad_out_all * scale_weights,
    )


def solution(mesh):
    in_specs = (
        P("ent", None),
        P("ent", None),
        P("ent", None),
        P("ent", None),
        P("ent", None),
        P("rel", None),
        P(),
        P(),
        P(),
        P(None, "ent"),
        P(None, "ent"),
        P(("ent", "rel")),
        P(("ent", "rel")),
        P(("ent", "rel")),
        P(("ent", "rel"), None),
    )
    out_specs = (P(("ent", "rel"), None), P("rel", None), P(), P(), P())
    return jax.shard_map(shards, mesh=mesh, in_specs=in_specs, out_specs=out_specs, check_vma=False)
```

profile of v0, /device:TPU:1, one launch (start us, length us, event | category | flops | bytes accessed | tf_op | source)
XLA Modules:
  0.0 625.6 jit_solution(3884639619966283850)
XLA Ops:
  7.9 18.0 %reduce-window.6 = s32[64,8,128]{2,1,0:T(8,128)S(1)} reduce-window(s32[64,8,128]{2,1,0:T(8,128)S(1)} %fusion.77, s32[]{:T(128)} %constant.31.clone.1), window={size=1x1x128 pad=0_0x0_0x127_0}, to_apply=%region_3.4 | reduce-window | flops 8323072 | bytes 524292 | tf_op jit(solution)/shard_map/reduce-window
  28.0 4.5 scatter_custom_fusion
  33.1 13.0 %all-to-all-start = ((s32[64,1,24]{2,1,0:T(1,128)}), s32[64,1,24]{2,1,0:T(1,128)S(1)}, u32[]{:S(2)}, u32[]{:S(2)}) async-start(s32[64,1,24]{2,1,0:T(1,128)} %bitcast.13), calls=%async_computation | async-start | bytes 65536 | tf_op jit(solution)/shard_map/all_to_all | solution.py:128
  50.7 36.2 %while.38 = (s32[]{:T(128)}, f32[64,256]{1,0:T(8,128)S(1)}, f32[256]{0:T(256)S(1)}, f32[256,32]{0,1:T(8,128)S(1)}, bf16[2,512,256]{2,1,0:T(8,128)(2,1)S(1)}, /*i...) while((s32[]{:T(128)}, f32[64,256]{1,0:T(8,128)S(1)}, ...), condition=%wide.region_2.3_spmd.clone, body=%wide.region_0.2_spmd.clone.sunk | while | flops 556843264 | bytes 33839300 | solution.py:86
  56.6 4.0 fusion.123
  74.6 4.0 fusion.123
  87.0 5.4 gather_fusion
  92.4 10.4 %all-to-all-start.1 = ((bf16[64,24,256]{2,1,0:T(8,128)(2,1)}), bf16[64,24,256]{2,1,0:T(8,128)(2,1)S(1)}, u32[]{:S(2)}, u32[]{:S(2)}) async-start(bf16[64,24,256]{2,1,0:T(8,128)(2,1)} %bitcast.15), calls=%async_computation.1 | async-start | bytes 1572864 | tf_op jit(solution)/shard_map/all_to_all | solution.py:146
  105.7 4.5 gather_fusion.2
  110.7 15.0 %all-to-all-done.1 = bf16[64,24,256]{2,1,0:T(8,128)(2,1)S(1)} async-done(((bf16[64,24,256]{2,1,0:T(8,128)(2,1)}), bf16[64,24,256]{2,1,0:T(8,128)(2,1)S(1)}, u32[]{:S(2)}, u32[]{:S(2)}) %all-to-all-start.1) | async-done | bytes 786464 | tf_op jit(solution)/shard_map/all_to_all | solution.py:146
  125.7 3.9 gather_fusion.1
  132.5 43.2 %all-reduce.5.cloned.1.call-done = bf16[1024,256]{1,0:T(8,128)(2,1)} async-done(((bf16[1024,256]{1,0:T(8,128)(2,1)}), bf16[1024,256]{1,0:T(8,128)(2,1)}) %all-reduce.5.cloned.1.call-update) | async-done | bytes 524304 | tf_op jit(solution)/shard_map/psum | solution.py:155
  179.5 35.8 %while.39 = (s32[]{:T(128)}, f32[64,256]{1,0:T(8,128)S(1)}, f32[256]{0:T(256)S(1)}, f32[256,32]{0,1:T(8,128)S(1)}, bf16[2,512,256]{2,1,0:T(8,128)(2,1)S(1)}, /*i...) while((s32[]{:T(128)}, f32[64,256]{1,0:T(8,128)S(1)}, ...), condition=%wide.region_11.12_spmd.clone, body=%wide.region_9.11_spmd.clone.sunk | while | flops 556843264 | bytes 33839300 | solution.py:86
  185.4 4.0 fusion.134
  203.3 4.0 fusion.134
  215.3 5.4 gather_fusion.3
  220.6 12.8 %all-to-all-start.2 = ((bf16[64,24,256]{2,1,0:T(8,128)(2,1)}), bf16[64,24,256]{2,1,0:T(8,128)(2,1)S(1)}, u32[]{:S(2)}, u32[]{:S(2)}) async-start(bf16[64,24,256]{2,1,0:T(8,128)(2,1)} %bitcast.27), calls=%async_computation.2 | async-start | bytes 1572864 | tf_op jit(solution)/shard_map/all_to_all | solution.py:146
  233.8 5.7 gather_fusion.7
  239.5 4.6 gather_fusion.6
  244.2 4.5 gather_fusion.5
  250.5 124.1 %psum.46 = f32[2,256]{1,0:T(2,128)S(1)} all-reduce(f32[2,256]{1,0:T(2,128)S(1)} %pad_maximum_fusion.8), channel_id=1, replica_groups=mesh['ent'=64,'rel'=4] {'ent'}, use_global_device_ids=true, to_apply=%region_16.17 | all-reduce | flops 512 | bytes 4096 | tf_op jit(solution)/shard_map/psum | solution.py:161
  376.4 4.9 gather_fusion.4
  392.4 176.6 %all-reduce.9.cloned.1.call-done = (f32[328,256]{1,0:T(8,128)}, f32[2,64,256]{2,1,0:T(8,128)}, f32[2,256,32]{1,2,0:T(8,128)}) async-done(((f32[328,256]{1,0:T(8,128)}, f32[2,64,256]{2,1,0:T(8,128)}, f32[2,256,32]{1,2,0:T(8,128)}), (f32[328,256]{1,0:T(8,128)}, f32[2,64,256]{2,1,0:T(8,128)}, f32[2,256,32]{1,2,0:T(8,128)})) %all-reduce.9.cloned.1.call-update) | async-done | bytes 532496 | tf_op jit(solution)/shard_map/psum | solution.py:161
  573.8 43.5 %all-reduce.7.cloned.1.call-done = bf16[1024,256]{1,0:T(8,128)(2,1)} async-done(((bf16[1024,256]{1,0:T(8,128)(2,1)}), bf16[1024,256]{1,0:T(8,128)(2,1)}) %all-reduce.7.cloned.1.call-update) | async-done | bytes 524304 | tf_op jit(solution)/shard_map/psum | solution.py:155
  (178 shorter events, 94.9 us)
Async XLA Ops:
  7.2 103.1 %copy-start = (bf16[328,256]{1,0:T(8,128)(2,1)S(1)}, bf16[328,256]{1,0:T(8,128)(2,1)}, u32[]{:S(2)}) copy-start(bf16[328,256]{1,0:T(8,128)(2,1)} %param.24) | copy-start | bytes 503812
  33.1 53.7 %all-to-all-start = ((s32[64,1,24]{2,1,0:T(1,128)}), s32[64,1,24]{2,1,0:T(1,128)S(1)}, u32[]{:S(2)}, u32[]{:S(2)}) async-start(s32[64,1,24]{2,1,0:T(1,128)} %bitcast.13), calls=%async_computation | async-start | bytes 65536 | tf_op jit(solution)/shard_map/all_to_all | solution.py:128
  86.8 5.5 copy-start.11
  87.0 16.1 %copy-start.19 = (s32[2,1]{0,1:T(1,128)S(1)}, s32[2,1]{0,1:T(1,128)}, u32[]{:S(2)}) copy-start(s32[2,1]{0,1:T(1,128)} %param.29) | copy-start | bytes 28
  87.0 18.0 %copy-start.20 = (s32[2,2]{1,0:T(2,128)S(1)}, s32[2,2]{1,0:T(2,128)}, u32[]{:S(2)}) copy-start(s32[2,2]{1,0:T(2,128)} %param.28) | copy-start | bytes 52
  87.0 18.7 %copy-start.15 = (s32[1024]{0:T(1024)S(1)}, s32[1024]{0:T(1024)}, u32[]{:S(2)}) copy-start(s32[1024]{0:T(1024)} %param.30) | copy-start | bytes 12292
  92.3 17.9 %copy-start.13 = (s32[1024]{0:T(1024)S(1)}, s32[1024]{0:T(1024)}, u32[]{:S(2)}) copy-start(s32[1024]{0:T(1024)} %param.31) | copy-start | bytes 12292
  92.4 33.4 %all-to-all-start.1 = ((bf16[64,24,256]{2,1,0:T(8,128)(2,1)}), bf16[64,24,256]{2,1,0:T(8,128)(2,1)S(1)}, u32[]{:S(2)}, u32[]{:S(2)}) async-start(bf16[64,24,256]{2,1,0:T(8,128)(2,1)} %bitcast.15), calls=%async_computation.1 | async-start | bytes 1572864 | tf_op jit(solution)/shard_map/all_to_all | solution.py:146
  102.8 72.9 %all-reduce.5.cloned.1.call-start = ((), (), s32[]{:S(2)}) async-start(), calls=%async_computation.3 | async-start | bytes 1048576 | tf_op jit(solution)/shard_map/psum | solution.py:155
  110.2 20.5 %copy-start.17 = (f32[1024]{0:T(1024)}, f32[1024]{0:T(1024)S(1)}, u32[]{:S(2)}) copy-start(f32[1024]{0:T(1024)S(1)} %gather_fusion.2) | copy-start | bytes 12292
  110.7 20.0 %copy-start.5 = (f32[1024,256]{1,0:T(8,128)}, f32[1024,256]{1,0:T(8,128)S(1)}, u32[]{:S(2)}) copy-start(f32[1024,256]{1,0:T(8,128)S(1)} %fusion.40) | copy-start | bytes 3145732
  129.7 46.0 %copy-start.4 = (f32[2,512,256]{2,1,0:T(8,128)S(1)}, f32[2,512,256]{2,1,0:T(8,128)}, u32[]{:S(2)}) copy-start(f32[2,512,256]{2,1,0:T(8,128)} %get-tuple-element.137) | copy-start | bytes 3145732
  220.6 155.8 %all-to-all-start.2 = ((bf16[64,24,256]{2,1,0:T(8,128)(2,1)}), bf16[64,24,256]{2,1,0:T(8,128)(2,1)S(1)}, u32[]{:S(2)}, u32[]{:S(2)}) async-start(bf16[64,24,256]{2,1,0:T(8,128)(2,1)} %bitcast.27), calls=%async_computation.2 | async-start | bytes 1572864 | tf_op jit(solution)/shard_map/all_to_all | solution.py:146
  233.5 335.5 %all-reduce.9.cloned.1.call-start = ((), (), s32[]{:S(2)}) async-start(), calls=%async_computation.5 | async-start | bytes 1064960 | tf_op jit(solution)/shard_map/psum | solution.py:161
  233.8 10.4 %copy-start.21 = (pred[8]{0:T(512)(128)(4,1)S(1)}, pred[8]{0:T(512)(128)(4,1)}, u32[]{:S(2)}) copy-start(pred[8]{0:T(512)(128)(4,1)} %get-tuple-element.390) | copy-start | bytes 28
  239.5 9.3 %copy-start.8 = (bf16[1024,256]{1,0:T(8,128)(2,1)S(1)}, bf16[1024,256]{1,0:T(8,128)(2,1)}, u32[]{:S(2)}) copy-start(bf16[1024,256]{1,0:T(8,128)(2,1)} %copy-done.7) | copy-start | bytes 1572868
  239.5 9.3 %copy-start.14 = (s32[1024]{0:T(1024)S(1)}, s32[1024]{0:T(1024)}, u32[]{:S(2)}) copy-start(s32[1024]{0:T(1024)} %param.31) | copy-start | bytes 12292
  239.5 9.3 %copy-start.18 = (f32[1024]{0:T(1024)S(1)}, f32[1024]{0:T(1024)}, u32[]{:S(2)}) copy-start(f32[1024]{0:T(1024)} %copy-done.17) | copy-start | bytes 12292
  244.1 130.5 %copy-start.12 = (f32[256,32]{0,1:T(8,128)S(1)}, f32[256,32]{0,1:T(8,128)}, u32[]{:S(2)}) copy-start(f32[256,32]{0,1:T(8,128)} %copy-done.11) | copy-start | bytes 98308
  248.7 132.7 %copy-start.6 = (f32[1024,256]{1,0:T(8,128)S(1)}, f32[1024,256]{1,0:T(8,128)}, u32[]{:S(2)}) copy-start(f32[1024,256]{1,0:T(8,128)} %copy-done.5) | copy-start | bytes 3145732
  248.7 132.6 %copy-start.16 = (s32[1024]{0:T(1024)S(1)}, s32[1024]{0:T(1024)}, u32[]{:S(2)}) copy-start(s32[1024]{0:T(1024)} %param.30) | copy-start | bytes 12292
  381.4 5.3 copy-start.10
  381.4 6.2 copy-start.22
  389.3 228.0 %all-reduce.7.cloned.1.call-start = ((), (), s32[]{:S(2)}) async-start(), calls=%async_computation.4 | async-start | bytes 1048576 | tf_op jit(solution)/shard_map/psum | solution.py:155
  (7 other events, 13.3 us)
Sparse Core Ops, SparseCore 0:
  132.6 43.0 all-reduce.4
  389.4 179.5 all-reduce.8
  571.4 45.8 all-reduce.6
where the time goes:
time: 628 us; the launch traced here: 626 us
  waiting for transfers between devices  278 us (44%)
  blocking collectives  124 us (20%)
  local copies, waits for them, and re-layouts  77.1 us (12%)
  matrix products  61.5 us (10%)
  starting transfers between devices  36.8 us (6%)
  other arithmetic  33.2 us (5%)
  between operations  14.3 us (2%)
    psum x1, waiting for transfers between devices, shards(): lax.psum((stacked_in, stacked_bias, stacked_out, relation_grad), 'ent')  177 us
    psum x1, blocking collectives, shards(): lax.psum((stacked_in, stacked_bias, stacked_out, relation_grad), 'ent')  124 us
    psum x2, waiting for transfers between devices, shards(): lax.psum(contrib.astype(jnp.bfloat16), 'rel').astype(jnp.float32)  86.6 us
    all_to_all x2, starting transfers between devices, shards(): lax.all_to_all(picked, 'ent', split_axis=0, concat_axis=0, tiled=True)  23.3 us
    another operation x3, other arithmetic  18.2 us
    dot_general x4, matrix products, update_backward(): jnp.einsum('nqd,ed->nqe', upstream_low, update_out, preferred_element_typ...  16 us
    all_to_all x2, waiting for transfers between devices, shards(): lax.all_to_all(picked, 'ent', split_axis=0, concat_axis=0, tiled=True)  15 us
    dot_general x4, matrix products, update_backward(): jnp.einsum('nqe,nqd->ed', activated, upstream_low, preferred_element_type...  13.9 us
  transfers between devices with their start and end apart: 6, of which 4 were waited for; matrix products, arithmetic and copies ran while one was open for 12% of the time, Pallas kernels for 0%

commit v1 on v0

v1 whole, which is shorter than its diff:
```python
import functools
import math

import jax
import jax.numpy as jnp
from jax import lax
from jax.experimental import pallas as pl
from jax.experimental.pallas import tpu as pltpu
from jax.sharding import PartitionSpec as P

QUERIES = 8
DIM = 32
TILE = 128
WIDE = 256
HALF_Q = 4
F32 = jnp.float32
BF16 = jnp.bfloat16
VMEM = pl.BlockSpec(memory_space=pltpu.VMEM)
SMEM = pl.BlockSpec(memory_space=pltpu.SMEM)


def iota(shape, dim):
    return lax.broadcasted_iota(jnp.int32, shape, dim)


def dot_nn(a, b):
    return lax.dot_general(a, b, (((1,), (0,)), ((), ())), preferred_element_type=F32)


def dot_nt(a, b):
    return lax.dot_general(a, b, (((1,), (1,)), ((), ())), preferred_element_type=F32)


def dot_tn(a, b):
    return lax.dot_general(a, b, (((0,), (0,)), ((), ())), preferred_element_type=F32)


def params(vmem=60 << 20):
    return pltpu.CompilerParams(vmem_limit_bytes=vmem)


def cost(flops, nbytes, trans=0):
    return pl.CostEstimate(flops=int(flops), bytes_accessed=int(nbytes), transcendentals=int(trans))


def slots_kernel(peers, owner_ref, target_ref, source_ref, relation_ref, request_ref, ids_ref):
    edges = owner_ref.shape[1]
    owner = owner_ref[...]
    hit = (iota((peers, edges), 0) == owner).astype(F32)
    hit_low = hit.astype(BF16)
    below = (iota((TILE, TILE), 0) < iota((TILE, TILE), 1)).astype(BF16)
    offset = jnp.zeros((peers, 1), F32)
    pieces = []
    for b in range(edges // TILE):
        block = hit_low[:, b * TILE:(b + 1) * TILE]
        pieces.append(dot_nn(block, below) + offset)
        offset = offset + jnp.sum(hit[:, b * TILE:(b + 1) * TILE], axis=1, keepdims=True)
    before = jnp.concatenate(pieces, axis=1)
    earlier = jnp.sum(before * hit, axis=0, keepdims=True).astype(jnp.int32)
    place = (iota((32, edges), 0) == earlier).astype(F32)

    def spread(values):
        high = lax.shift_right_logical(values, 5)
        low = values & 31
        return [place * high.astype(F32), place * low.astype(F32)]

    zero = jnp.zeros((64, edges), F32)
    first = jnp.concatenate(spread(target_ref[...]) + [zero], axis=0).astype(BF16)
    request_ref[:, 0, :] = dot_nt(hit_low, first)
    second = jnp.concatenate(
        spread(source_ref[...] + 1) + spread(relation_ref[...] + 1), axis=0
    ).astype(BF16)
    ids_ref[...] = dot_nt(hit_low, second)


def slot_columns(table, capacity, bases):
    peers = table.shape[0]
    slots = peers * capacity
    row = iota((slots, peers), 0)
    start = iota((slots, peers), 1) * capacity
    expand = ((row >= start) & (row < start + capacity)).astype(BF16)
    spread = dot_nn(expand, table.astype(BF16))
    row = iota((slots, 128), 0)
    group = ((row.astype(F32) + 0.5) * (1.0 / capacity)).astype(jnp.int32)
    place = row - group * capacity
    lane = iota((slots, 128), 1)
    columns = []
    for base in bases:
        weight = jnp.where(lane == place + base, 32.0, 0.0) + jnp.where(
            lane == place + (base + 32), 1.0, 0.0
        )
        columns.append(jnp.sum(spread * weight, axis=1, keepdims=True).astype(jnp.int32))
    return columns


def compact_column(column, tiles, count):
    tile = lax.shift_right_arithmetic(column, 7)
    inner = column & 127
    result = jnp.full(column.shape, -1, jnp.int32)
    for k in range(len(tiles)):
        live = (tile == tiles[k]) & (count > k)
        result = jnp.where(live, inner + k * TILE, result)
    return result


def onehot(column, width):
    return (iota((column.shape[0], width), 1) == column).astype(F32).astype(BF16)


def build_weights(w_in_ref, w_bias_ref, w_out_ref, wx_ref, wu_ref, wb_ref):
    wx_ref[...] = jnp.zeros_like(wx_ref)
    wu_ref[...] = jnp.zeros_like(wu_ref)
    eye = (iota((DIM, DIM), 0) == iota((DIM, DIM), 1)).astype(BF16)
    w_out_t = dot_nt(eye, w_out_ref[...]).astype(BF16)
    for q in range(HALF_Q):
        rows, cols = slice(q * DIM, (q + 1) * DIM), slice(q * WIDE, (q + 1) * WIDE)
        low = slice(TILE + q * DIM, TILE + (q + 1) * DIM)
        wx_ref[rows, cols] = w_in_ref[0:DIM, :]
        wx_ref[low, cols] = w_in_ref[DIM:2 * DIM, :]
        wu_ref[rows, cols] = w_out_t
        wb_ref[:, cols] = w_bias_ref[...]


def mlp_half(s, agg, state, up_low, wx, wu, bias, acc_in, acc_out, acc_bias):
    lanes = slice(s * TILE, (s + 1) * TILE)
    x = jnp.concatenate([agg[:, lanes], state[:, lanes]], axis=1)
    up = up_low[:, lanes]
    pre = dot_nn(x, wx[...]) + bias[...]
    gate = 0.5 * jnp.tanh(0.5 * pre) + 0.5
    act = pre * gate
    slope = gate + act * (1.0 - gate)
    grad_pre = dot_nn(up, wu[...]) * slope
    low = grad_pre.astype(BF16)
    acc_in[...] += dot_tn(x, low)
    acc_out[...] += dot_tn(up, act.astype(BF16))
    acc_bias[...] += jnp.sum(grad_pre, axis=0, keepdims=True)
    return dot_nt(low, wx[...])


def store_sums(acc_in, acc_out, acc_bias, sums_ref):
    first = jnp.zeros((DIM, WIDE), F32)
    second = jnp.zeros((DIM, WIDE), F32)
    third = jnp.zeros((DIM, WIDE), F32)
    fourth = jnp.zeros((1, WIDE), F32)
    for q in range(HALF_Q):
        cols = slice(q * WIDE, (q + 1) * WIDE)
        first += acc_in[q * DIM:(q + 1) * DIM, cols]
        second += acc_in[TILE + q * DIM:TILE + (q + 1) * DIM, cols]
        third += acc_out[q * DIM:(q + 1) * DIM, cols]
        fourth += acc_bias[:, cols]
    sums_ref[0:DIM, :] = first
    sums_ref[DIM:2 * DIM, :] = second
    sums_ref[2 * DIM:3 * DIM, :] = third
    sums_ref[3 * DIM:3 * DIM + 8, :] = jnp.concatenate([fourth, jnp.zeros((7, WIDE), F32)], axis=0)


def clear(acc_in, acc_out, acc_bias):
    acc_in[...] = jnp.zeros_like(acc_in)
    acc_out[...] = jnp.zeros_like(acc_out)
    acc_bias[...] = jnp.zeros_like(acc_bias)


MLP_SCRATCH = [
    pltpu.VMEM((256, HALF_Q * WIDE), BF16),
    pltpu.VMEM((TILE, HALF_Q * WIDE), BF16),
    pltpu.VMEM((1, HALF_Q * WIDE), F32),
    pltpu.VMEM((256, HALF_Q * WIDE), F32),
    pltpu.VMEM((TILE, HALF_Q * WIDE), F32),
    pltpu.VMEM((1, HALF_Q * WIDE), F32),
]
SUM_ROWS = 3 * DIM + 8


def pick_rows(asked, grad_agg, picked_ref, chunks=4):
    rows, slots = grad_agg.shape[0], asked.shape[0]
    step = slots // chunks
    for c in range(chunks):
        part = slice(c * step, (c + 1) * step)
        picked_ref[part, :] = dot_nn(onehot(asked[part], rows), grad_agg[...]).astype(BF16)


def dense_kernel(capacity, masked, tiles_ref, count_ref, agg_ref, state_ref, up_ref, w_in_ref,
                 w_bias_ref, w_out_ref, asked_ref, next_ref, picked_ref, sums_ref,
                 wx, wu, wb, acc_in, acc_out, acc_bias, grad_agg):
    step = pl.program_id(0)
    rows = agg_ref.shape[0]

    @pl.when(step == 0)
    def _():
        build_weights(w_in_ref, w_bias_ref, w_out_ref, wx, wu, wb)
        clear(acc_in, acc_out, acc_bias)

    up = up_ref[...].astype(F32)
    up_low = up_ref[...].astype(BF16)
    if masked:
        tile = lax.shift_right_logical(iota((rows, 1), 0) + step * rows, 7)
        dead = (tile == tiles_ref[1, 0]) | ((tile == tiles_ref[1, 1]) & (count_ref[1, 0] > 1))
        up_low = jnp.where(dead, 0.0, up).astype(BF16)
    aggs, states = [], []
    for s in range(2):
        grad_x = mlp_half(s, agg_ref[...], state_ref[...], up_low, wx, wu, wb, acc_in, acc_out, acc_bias)
        aggs.append(grad_x[:, :TILE])
        states.append(grad_x[:, TILE:])
    grad_agg[pl.ds(pl.multiple_of(step * rows, rows), rows), :] = jnp.concatenate(aggs, axis=1).astype(BF16)
    next_ref[...] = up + jnp.concatenate(states, axis=1)

    @pl.when(step == pl.num_programs(0) - 1)
    def _():
        store_sums(acc_in, acc_out, acc_bias, sums_ref)
        asked = slot_columns(asked_ref[:, 0, :], capacity, (0,))[0]
        pick_rows(asked, grad_agg, picked_ref)


def dense_pass(masked, capacity, tiles, count, agg, state, up, w_in, w_bias, w_out, asked):
    rows, feat = agg.shape
    slots = asked.shape[0] * capacity
    block = 256
    row_spec = pl.BlockSpec((block, feat), lambda i: (i, 0))

    def whole(shape):
        return pl.BlockSpec(shape, lambda i: (0,) * len(shape))

    return pl.pallas_call(
        functools.partial(dense_kernel, capacity, masked),
        grid=(rows // block,),
        in_specs=[SMEM, SMEM, row_spec, row_spec, row_spec, whole(w_in.shape), whole(w_bias.shape),
                  whole(w_out.shape), whole(asked.shape)],
        out_specs=[row_spec, whole((slots, feat)), whole((SUM_ROWS, WIDE))],
        out_shape=[
            jax.ShapeDtypeStruct((rows, feat), F32),
            jax.ShapeDtypeStruct((slots, feat), BF16),
            jax.ShapeDtypeStruct((SUM_ROWS, WIDE), F32),
        ],
        scratch_shapes=MLP_SCRATCH + [pltpu.VMEM((rows, feat), BF16)],
        compiler_params=params(),
        cost_estimate=cost(5.4e9, 4 << 20, 2 << 20),
        name="dense_masked" if masked else "dense",
    )(tiles, count, agg, state, up, w_in, w_bias, w_out, asked)


def tables_kernel(capacity, tiles_ref, count_ref, ids_ref, table_ref, one_a, one_b, zero_a, zero_b,
                  t_ref, s2_ref, h2_ref, s1_ref, h1_ref, r_ref):
    source, relation = slot_columns(ids_ref[...], capacity, (0, 64))
    source, relation = source - 1, relation - 1
    width = r_ref.shape[1]
    pad = width - table_ref.shape[0]
    table = jnp.concatenate([table_ref[...], jnp.zeros((pad, table_ref.shape[1]), BF16)], axis=0)
    select = onehot(relation, width)
    r_ref[...] = select
    t_ref[...] = dot_nn(select, table).astype(BF16)
    for hop, s_ref, h_ref, a, b in ((1, s2_ref, h2_ref, one_a, one_b), (0, s1_ref, h1_ref, zero_a, zero_b)):
        column = compact_column(source, (tiles_ref[hop, 0], tiles_ref[hop, 1]), count_ref[hop, 0])
        select = onehot(column, 2 * TILE)
        s_ref[...] = select
        h_ref[...] = dot_nn(select, jnp.concatenate([a[...], b[...]], axis=0)).astype(BF16)


def slot_tables(capacity, tiles, count, ids, table, state_one, state_zero):
    feat = table.shape[1]
    slots = ids.shape[0] * capacity
    width = -(-table.shape[0] // TILE) * TILE

    def whole(shape):
        return pl.BlockSpec(shape, lambda i, *_: (0,) * len(shape))

    def tile(hop, k):
        return pl.BlockSpec((TILE, feat), lambda i, tiles, count: (tiles[hop, k], 0))

    shape = jax.ShapeDtypeStruct((slots, feat), BF16)
    return pl.pallas_call(
        functools.partial(tables_kernel, capacity),
        grid_spec=pltpu.PrefetchScalarGridSpec(
            num_scalar_prefetch=2,
            grid=(1,),
            in_specs=[whole(ids.shape), whole(table.shape), tile(1, 0), tile(1, 1), tile(0, 0), tile(0, 1)],
            out_specs=[whole((slots, feat))] * 5 + [whole((slots, width))],
        ),
        out_shape=[shape] * 5 + [jax.ShapeDtypeStruct((slots, width), BF16)],
        compiler_params=params(),
        cost_estimate=cost(2e9, 6 << 20),
        name="tables",
    )(tiles, count, ids, table, state_one, state_one, state_zero, state_zero)


def contribution_kernel(answer_ref, t_ref, s_ref, out_ref):
    out_ref[...] = dot_tn(s_ref[...], answer_ref[...] * t_ref[...]).astype(BF16)


def contribution(answer, table, select):
    return pl.pallas_call(
        contribution_kernel,
        in_specs=[VMEM] * 3,
        out_specs=VMEM,
        out_shape=jax.ShapeDtypeStruct((select.shape[1], answer.shape[1]), BF16),
        compiler_params=params(),
        cost_estimate=cost(2e8, 3 << 20),
        name="contribution",
    )(answer, table, select)


def relation_kernel(answer_ref, h_ref, r_ref, out_ref):
    out_ref[...] = dot_tn(r_ref[...], answer_ref[...] * h_ref[...])


def relation_part(answer, states, select):
    return pl.pallas_call(
        relation_kernel,
        in_specs=[VMEM] * 3,
        out_specs=VMEM,
        out_shape=jax.ShapeDtypeStruct((select.shape[1], answer.shape[1]), F32),
        compiler_params=params(),
        cost_estimate=cost(4e8, 3 << 20),
        name="relation_part",
    )(answer, states, select)


def live_kernel(capacity, tiles_ref, count_ref, agg_a, agg_b, state_a, state_b, up_a, up_b, c0, c1, c2, c3,
                w_in_ref, w_bias_ref, w_out_ref, asked_ref, rest_ref, picked_ref, next_ref, sums_ref,
                wx, wu, wb, acc_in, acc_out, acc_bias):
    build_weights(w_in_ref, w_bias_ref, w_out_ref, wx, wu, wb)
    clear(acc_in, acc_out, acc_bias)
    count = count_ref[1, 0]
    source = (c0[...].astype(F32) + c1[...].astype(F32)) + (c2[...].astype(F32) + c3[...].astype(F32))
    up = jnp.concatenate([up_a[...], up_b[...]], axis=0) + source
    keep = (iota((2 * TILE, 1), 0) < TILE) | (count > 1)
    up_low = jnp.where(keep, up, 0.0).astype(BF16)
    agg = jnp.concatenate([agg_a[...], agg_b[...]], axis=0)
    state = jnp.concatenate([state_a[...], state_b[...]], axis=0)
    aggs, states = [], []
    for s in range(2):
        grad_x = mlp_half(s, agg, state, up_low, wx, wu, wb, acc_in, acc_out, acc_bias)
        aggs.append(grad_x[:, :TILE])
        states.append(grad_x[:, TILE:])
    grad_agg = jnp.concatenate(aggs, axis=1).astype(BF16)
    next_ref[...] = up + jnp.concatenate(states, axis=1)
    store_sums(acc_in, acc_out, acc_bias, sums_ref)
    asked = slot_columns(asked_ref[:, 0, :], capacity, (0,))[0]
    column = compact_column(asked, (tiles_ref[1, 0], tiles_ref[1, 1]), count)
    live = dot_nn(onehot(column, 2 * TILE), grad_agg)
    picked_ref[...] = jnp.where(column >= 0, live, rest_ref[...].astype(F32)).astype(BF16)


def live_pass(capacity, tiles, count, agg, state, up, parts, w_in, w_bias, w_out, asked, rest):
    feat = agg.shape[1]

    def whole(shape):
        return pl.BlockSpec(shape, lambda i, *_: (0,) * len(shape))

    def tile(k):
        return pl.BlockSpec((TILE, feat), lambda i, tiles, count: (tiles[1, k], 0))

    return pl.pallas_call(
        functools.partial(live_kernel, capacity),
        grid_spec=pltpu.PrefetchScalarGridSpec(
            num_scalar_prefetch=2,
            grid=(1,),
            in_specs=[tile(0), tile(1)] * 3 + [whole(parts[0].shape)] * 4
            + [whole(w_in.shape), whole(w_bias.shape), whole(w_out.shape), whole(asked.shape), whole(rest.shape)],
            out_specs=[whole(rest.shape), whole((2 * TILE, feat)), whole((SUM_ROWS, WIDE))],
            scratch_shapes=MLP_SCRATCH,
        ),
        out_shape=[
            jax.ShapeDtypeStruct(rest.shape, BF16),
            jax.ShapeDtypeStruct((2 * TILE, feat), F32),
            jax.ShapeDtypeStruct((SUM_ROWS, WIDE), F32),
        ],
        compiler_params=params(),
        cost_estimate=cost(1.6e9, 4 << 20, 1 << 19),
        name="live",
    )(tiles, count, agg, agg, state, state, up, up, *parts, w_in, w_bias, w_out, asked, rest)


GAP = SUM_ROWS


def pack_kernel(answer_ref, h_ref, r_ref, before_ref, w2_ref, w1a_ref, w1b_ref, out_ref):
    total = before_ref[...] + dot_tn(r_ref[...], answer_ref[...] * h_ref[...])
    used, rows = total.shape[0], out_ref.shape[0]
    feat = total.shape[1]
    out_ref[...] = jnp.zeros_like(out_ref)
    out_ref[0:used, 0:feat] = total.astype(BF16)
    layers = (w1a_ref[...] + w1b_ref[...], w2_ref[...])
    parts = []
    for layer in layers:
        parts += [layer[:, :TILE], layer[:, TILE:]]
    parts = jnp.concatenate(parts, axis=0).astype(BF16)
    out_ref[0:4 * GAP, feat:feat + TILE] = parts


def pack_sums(answer, states, select, before, w2, w1a, w1b, rows):
    feat = answer.shape[1]
    return pl.pallas_call(
        pack_kernel,
        in_specs=[VMEM] * 7,
        out_specs=VMEM,
        out_shape=jax.ShapeDtypeStruct((rows, feat + TILE), BF16),
        compiler_params=params(),
        cost_estimate=cost(4e8, 4 << 20),
        name="pack_sums",
    )(answer, states, select, before, w2, w1a, w1b)


def combine_kernel(feat, scale_relations, scale_weights, in_ref, out_ref):
    total = jnp.sum(in_ref[...].astype(F32), axis=0)
    lane = iota(total.shape, 1)
    total = total * jnp.where(lane < feat, scale_relations, scale_weights)
    out_ref[...] = jnp.broadcast_to(total.astype(BF16)[None], out_ref.shape)


def combine(chunks, feat, scale_relations, scale_weights):
    return pl.pallas_call(
        functools.partial(combine_kernel, feat, scale_relations, scale_weights),
        in_specs=[VMEM],
        out_specs=VMEM,
        out_shape=jax.ShapeDtypeStruct(chunks.shape, BF16),
        compiler_params=params(),
        cost_estimate=cost(1e6, 1 << 20),
        name="combine",
    )(chunks)


def unpack_kernel(feat, in_ref, relation_ref, w_in_ref, w_bias_ref, w_out_ref):
    groups = relation_ref.shape[0]
    relation_ref[...] = in_ref[0:groups, 0:feat].astype(F32)
    for layer in range(2):
        at = 2 * layer * GAP
        left = in_ref[at:at + GAP, feat:feat + TILE].astype(F32)
        right = in_ref[at + GAP:at + 2 * GAP, feat:feat + TILE].astype(F32)
        both = jnp.concatenate([left, right], axis=1)
        w_in_ref[layer] = both[0:2 * DIM]
        w_out_ref[layer] = both[2 * DIM:3 * DIM].T
        w_bias_ref[layer:layer + 1, :] = both[3 * DIM:3 * DIM + 1]


def unpack(gathered, groups, feat):
    return pl.pallas_call(
        functools.partial(unpack_kernel, feat),
        in_specs=[VMEM],
        out_specs=[VMEM] * 4,
        out_shape=[
            jax.ShapeDtypeStruct((groups, feat), F32),
            jax.ShapeDtypeStruct((2, 2 * DIM, WIDE), F32),
            jax.ShapeDtypeStruct((2, WIDE), F32),
            jax.ShapeDtypeStruct((2, WIDE, DIM), F32),
        ],
        compiler_params=params(),
        cost_estimate=cost(1e6, 2 << 20),
        name="unpack",
    )(gathered)


def final_kernel(tiles_ref, count_ref, quarter_ref, next_ref, live_ref, c0, c1, c2, c3, out_ref):
    tile = 2 * quarter_ref[0] + pl.program_id(0)
    value = next_ref[...]
    for k in range(2):
        rows = slice(k * TILE, (k + 1) * TILE)
        is_live = (tile == tiles_ref[1, k]) & (count_ref[1, 0] > k)
        value = jnp.where(is_live, live_ref[rows, :], value)
    for k in range(2):
        rows = slice(k * TILE, (k + 1) * TILE)
        is_live = (tile == tiles_ref[0, k]) & (count_ref[0, 0] > k)
        source = (c0[rows, :].astype(F32) + c1[rows, :].astype(F32)) + (
            c2[rows, :].astype(F32) + c3[rows, :].astype(F32)
        )
        value = jnp.where(is_live, value + source, value)
    out_ref[...] = value.astype(BF16)


def final_pass(tiles, count, quarter_id, after, live, parts, quarter):
    feat = after.shape[1]
    blocks = quarter // TILE

    def whole(shape):
        return pl.BlockSpec(shape, lambda i, *_: (0,) * len(shape))

    return pl.pallas_call(
        final_kernel,
        grid_spec=pltpu.PrefetchScalarGridSpec(
            num_scalar_prefetch=3,
            grid=(blocks,),
            in_specs=[pl.BlockSpec((TILE, feat), lambda i, t, c, q: (q[0] * blocks + i, 0)), whole(live.shape)]
            + [whole(parts[0].shape)] * 4,
            out_specs=pl.BlockSpec((TILE, feat), lambda i, *_: (i, 0)),
        ),
        out_shape=jax.ShapeDtypeStruct((quarter, feat), BF16),
        compiler_params=params(),
        cost_estimate=cost(1e6, 1 << 20),
        name="final",
    )(tiles, count, quarter_id, after, live, *parts)


def shards(state_zero, state_one, aggregate_one, aggregate_two, cotangent, relation_table, update_in, update_bias,
           update_out, frontier_tiles, frontier_count, edge_source, edge_relation, edge_target, edge_owner):
    block_rows, feat = state_zero.shape
    groups = relation_table.shape[0]
    group_size = lax.axis_size("rel")
    peers = lax.axis_size("ent")
    quarter = block_rows // group_size
    edges = edge_source.shape[0]
    capacity = 3 * edges // (2 * peers)
    slots = peers * capacity
    sum_rows = 8 * peers

    def exchange(chunks):
        return lax.all_to_all(chunks, "ent", split_axis=0, concat_axis=0, tiled=True)

    def over_rel(part):
        turned = [
            lax.ppermute(part, "rel", [(i, (i + k) % group_size) for i in range(group_size)])
            for k in range(1, group_size)
        ]
        return [part] + turned

    def layer(index):
        return update_in[index], update_bias[index][None, :], update_out[index]

    row = lambda values: values.reshape(1, edges)
    request, ids = pl.pallas_call(
        functools.partial(slots_kernel, peers),
        in_specs=[VMEM] * 4,
        out_specs=[VMEM] * 2,
        out_shape=[
            jax.ShapeDtypeStruct((peers, 1, 128), F32),
            jax.ShapeDtypeStruct((peers, 128), F32),
        ],
        compiler_params=params(),
        cost_estimate=cost(1e8, 1 << 20),
        name="slots",
    )(row(edge_owner), row(edge_target), row(edge_source), row(edge_relation))
    asked = exchange(request)

    upstream_one, picked_two, sums_two = dense_pass(
        False, capacity, frontier_tiles, frontier_count, aggregate_two, state_one, cotangent, *layer(1), asked
    )
    answered_two = exchange(picked_two.reshape(peers, capacity, feat)).reshape(slots, feat)
    after, rest, sums_rest = dense_pass(
        True, capacity, frontier_tiles, frontier_count, aggregate_one, state_zero, upstream_one, *layer(0), asked
    )
    edge_table, select_two, states_two, select_one, states_one, select_rel = slot_tables(
        capacity, frontier_tiles, frontier_count, ids, relation_table, state_one, state_zero
    )
    parts = over_rel(contribution(answered_two, edge_table, select_two))
    picked_one, after_live, sums_live = live_pass(
        capacity, frontier_tiles, frontier_count, aggregate_one, state_zero, upstream_one, parts, *layer(0), asked, rest
    )
    answered_one = exchange(picked_one.reshape(peers, capacity, feat)).reshape(slots, feat)
    relation_two = relation_part(answered_two, states_two, select_rel)

    parts = over_rel(contribution(answered_one, edge_table, select_one))
    packed = pack_sums(
        answered_one, states_one, select_rel, relation_two, sums_two, sums_rest, sums_live, sum_rows
    )
    scale_weights = 1.0 / math.sqrt(block_rows * peers * QUERIES)
    scale_relations = math.sqrt(groups * group_size / (edges * peers * group_size))
    chunks = exchange(packed.reshape(peers, 8, feat + TILE))
    gathered = exchange(combine(chunks, feat, scale_relations, scale_weights)).reshape(sum_rows, feat + TILE)
    quarter_id = lax.axis_index("rel").astype(jnp.int32).reshape(1)
    grad_zero = final_pass(frontier_tiles, frontier_count, quarter_id, after, after_live, parts, quarter)
    return (grad_zero,) + tuple(unpack(gathered, groups, feat))


def solution(mesh):
    in_specs = (
        P("ent", None),
        P("ent", None),
        P("ent", None),
        P("ent", None),
        P("ent", None),
        P("rel", None),
        P(),
        P(),
        P(),
        P(None, "ent"),
        P(None, "ent"),
        P(("ent", "rel")),
        P(("ent", "rel")),
        P(("ent", "rel")),
        P(("ent", "rel"), None),
    )
    out_specs = (P(("ent", "rel"), None), P("rel", None), P(), P(), P())
    return jax.shard_map(shards, mesh=mesh, in_specs=in_specs, out_specs=out_specs, check_vma=False)
```

time: 628 us -> 179 us (0.29)
  waiting for transfers between devices: 278 us -> 48.3 us
  blocking collectives: 124 us -> 20.9 us
  local copies, waits for them, and re-layouts: 77.1 us -> 12.4 us
  matrix products: 61.5 us -> 0 us
  Pallas kernels: 0 us -> 55.3 us
  other arithmetic: 33.2 us -> 0 us
  between operations: 14.3 us -> 0.75 us
    psum x3 -> x0, waiting for transfers between devices: 263 us -> none  [the longest x1 177 us: shards(): lax.psum((stacked_in, stacked_bias, stacked_out, relation_grad), 'ent')]
    psum x1 -> x0, blocking collectives: 124 us -> none  [shards(): lax.psum((stacked_in, stacked_bias, stacked_out, relation_grad), 'ent')]
    dot_general x29 -> x0, matrix products: 61.5 us -> none  [the longest x4 16 us: update_backward(): jnp.einsum('nqd,ed->nqe', upstream_low, update_out, preferred_element_typ...]
    pallas_call x0 -> x12, Pallas kernels: none -> 55.3 us  [the longest x2 23.7 us: dense_pass(): pl.pallas_call(functools.partial(dense_kernel, capacity, masked), grid=(r...]
    gather x8 -> x0, local copies, waits for them, and re-layouts: 38.9 us -> none  [the longest x2 10.7 us: shards(): picked = grad_agg[asked]]
    all_to_all x3 -> x4, waiting for transfers between devices: 15 us -> 40.2 us  [exchange(): lax.all_to_all(chunks, 'ent', split_axis=0, concat_axis=0, tiled=True)]
    all_to_all x0 -> x1, blocking collectives: none -> 20.9 us  [exchange(): lax.all_to_all(chunks, 'ent', split_axis=0, concat_axis=0, tiled=True)]
    another operation x6 -> x0, other arithmetic: 19.5 us -> none
  transfers between devices with their start and end apart: 6 -> 10, of which waited for: 4 -> 6; matrix products, arithmetic and copies ran while one was open for 12% -> 4% of each run, Pallas kernels for 0% -> 15%
where the time goes in v1:
time: 179 us; the launch traced here: 178 us
  Pallas kernels  55.3 us (31%)
  waiting for transfers between devices  48.3 us (27%)
  starting transfers between devices  40.1 us (22%)
  blocking collectives  20.9 us (12%)
  local copies, waits for them, and re-layouts  12.4 us (7%)
    all_to_all x4, waiting for transfers between devices, exchange(): lax.all_to_all(chunks, 'ent', split_axis=0, concat_axis=0, tiled=True)  40.2 us
    all_to_all x4, starting transfers between devices, exchange(): lax.all_to_all(chunks, 'ent', split_axis=0, concat_axis=0, tiled=True)  32.9 us
    pallas_call x2, Pallas kernels, dense_pass(): pl.pallas_call(functools.partial(dense_kernel, capacity, masked), grid=(r...  23.7 us
    all_to_all x1, blocking collectives, exchange(): lax.all_to_all(chunks, 'ent', split_axis=0, concat_axis=0, tiled=True)  20.9 us
    unnamed x24, local copies, waits for them, and re-layouts  8.93 us
    ppermute x6, waiting for transfers between devices, over_rel(): lax.ppermute(part, 'rel', [(i, (i + k) % group_size) for i in range(group...  8.14 us
    ppermute x6, starting transfers between devices, over_rel(): lax.ppermute(part, 'rel', [(i, (i + k) % group_size) for i in range(group...  7.18 us
    pallas_call x1, Pallas kernels, live_pass(): pl.pallas_call(functools.partial(live_kernel, capacity), grid_spec=pltpu....  6.06 us
  transfers between devices with their start and end apart: 10, of which 6 were waited for; matrix products, arithmetic and copies ran while one was open for 4% of the time, Pallas kernels for 15%

profile of v1, /device:TPU:1, one launch (start us, length us, event | category | flops | bytes accessed | tf_op | source)
XLA Modules:
  0.0 177.7 jit_solution(2970714173898464330)
XLA Ops:
  0.6 1.8 %slots.1 = (f32[64,1,128]{2,1,0:T(1,128)}, f32[64,128]{1,0:T(8,128)}) custom-call(s32[1,1024]{1,0:T(1,128)} %bitcast.28, s32[1,1024]{1,0:T(1,128)} %bitcast.29, s32[1,1024]{1,0:T(1,128)} %bitcast.30, s32[1,1024]{1,0:T(1,128)} %bitcast.31), custom_call_target="tpu_custom_call" | custom-call | flops 100000000 | bytes 1048576 | tf_op jit(solution)/shard_map/slots/pallas_call | solution.py:518
  2.4 13.0 %all-to-all-start = ((f32[64,1,128]{2,1,0:T(1,128)}), f32[64,1,128]{2,1,0:T(1,128)S(1)}, u32[]{:S(2)}, u32[]{:S(2)}) async-start(f32[64,1,128]{2,1,0:T(1,128)} %get-tuple-element.26), calls=%async_computation | async-start | bytes 65536 | tf_op jit(solution)/shard_map/all_to_all | solution.py:505
  20.9 3.7 %all-to-all-done.asked_ref = f32[64,1,128]{2,1,0:T(1,128)S(1)} async-done(((f32[64,1,128]{2,1,0:T(1,128)}), f32[64,1,128]{2,1,0:T(1,128)S(1)}, u32[]{:S(2)}, u32[]{:S(2)}) %all-to-all-start) | async-done | bytes 32800 | tf_op jit(solution)/shard_map/all_to_all | solution.py:505
  25.2 11.7 %dense.1 = (f32[1024,256]{1,0:T(8,128)}, bf16[1536,256]{1,0:T(8,128)(2,1)}, f32[104,256]{1,0:T(8,128)}) custom-call(s32[2,2]{1,0:T(2,128)} %tiles_ref.9, s32[2,1]{1,0:T(2,128)} %copy.26.count_ref, bf16[1024,256]{1,0:T(8,128)(2,1)} %agg_ref.2, bf16[1024,256]{1,0:T(8,128)(2,1)} %one_b.1, bf16[1024,256]{1,0:T(8,128)(2,1)} %up_ref.1, ...), custom_call_target="tpu_custom_call" | custom-call | flops 5400000000 | bytes 4194304 | tf_op jit(solution)/shard_map/dense/pallas_call | solution.py:223
  37.0 6.6 %all-to-all-start.1 = ((bf16[64,24,256]{2,1,0:T(8,128)(2,1)}), bf16[64,24,256]{2,1,0:T(8,128)(2,1)S(1)}, u32[]{:S(2)}, u32[]{:S(2)}) async-start(bf16[64,24,256]{2,1,0:T(8,128)(2,1)} %bitcast.23), calls=%async_computation.1 | async-start | bytes 1572864 | tf_op jit(solution)/shard_map/all_to_all | solution.py:505
  44.3 5.6 %tables.1 = (bf16[1536,256]{1,0:T(8,128)(2,1)}, bf16[1536,256]{1,0:T(8,128)(2,1)}, bf16[1536,256]{1,0:T(8,128)(2,1)}, bf16[1536,256]{1,0:T(8,128)(2,1)}, bf16[15...) custom-call(s32[2,2]{1,0:T(2,128)} %tiles_ref.9, s32[2,1]{1,0:T(2,128)} %copy.26.count_ref, ...), custom_call_target="tpu_custom_call" | custom-call | flops 2000000000 | bytes 6291456 | tf_op jit(solution)/shard_map/tables/pallas_call | solution.py:270
  49.9 16.6 %all-to-all-done.1 = bf16[64,24,256]{2,1,0:T(8,128)(2,1)S(1)} async-done(((bf16[64,24,256]{2,1,0:T(8,128)(2,1)}), bf16[64,24,256]{2,1,0:T(8,128)(2,1)S(1)}, u32[]{:S(2)}, u32[]{:S(2)}) %all-to-all-start.1) | async-done | bytes 786464 | tf_op jit(solution)/shard_map/all_to_all | solution.py:505
  67.4 2.7 %contribution.2.c0 = bf16[256,256]{1,0:T(8,128)(2,1)} custom-call(bf16[1536,256]{1,0:T(8,128)(2,1)} %bitcast.17, bf16[1536,256]{1,0:T(8,128)(2,1)} %get-tuple-element.31.t_ref, bf16[1536,256]{1,0:T(8,128)(2,1)} %get-tuple-element.32.s_ref), custom_call_target="tpu_custom_call" | custom-call | flops 200000000 | bytes 3145728 | tf_op jit(solution)/shard_map/contribution/pallas_call | solution.py:290
  70.1 2.7 %collective-permute-start.2 = (bf16[256,256]{1,0:T(8,128)(2,1)}, bf16[256,256]{1,0:T(8,128)(2,1)S(1)}, u32[]{:S(2)}, u32[]{:S(2)}) collective-permute-start(bf16[256,256]{1,0:T(8,128)(2,1)} %contribution.2.c0), channel_id=1, source_target_pairs={{0,3},{1,0},{2,1},{3,2},{4,7},{5,4},{6,5},{7,6},{8,11},{9,8},{10,9... | collective-permute-start | bytes 393224 | tf_op jit(solution)/shard_map/ppermute | solution.py:509
  73.9 12.0 %dense_masked.1 = (f32[1024,256]{1,0:T(8,128)}, bf16[1536,256]{1,0:T(8,128)(2,1)}, f32[104,256]{1,0:T(8,128)}) custom-call(s32[2,2]{1,0:T(2,128)} %tiles_ref.9, s32[2,1]{1,0:T(2,128)} %copy.26.count_ref, bf16[1024,256]{1,0:T(8,128)(2,1)} %agg_b.1, bf16[1024,256]{1,0:T(8,128)(2,1)} %state_b.1, f32[1024,256]{1,0:T(8,128)} %get-tuple-element.27.up_ref.up_a.up_b, ...), custom_call_target="tpu_custom_call" | custom-call | flops 5400000000 | bytes 4194304 | tf_op jit(solution)/shard_map/dense_masked/pallas_call | solution.py:223
  86.6 6.1 %live.1 = (bf16[1536,256]{1,0:T(8,128)(2,1)}, f32[256,256]{1,0:T(8,128)}, f32[104,256]{1,0:T(8,128)}) custom-call(s32[2,2]{1,0:T(2,128)} %tiles_ref.9, s32[2,1]{1,0:T(2,128)} %copy.26.count_ref, bf16[1024,256]{1,0:T(8,128)(2,1)} %agg_b.1, bf16[1024,256]{1,0:T(8,128)(2,1)} %agg_b.1, bf16[1024,256]{1,0:T(8,128)(2,1)} %state_b.1, bf16[1024,256]{1,0:T(8,128)(2,1)} %state_b.1, ...), custom_call_target="tpu_custom_call" | custom-call | flops 1600000000 | bytes 4194304 | tf_op jit(solution)/shard_map/live/pallas_call | solution.py:352
  92.7 7.1 %all-to-all-start.2 = ((bf16[64,24,256]{2,1,0:T(8,128)(2,1)}), bf16[64,24,256]{2,1,0:T(8,128)(2,1)S(1)}, u32[]{:S(2)}, u32[]{:S(2)}) async-start(bf16[64,24,256]{2,1,0:T(8,128)(2,1)} %bitcast.24), calls=%async_computation.2 | async-start | bytes 1572864 | tf_op jit(solution)/shard_map/all_to_all | solution.py:505
  99.7 3.0 %relation_part.1.before_ref = f32[384,256]{1,0:T(8,128)} custom-call(bf16[1536,256]{1,0:T(8,128)(2,1)} %bitcast.18, bf16[1536,256]{1,0:T(8,128)(2,1)} %get-tuple-element.39.h_ref, bf16[1536,384]{1,0:T(8,128)(2,1)} %get-tuple-element.38.r_ref), custom_call_target="tpu_custom_call" | custom-call | flops 400000000 | bytes 3145728 | tf_op jit(solution)/shard_map/relation_part/pallas_call | solution.py:306
  102.8 19.9 %all-to-all-done.2 = bf16[64,24,256]{2,1,0:T(8,128)(2,1)S(1)} async-done(((bf16[64,24,256]{2,1,0:T(8,128)(2,1)}), bf16[64,24,256]{2,1,0:T(8,128)(2,1)S(1)}, u32[]{:S(2)}, u32[]{:S(2)}) %all-to-all-start.2) | async-done | bytes 786464 | tf_op jit(solution)/shard_map/all_to_all | solution.py:505
  123.6 3.2 %pack_sums.1 = bf16[512,384]{1,0:T(8,128)(2,1)} custom-call(bf16[1536,256]{1,0:T(8,128)(2,1)} %bitcast.19, bf16[1536,256]{1,0:T(8,128)(2,1)} %get-tuple-element.37.h_ref, bf16[1536,384]{1,0:T(8,128)(2,1)} %get-tuple-element.38.r_ref, f32[384,256]{1,0:T(8,128)} %relation_part.1.before_ref, f32[104,256]{1,0:T(8,128)} %get-tuple-element.40.w2_ref, ...), custom_call_target="tpu_custom_call" | custom-call | flops 400000000 | bytes 4194304 | tf_op jit(solution)/shard_map/pack_sums/pallas_call | solution.py:392
  126.7 20.9 %all_to_all.25.in_ref = bf16[64,8,384]{2,1,0:T(8,128)(2,1)} all-to-all(bf16[64,8,384]{2,1,0:T(8,128)(2,1)} %bitcast.22), channel_id=1, replica_groups=mesh['ent'=64,'rel'=4] {'ent'}, dimensions={0} | all-to-all | bytes 786432 | tf_op jit(solution)/shard_map/all_to_all | solution.py:505
  147.6 1.9 %combine.1 = bf16[64,8,384]{2,1,0:T(8,128)(2,1)} custom-call(bf16[64,8,384]{2,1,0:T(8,128)(2,1)} %all_to_all.25.in_ref), custom_call_target="tpu_custom_call" | custom-call | flops 1000000 | bytes 1048576 | tf_op jit(solution)/shard_map/combine/pallas_call | solution.py:411
  149.5 6.2 %all-to-all-start.4 = ((bf16[64,8,384]{2,1,0:T(8,128)(2,1)}), bf16[64,8,384]{2,1,0:T(8,128)(2,1)S(1)}, u32[]{:S(2)}, u32[]{:S(2)}) async-start(bf16[64,8,384]{2,1,0:T(8,128)(2,1)} %combine.1), calls=%async_computation.4 | async-start | bytes 786432 | tf_op jit(solution)/shard_map/all_to_all | solution.py:505
  155.7 2.7 %contribution.3.c0 = bf16[256,256]{1,0:T(8,128)(2,1)} custom-call(bf16[1536,256]{1,0:T(8,128)(2,1)} %bitcast.20, bf16[1536,256]{1,0:T(8,128)(2,1)} %get-tuple-element.31.t_ref, bf16[1536,256]{1,0:T(8,128)(2,1)} %get-tuple-element.36.s_ref), custom_call_target="tpu_custom_call" | custom-call | flops 200000000 | bytes 3145728 | tf_op jit(solution)/shard_map/contribution/pallas_call | solution.py:290
  158.4 2.0 %collective-permute-start.5 = (bf16[256,256]{1,0:T(8,128)(2,1)}, bf16[256,256]{1,0:T(8,128)(2,1)S(1)}, u32[]{:S(2)}, u32[]{:S(2)}) collective-permute-start(bf16[256,256]{1,0:T(8,128)(2,1)} %contribution.3.c0), channel_id=1, source_target_pairs={{0,3},{1,0},{2,1},{3,2},{4,7},{5,4},{6,5},{7,6},{8,11},{9,8},{10,9... | collective-permute-start | bytes 393224 | tf_op jit(solution)/shard_map/ppermute | solution.py:509
  163.5 2.9 %collective-permute-done.4.c2 = bf16[256,256]{1,0:T(8,128)(2,1)S(1)} collective-permute-done((bf16[256,256]{1,0:T(8,128)(2,1)}, bf16[256,256]{1,0:T(8,128)(2,1)S(1)}, u32[]{:S(2)}, u32[]{:S(2)}) %collective-permute-start.4) | collective-permute-done | bytes 131104 | tf_op jit(solution)/shard_map/ppermute | solution.py:509
  166.4 3.5 %collective-permute-done.3.c1 = bf16[256,256]{1,0:T(8,128)(2,1)S(1)} collective-permute-done((bf16[256,256]{1,0:T(8,128)(2,1)}, bf16[256,256]{1,0:T(8,128)(2,1)S(1)}, u32[]{:S(2)}, u32[]{:S(2)}) %collective-permute-start.3) | collective-permute-done | bytes 131104 | tf_op jit(solution)/shard_map/ppermute | solution.py:509
  170.6 2.8 %final.1 = bf16[256,256]{1,0:T(8,128)(2,1)} custom-call(s32[2,2]{1,0:T(2,128)} %tiles_ref.9, s32[2,1]{1,0:T(2,128)} %copy.26.count_ref, s32[1]{0:T(128)} %bitcast.quarter_ref, f32[1024,256]{1,0:T(8,128)} %get-tuple-element.28.next_ref, f32[256,256]{1,0:T(8,128)} %get-tuple-element.34.live_ref, bf16[256,256]{1,0:T(8,128)(2,1)} %contribution.3.c0, ...), custom_call_target="tpu_custom_call" | custom-call | flops 1000000 | bytes 1048576 | tf_op jit(solution)/shard_map/final/pallas_call | solution.py:476
  174.2 1.9 %unpack.1 = (f32[328,256]{1,0:T(8,128)}, f32[2,64,256]{2,1,0:T(8,128)}, f32[2,256]{1,0:T(2,128)}, f32[2,256,32]{2,1,0:T(8,128)}) custom-call(bf16[512,384]{1,0:T(8,128)(2,1)} %bitcast.21), custom_call_target="tpu_custom_call" | custom-call | flops 1000000 | bytes 2097152 | tf_op jit(solution)/shard_map/unpack/pallas_call | solution.py:436
  (36 shorter events, 16.6 us)
Async XLA Ops:
  2.4 22.2 %all-to-all-start = ((f32[64,1,128]{2,1,0:T(1,128)}), f32[64,1,128]{2,1,0:T(1,128)S(1)}, u32[]{:S(2)}, u32[]{:S(2)}) async-start(f32[64,1,128]{2,1,0:T(1,128)} %get-tuple-element.26), calls=%async_computation | async-start | bytes 65536 | tf_op jit(solution)/shard_map/all_to_all | solution.py:505
  24.6 0.6 copy-start.6
  37.0 29.6 %all-to-all-start.1 = ((bf16[64,24,256]{2,1,0:T(8,128)(2,1)}), bf16[64,24,256]{2,1,0:T(8,128)(2,1)S(1)}, u32[]{:S(2)}, u32[]{:S(2)}) async-start(bf16[64,24,256]{2,1,0:T(8,128)(2,1)} %bitcast.23), calls=%async_computation.1 | async-start | bytes 1572864 | tf_op jit(solution)/shard_map/all_to_all | solution.py:505
  66.5 0.9 copy-start
  70.1 15.8 %collective-permute-start.2 = (bf16[256,256]{1,0:T(8,128)(2,1)}, bf16[256,256]{1,0:T(8,128)(2,1)S(1)}, u32[]{:S(2)}, u32[]{:S(2)}) collective-permute-start(bf16[256,256]{1,0:T(8,128)(2,1)} %contribution.2.c0), channel_id=1, source_target_pairs={{0,3},{1,0},{2,1},{3,2},{4,7},{5,4},{6,5},{7,6},{8,11},{9,8},{10,9... | collective-permute-start | bytes 393224 | tf_op jit(solution)/shard_map/ppermute | solution.py:509
  72.8 13.0 %collective-permute-start.1 = (bf16[256,256]{1,0:T(8,128)(2,1)}, bf16[256,256]{1,0:T(8,128)(2,1)S(1)}, u32[]{:S(2)}, u32[]{:S(2)}) collective-permute-start(bf16[256,256]{1,0:T(8,128)(2,1)} %contribution.2.c0), channel_id=1, source_target_pairs={{0,2},{1,3},{2,0},{3,1},{4,6},{5,7},{6,4},{7,5},{8,10},{9,11},{10,... | collective-permute-start | bytes 393224 | tf_op jit(solution)/shard_map/ppermute | solution.py:509
  73.2 12.7 %collective-permute-start = (bf16[256,256]{1,0:T(8,128)(2,1)}, bf16[256,256]{1,0:T(8,128)(2,1)S(1)}, u32[]{:S(2)}, u32[]{:S(2)}) collective-permute-start(bf16[256,256]{1,0:T(8,128)(2,1)} %contribution.2.c0), channel_id=1, source_target_pairs={{0,1},{1,2},{2,3},{3,0},{4,5},{5,6},{6,7},{7,4},{8,9},{9,10},{10,1... | collective-permute-start | bytes 393224 | tf_op jit(solution)/shard_map/ppermute | solution.py:509
  85.9 0.7 copy-start.7
  85.9 0.7 copy-start.8
  85.9 0.7 copy-start.9
  92.7 30.0 %all-to-all-start.2 = ((bf16[64,24,256]{2,1,0:T(8,128)(2,1)}), bf16[64,24,256]{2,1,0:T(8,128)(2,1)S(1)}, u32[]{:S(2)}, u32[]{:S(2)}) async-start(bf16[64,24,256]{2,1,0:T(8,128)(2,1)} %bitcast.24), calls=%async_computation.2 | async-start | bytes 1572864 | tf_op jit(solution)/shard_map/all_to_all | solution.py:505
  122.7 0.9 copy-start.1
  149.5 23.9 %all-to-all-start.4 = ((bf16[64,8,384]{2,1,0:T(8,128)(2,1)}), bf16[64,8,384]{2,1,0:T(8,128)(2,1)S(1)}, u32[]{:S(2)}, u32[]{:S(2)}) async-start(bf16[64,8,384]{2,1,0:T(8,128)(2,1)} %combine.1), calls=%async_computation.4 | async-start | bytes 786432 | tf_op jit(solution)/shard_map/all_to_all | solution.py:505
  158.4 5.1 %collective-permute-start.5 = (bf16[256,256]{1,0:T(8,128)(2,1)}, bf16[256,256]{1,0:T(8,128)(2,1)S(1)}, u32[]{:S(2)}, u32[]{:S(2)}) collective-permute-start(bf16[256,256]{1,0:T(8,128)(2,1)} %contribution.3.c0), channel_id=1, source_target_pairs={{0,3},{1,0},{2,1},{3,2},{4,7},{5,4},{6,5},{7,6},{8,11},{9,8},{10,9... | collective-permute-start | bytes 393224 | tf_op jit(solution)/shard_map/ppermute | solution.py:509
  160.4 6.0 %collective-permute-start.4 = (bf16[256,256]{1,0:T(8,128)(2,1)}, bf16[256,256]{1,0:T(8,128)(2,1)S(1)}, u32[]{:S(2)}, u32[]{:S(2)}) collective-permute-start(bf16[256,256]{1,0:T(8,128)(2,1)} %contribution.3.c0), channel_id=1, source_target_pairs={{0,2},{1,3},{2,0},{3,1},{4,6},{5,7},{6,4},{7,5},{8,10},{9,11},{10,... | collective-permute-start | bytes 393224 | tf_op jit(solution)/shard_map/ppermute | solution.py:509
  161.8 8.1 %collective-permute-start.3 = (bf16[256,256]{1,0:T(8,128)(2,1)}, bf16[256,256]{1,0:T(8,128)(2,1)S(1)}, u32[]{:S(2)}, u32[]{:S(2)}) collective-permute-start(bf16[256,256]{1,0:T(8,128)(2,1)} %contribution.3.c0), channel_id=1, source_target_pairs={{0,1},{1,2},{2,3},{3,0},{4,5},{5,6},{6,7},{7,4},{8,9},{9,10},{10,1... | collective-permute-start | bytes 393224 | tf_op jit(solution)/shard_map/ppermute | solution.py:509
  163.5 6.4 %copy-start.3 = (bf16[256,256]{1,0:T(8,128)(2,1)}, bf16[256,256]{1,0:T(8,128)(2,1)S(1)}, u32[]{:S(2)}) copy-start(bf16[256,256]{1,0:T(8,128)(2,1)S(1)} %collective-permute-done.5.c3) | copy-start | bytes 393220
  166.4 3.5 %copy-start.4 = (bf16[256,256]{1,0:T(8,128)(2,1)}, bf16[256,256]{1,0:T(8,128)(2,1)S(1)}, u32[]{:S(2)}) copy-start(bf16[256,256]{1,0:T(8,128)(2,1)S(1)} %collective-permute-done.4.c2) | copy-start | bytes 393220
  169.9 0.7 copy-start.5
  173.4 0.8 copy-start.2

commit v2 on v1

--- a/solution.py
+++ b/solution.py
@@ -35,7 +35,7 @@
     return lax.dot_general(a, b, (((0,), (0,)), ((), ())), preferred_element_type=F32)
 
 
-def params(vmem=60 << 20):
+def params(vmem=20 << 20):
     return pltpu.CompilerParams(vmem_limit_bytes=vmem)
 
 
@@ -107,18 +107,16 @@
     return (iota((column.shape[0], width), 1) == column).astype(F32).astype(BF16)
 
 
-def build_weights(w_in_ref, w_bias_ref, w_out_ref, wx_ref, wu_ref, wb_ref):
+def build_weights(layer, w_in_ref, w_bias_ref, w_out_ref, wx_ref, wu_ref, wb_ref):
     wx_ref[...] = jnp.zeros_like(wx_ref)
     wu_ref[...] = jnp.zeros_like(wu_ref)
-    eye = (iota((DIM, DIM), 0) == iota((DIM, DIM), 1)).astype(BF16)
-    w_out_t = dot_nt(eye, w_out_ref[...]).astype(BF16)
     for q in range(HALF_Q):
         rows, cols = slice(q * DIM, (q + 1) * DIM), slice(q * WIDE, (q + 1) * WIDE)
         low = slice(TILE + q * DIM, TILE + (q + 1) * DIM)
-        wx_ref[rows, cols] = w_in_ref[0:DIM, :]
-        wx_ref[low, cols] = w_in_ref[DIM:2 * DIM, :]
-        wu_ref[rows, cols] = w_out_t
-        wb_ref[:, cols] = w_bias_ref[...]
+        wx_ref[rows, cols] = w_in_ref[layer, 0:DIM, :]
+        wx_ref[low, cols] = w_in_ref[layer, DIM:2 * DIM, :]
+        wu_ref[rows, cols] = w_out_ref[layer]
+        wb_ref[:, cols] = w_bias_ref[layer:layer + 1, :]
 
 
 def mlp_half(s, agg, state, up_low, wx, wu, bias, acc_in, acc_out, acc_bias):
@@ -160,15 +158,25 @@
     acc_bias[...] = jnp.zeros_like(acc_bias)
 
 
-MLP_SCRATCH = [
-    pltpu.VMEM((256, HALF_Q * WIDE), BF16),
-    pltpu.VMEM((TILE, HALF_Q * WIDE), BF16),
-    pltpu.VMEM((1, HALF_Q * WIDE), F32),
-    pltpu.VMEM((256, HALF_Q * WIDE), F32),
-    pltpu.VMEM((TILE, HALF_Q * WIDE), F32),
-    pltpu.VMEM((1, HALF_Q * WIDE), F32),
+WEIGHT_SHAPES = [
+    ((2 * TILE, HALF_Q * WIDE), BF16),
+    ((TILE, HALF_Q * WIDE), BF16),
+    ((1, HALF_Q * WIDE), F32),
+]
+SUM_SHAPES = [
+    ((2 * TILE, HALF_Q * WIDE), F32),
+    ((TILE, HALF_Q * WIDE), F32),
+    ((1, HALF_Q * WIDE), F32),
 ]
 SUM_ROWS = 3 * DIM + 8
+
+
+def scratch(shapes):
+    return [pltpu.VMEM(shape, dtype) for shape, dtype in shapes]
+
+
+def whole(shape):
+    return pl.BlockSpec(shape, lambda i, *_: (0,) * len(shape))
 
 
 def pick_rows(asked, grad_agg, picked_ref, chunks=4):
@@ -179,23 +187,8 @@
         picked_ref[part, :] = dot_nn(onehot(asked[part], rows), grad_agg[...]).astype(BF16)
 
 
-def dense_kernel(capacity, masked, tiles_ref, count_ref, agg_ref, state_ref, up_ref, w_in_ref,
-                 w_bias_ref, w_out_ref, asked_ref, next_ref, picked_ref, sums_ref,
-                 wx, wu, wb, acc_in, acc_out, acc_bias, grad_agg):
-    step = pl.program_id(0)
+def dense_step(step, agg_ref, state_ref, up, up_low, wx, wu, wb, acc_in, acc_out, acc_bias, grad_agg, next_ref):
     rows = agg_ref.shape[0]
-
-    @pl.when(step == 0)
-    def _():
-        build_weights(w_in_ref, w_bias_ref, w_out_ref, wx, wu, wb)
-        clear(acc_in, acc_out, acc_bias)
-
-    up = up_ref[...].astype(F32)
-    up_low = up_ref[...].astype(BF16)
-    if masked:
-        tile = lax.shift_right_logical(iota((rows, 1), 0) + step * rows, 7)
-        dead = (tile == tiles_ref[1, 0]) | ((tile == tiles_ref[1, 1]) & (count_ref[1, 0] > 1))
-        up_low = jnp.where(dead, 0.0, up).astype(BF16)
     aggs, states = [], []
     for s in range(2):
         grad_x = mlp_half(s, agg_ref[...], state_ref[...], up_low, wx, wu, wb, acc_in, acc_out, acc_bias)
@@ -204,6 +197,20 @@
     grad_agg[pl.ds(pl.multiple_of(step * rows, rows), rows), :] = jnp.concatenate(aggs, axis=1).astype(BF16)
     next_ref[...] = up + jnp.concatenate(states, axis=1)
 
+
+def first_kernel(capacity, agg_ref, state_ref, up_ref, w_in_ref, w_bias_ref, w_out_ref, asked_ref,
+                 next_ref, picked_ref, sums_ref, wx, wu, wb, acc_in, acc_out, acc_bias, grad_agg):
+    step = pl.program_id(0)
+
+    @pl.when(step == 0)
+    def _():
+        build_weights(1, w_in_ref, w_bias_ref, w_out_ref, wx, wu, wb)
+        clear(acc_in, acc_out, acc_bias)
+
+    up_low = up_ref[...]
+    dense_step(step, agg_ref, state_ref, up_low.astype(F32), up_low, wx, wu, wb, acc_in, acc_out, acc_bias,
+               grad_agg, next_ref)
+
     @pl.when(step == pl.num_programs(0) - 1)
     def _():
         store_sums(acc_in, acc_out, acc_bias, sums_ref)
@@ -211,79 +218,153 @@
         pick_rows(asked, grad_agg, picked_ref)
 
 
-def dense_pass(masked, capacity, tiles, count, agg, state, up, w_in, w_bias, w_out, asked):
+def first_pass(capacity, agg, state, up, w_in, w_bias, w_out, asked):
     rows, feat = agg.shape
     slots = asked.shape[0] * capacity
     block = 256
     row_spec = pl.BlockSpec((block, feat), lambda i: (i, 0))
-
-    def whole(shape):
-        return pl.BlockSpec(shape, lambda i: (0,) * len(shape))
-
-    return pl.pallas_call(
-        functools.partial(dense_kernel, capacity, masked),
+    return pl.pallas_call(
+        functools.partial(first_kernel, capacity),
         grid=(rows // block,),
-        in_specs=[SMEM, SMEM, row_spec, row_spec, row_spec, whole(w_in.shape), whole(w_bias.shape),
-                  whole(w_out.shape), whole(asked.shape)],
+        in_specs=[row_spec, row_spec, row_spec, whole(w_in.shape), whole(w_bias.shape), whole(w_out.shape),
+                  whole(asked.shape)],
         out_specs=[row_spec, whole((slots, feat)), whole((SUM_ROWS, WIDE))],
         out_shape=[
             jax.ShapeDtypeStruct((rows, feat), F32),
             jax.ShapeDtypeStruct((slots, feat), BF16),
             jax.ShapeDtypeStruct((SUM_ROWS, WIDE), F32),
         ],
-        scratch_shapes=MLP_SCRATCH + [pltpu.VMEM((rows, feat), BF16)],
+        scratch_shapes=scratch(WEIGHT_SHAPES + SUM_SHAPES) + [pltpu.VMEM((rows, feat), BF16)],
         compiler_params=params(),
         cost_estimate=cost(5.4e9, 4 << 20, 2 << 20),
-        name="dense_masked" if masked else "dense",
+        name="first",
+    )(agg, state, up, w_in, w_bias, w_out, asked)
+
+
+def rest_kernel(capacity, tiles_ref, count_ref, agg_ref, state_ref, up_ref, w_in_ref, w_bias_ref, w_out_ref,
+                asked_ref, next_ref, picked_ref, sums_ref, live_ref, wx, wu, wb,
+                acc_in, acc_out, acc_bias, grad_agg):
+    step = pl.program_id(0)
+    rows = agg_ref.shape[0]
+    count = count_ref[0, 1]
+
+    @pl.when(step == 0)
+    def _():
+        build_weights(0, w_in_ref, w_bias_ref, w_out_ref, wx, wu, wb)
+        clear(acc_in, acc_out, acc_bias)
+
+    up = up_ref[...]
+    tile = lax.shift_right_logical(iota((rows, 1), 0) + step * rows, 7)
+    dead = (tile == tiles_ref[1, 0]) | ((tile == tiles_ref[1, 1]) & (count > 1))
+    up_low = jnp.where(dead, 0.0, up).astype(BF16)
+    dense_step(step, agg_ref, state_ref, up, up_low, wx, wu, wb, acc_in, acc_out, acc_bias, grad_agg, next_ref)
+
+    @pl.when(step == pl.num_programs(0) - 1)
+    def _():
+        store_sums(acc_in, acc_out, acc_bias, sums_ref)
+        asked = slot_columns(asked_ref[:, 0, :], capacity, (0,))[0]
+        live_ref[...] = onehot(compact_column(asked, (tiles_ref[1, 0], tiles_ref[1, 1]), count), 2 * TILE)
+        pick_rows(asked, grad_agg, picked_ref)
+
+
+def rest_pass(capacity, tiles, count, agg, state, up, w_in, w_bias, w_out, asked):
+    rows, feat = agg.shape
+    slots = asked.shape[0] * capacity
+    block = 256
+    row_spec = pl.BlockSpec((block, feat), lambda i: (i, 0))
+    return pl.pallas_call(
+        functools.partial(rest_kernel, capacity),
+        grid=(rows // block,),
+        in_specs=[SMEM, SMEM, row_spec, row_spec, row_spec, whole(w_in.shape), whole(w_bias.shape),
+                  whole(w_out.shape), whole(asked.shape)],
+        out_specs=[row_spec, whole((slots, feat)), whole((SUM_ROWS, WIDE)), whole((slots, 2 * TILE))]
+        + [whole(shape) for shape, _ in WEIGHT_SHAPES],
+        out_shape=[
+            jax.ShapeDtypeStruct((rows, feat), F32),
+            jax.ShapeDtypeStruct((slots, feat), BF16),
+            jax.ShapeDtypeStruct((SUM_ROWS, WIDE), F32),
+            jax.ShapeDtypeStruct((slots, 2 * TILE), BF16),
+        ]
+        + [jax.ShapeDtypeStruct(shape, dtype) for shape, dtype in WEIGHT_SHAPES],
+        scratch_shapes=scratch(SUM_SHAPES) + [pltpu.VMEM((rows, feat), BF16)],
+        compiler_params=params(),
+        cost_estimate=cost(5.4e9, 4 << 20, 2 << 20),
+        name="rest",
     )(tiles, count, agg, state, up, w_in, w_bias, w_out, asked)
 
 
-def tables_kernel(capacity, tiles_ref, count_ref, ids_ref, table_ref, one_a, one_b, zero_a, zero_b,
-                  t_ref, s2_ref, h2_ref, s1_ref, h1_ref, r_ref):
+def tables_two_kernel(capacity, tiles_ref, count_ref, ids_ref, table_ref, t_ref, s_ref):
     source, relation = slot_columns(ids_ref[...], capacity, (0, 64))
-    source, relation = source - 1, relation - 1
-    width = r_ref.shape[1]
+    width = -(-table_ref.shape[0] // TILE) * TILE
     pad = width - table_ref.shape[0]
     table = jnp.concatenate([table_ref[...], jnp.zeros((pad, table_ref.shape[1]), BF16)], axis=0)
-    select = onehot(relation, width)
-    r_ref[...] = select
-    t_ref[...] = dot_nn(select, table).astype(BF16)
-    for hop, s_ref, h_ref, a, b in ((1, s2_ref, h2_ref, one_a, one_b), (0, s1_ref, h1_ref, zero_a, zero_b)):
-        column = compact_column(source, (tiles_ref[hop, 0], tiles_ref[hop, 1]), count_ref[hop, 0])
-        select = onehot(column, 2 * TILE)
-        s_ref[...] = select
-        h_ref[...] = dot_nn(select, jnp.concatenate([a[...], b[...]], axis=0)).astype(BF16)
-
-
-def slot_tables(capacity, tiles, count, ids, table, state_one, state_zero):
+    t_ref[...] = dot_nn(onehot(relation - 1, width), table).astype(BF16)
+    column = compact_column(source - 1, (tiles_ref[1, 0], tiles_ref[1, 1]), count_ref[0, 1])
+    s_ref[...] = onehot(column, 2 * TILE).T
+
+
+def tables_two(capacity, tiles, count, ids, table):
     feat = table.shape[1]
     slots = ids.shape[0] * capacity
-    width = -(-table.shape[0] // TILE) * TILE
-
-    def whole(shape):
-        return pl.BlockSpec(shape, lambda i, *_: (0,) * len(shape))
+    return pl.pallas_call(
+        functools.partial(tables_two_kernel, capacity),
+        in_specs=[SMEM, SMEM, VMEM, VMEM],
+        out_specs=[VMEM, VMEM],
+        out_shape=[
+            jax.ShapeDtypeStruct((slots, feat), BF16),
+            jax.ShapeDtypeStruct((2 * TILE, slots), BF16),
+        ],
+        compiler_params=params(),
+        cost_estimate=cost(1e9, 2 << 20),
+        name="tables_two",
+    )(tiles, count, ids, table)
+
+
+def tables_one_kernel(capacity, tiles_ref, count_ref, ids_ref, answer_ref, one_a, one_b, zero_a, zero_b,
+                      s_ref, h_ref, r_ref, total_ref):
+    source, relation = slot_columns(ids_ref[...], capacity, (0, 64))
+    columns = [
+        compact_column(source - 1, (tiles_ref[hop, 0], tiles_ref[hop, 1]), count_ref[0, hop]) for hop in range(2)
+    ]
+    select = onehot(columns[0], 2 * TILE)
+    s_ref[...] = select.T
+    h_ref[...] = dot_nn(select, jnp.concatenate([zero_a[...], zero_b[...]], axis=0)).astype(BF16)
+    states = dot_nn(onehot(columns[1], 2 * TILE), jnp.concatenate([one_a[...], one_b[...]], axis=0)).astype(BF16)
+    turned = onehot(relation - 1, r_ref.shape[0]).T
+    r_ref[...] = turned
+    total_ref[...] = dot_nn(turned, answer_ref[...] * states)
+
+
+def tables_one(capacity, tiles, count, ids, answer, state_one, state_zero, groups):
+    feat = answer.shape[1]
+    slots = ids.shape[0] * capacity
+    width = -(-groups // TILE) * TILE
 
     def tile(hop, k):
         return pl.BlockSpec((TILE, feat), lambda i, tiles, count: (tiles[hop, k], 0))
 
-    shape = jax.ShapeDtypeStruct((slots, feat), BF16)
-    return pl.pallas_call(
-        functools.partial(tables_kernel, capacity),
+    return pl.pallas_call(
+        functools.partial(tables_one_kernel, capacity),
         grid_spec=pltpu.PrefetchScalarGridSpec(
             num_scalar_prefetch=2,
             grid=(1,),
-            in_specs=[whole(ids.shape), whole(table.shape), tile(1, 0), tile(1, 1), tile(0, 0), tile(0, 1)],
-            out_specs=[whole((slots, feat))] * 5 + [whole((slots, width))],
+            in_specs=[whole(ids.shape), whole(answer.shape), tile(1, 0), tile(1, 1), tile(0, 0), tile(0, 1)],
+            out_specs=[whole((2 * TILE, slots)), whole((slots, feat)), whole((width, slots)), whole((width, feat))],
         ),
-        out_shape=[shape] * 5 + [jax.ShapeDtypeStruct((slots, width), BF16)],
-        compiler_params=params(),
-        cost_estimate=cost(2e9, 6 << 20),
-        name="tables",
-    )(tiles, count, ids, table, state_one, state_one, state_zero, state_zero)
+        out_shape=[
+            jax.ShapeDtypeStruct((2 * TILE, slots), BF16),
+            jax.ShapeDtypeStruct((slots, feat), BF16),
+            jax.ShapeDtypeStruct((width, slots), BF16),
+            jax.ShapeDtypeStruct((width, feat), F32),
+        ],
+        compiler_params=params(24 << 20),
+        cost_estimate=cost(2e9, 4 << 20),
+        name="tables_one",
+    )(tiles, count, ids, answer, state_one, state_one, state_zero, state_zero)
 
 
 def contribution_kernel(answer_ref, t_ref, s_ref, out_ref):
-    out_ref[...] = dot_tn(s_ref[...], answer_ref[...] * t_ref[...]).astype(BF16)
+    out_ref[...] = dot_nn(s_ref[...], answer_ref[...] * t_ref[...]).astype(BF16)
 
 
 def contribution(answer, table, select):
@@ -291,38 +372,19 @@
         contribution_kernel,
         in_specs=[VMEM] * 3,
         out_specs=VMEM,
-        out_shape=jax.ShapeDtypeStruct((select.shape[1], answer.shape[1]), BF16),
-        compiler_params=params(),
+        out_shape=jax.ShapeDtypeStruct((select.shape[0], answer.shape[1]), BF16),
+        compiler_params=params(8 << 20),
         cost_estimate=cost(2e8, 3 << 20),
         name="contribution",
     )(answer, table, select)
 
 
-def relation_kernel(answer_ref, h_ref, r_ref, out_ref):
-    out_ref[...] = dot_tn(r_ref[...], answer_ref[...] * h_ref[...])
-
-
-def relation_part(answer, states, select):
-    return pl.pallas_call(
-        relation_kernel,
-        in_specs=[VMEM] * 3,
-        out_specs=VMEM,
-        out_shape=jax.ShapeDtypeStruct((select.shape[1], answer.shape[1]), F32),
-        compiler_params=params(),
-        cost_estimate=cost(4e8, 3 << 20),
-        name="relation_part",
-    )(answer, states, select)
-
-
-def live_kernel(capacity, tiles_ref, count_ref, agg_a, agg_b, state_a, state_b, up_a, up_b, c0, c1, c2, c3,
-                w_in_ref, w_bias_ref, w_out_ref, asked_ref, rest_ref, picked_ref, next_ref, sums_ref,
-                wx, wu, wb, acc_in, acc_out, acc_bias):
-    build_weights(w_in_ref, w_bias_ref, w_out_ref, wx, wu, wb)
+def live_kernel(tiles_ref, count_ref, agg_a, agg_b, state_a, state_b, up_a, up_b, c0, c1, c2, c3,
+                wx, wu, wb, live_ref, rest_ref, picked_ref, next_ref, sums_ref, acc_in, acc_out, acc_bias):
     clear(acc_in, acc_out, acc_bias)
-    count = count_ref[1, 0]
     source = (c0[...].astype(F32) + c1[...].astype(F32)) + (c2[...].astype(F32) + c3[...].astype(F32))
     up = jnp.concatenate([up_a[...], up_b[...]], axis=0) + source
-    keep = (iota((2 * TILE, 1), 0) < TILE) | (count > 1)
+    keep = (iota((2 * TILE, 1), 0) < TILE) | (count_ref[0, 1] > 1)
     up_low = jnp.where(keep, up, 0.0).astype(BF16)
     agg = jnp.concatenate([agg_a[...], agg_b[...]], axis=0)
     state = jnp.concatenate([state_a[...], state_b[...]], axis=0)
@@ -334,30 +396,24 @@
     grad_agg = jnp.concatenate(aggs, axis=1).astype(BF16)
     next_ref[...] = up + jnp.concatenate(states, axis=1)
     store_sums(acc_in, acc_out, acc_bias, sums_ref)
-    asked = slot_columns(asked_ref[:, 0, :], capacity, (0,))[0]
-    column = compact_column(asked, (tiles_ref[1, 0], tiles_ref[1, 1]), count)
-    live = dot_nn(onehot(column, 2 * TILE), grad_agg)
-    picked_ref[...] = jnp.where(column >= 0, live, rest_ref[...].astype(F32)).astype(BF16)
-
-
-def live_pass(capacity, tiles, count, agg, state, up, parts, w_in, w_bias, w_out, asked, rest):
+    picked_ref[...] = (dot_nn(live_ref[...], grad_agg) + rest_ref[...].astype(F32)).astype(BF16)
+
+
+def live_pass(tiles, count, agg, state, up, parts, weights, live, rest):
     feat = agg.shape[1]
-
-    def whole(shape):
-        return pl.BlockSpec(shape, lambda i, *_: (0,) * len(shape))
 
     def tile(k):
         return pl.BlockSpec((TILE, feat), lambda i, tiles, count: (tiles[1, k], 0))
 
     return pl.pallas_call(
-        functools.partial(live_kernel, capacity),
+        live_kernel,
         grid_spec=pltpu.PrefetchScalarGridSpec(
             num_scalar_prefetch=2,
             grid=(1,),
             in_specs=[tile(0), tile(1)] * 3 + [whole(parts[0].shape)] * 4
-            + [whole(w_in.shape), whole(w_bias.shape), whole(w_out.shape), whole(asked.shape), whole(rest.shape)],
+            + [whole(w.shape) for w in weights] + [whole(live.shape), whole(rest.shape)],
             out_specs=[whole(rest.shape), whole((2 * TILE, feat)), whole((SUM_ROWS, WIDE))],
-            scratch_shapes=MLP_SCRATCH,
+            scratch_shapes=scratch(SUM_SHAPES),
         ),
         out_shape=[
             jax.ShapeDtypeStruct(rest.shape, BF16),
@@ -367,37 +423,41 @@
         compiler_params=params(),
         cost_estimate=cost(1.6e9, 4 << 20, 1 << 19),
         name="live",
-    )(tiles, count, agg, agg, state, state, up, up, *parts, w_in, w_bias, w_out, asked, rest)
+    )(tiles, count, agg, agg, state, state, up, up, *parts, *weights, live, rest)
 
 
 GAP = SUM_ROWS
 
 
-def pack_kernel(answer_ref, h_ref, r_ref, before_ref, w2_ref, w1a_ref, w1b_ref, out_ref):
-    total = before_ref[...] + dot_tn(r_ref[...], answer_ref[...] * h_ref[...])
-    used, rows = total.shape[0], out_ref.shape[0]
-    feat = total.shape[1]
-    out_ref[...] = jnp.zeros_like(out_ref)
+def pack_kernel(answer_ref, t_ref, s_ref, h_ref, r_ref, before_ref, w2_ref, w1a_ref, w1b_ref, part_ref, out_ref):
+    answer = answer_ref[...]
+    part_ref[...] = dot_nn(s_ref[...], answer * t_ref[...]).astype(BF16)
+    total = before_ref[...] + dot_nn(r_ref[...], answer * h_ref[...])
+    used, feat = total.shape
+    out_ref[used:, 0:feat] = jnp.zeros((out_ref.shape[0] - used, feat), BF16)
+    out_ref[4 * GAP:, feat:feat + TILE] = jnp.zeros((out_ref.shape[0] - 4 * GAP, TILE), BF16)
     out_ref[0:used, 0:feat] = total.astype(BF16)
     layers = (w1a_ref[...] + w1b_ref[...], w2_ref[...])
     parts = []
     for layer in layers:
         parts += [layer[:, :TILE], layer[:, TILE:]]
-    parts = jnp.concatenate(parts, axis=0).astype(BF16)
-    out_ref[0:4 * GAP, feat:feat + TILE] = parts
-
-
-def pack_sums(answer, states, select, before, w2, w1a, w1b, rows):
+    out_ref[0:4 * GAP, feat:feat + TILE] = jnp.concatenate(parts, axis=0).astype(BF16)
+
+
+def pack_sums(answer, table, select, states, select_rel, before, w2, w1a, w1b, rows):
     feat = answer.shape[1]
     return pl.pallas_call(
         pack_kernel,
-        in_specs=[VMEM] * 7,
-        out_specs=VMEM,
-        out_shape=jax.ShapeDtypeStruct((rows, feat + TILE), BF16),
+        in_specs=[VMEM] * 9,
+        out_specs=[VMEM, VMEM],
+        out_shape=[
+            jax.ShapeDtypeStruct((select.shape[0], feat), BF16),
+            jax.ShapeDtypeStruct((rows, feat + TILE), BF16),
+        ],
         compiler_params=params(),
         cost_estimate=cost(4e8, 4 << 20),
         name="pack_sums",
-    )(answer, states, select, before, w2, w1a, w1b)
+    )(answer, table, select, states, select_rel, before, w2, w1a, w1b)
 
 
 def combine_kernel(feat, scale_relations, scale_weights, in_ref, out_ref):
@@ -428,7 +488,7 @@
         right = in_ref[at + GAP:at + 2 * GAP, feat:feat + TILE].astype(F32)
         both = jnp.concatenate([left, right], axis=1)
         w_in_ref[layer] = both[0:2 * DIM]
-        w_out_ref[layer] = both[2 * DIM:3 * DIM].T
+        w_out_ref[layer] = both[2 * DIM:3 * DIM]
         w_bias_ref[layer:layer + 1, :] = both[3 * DIM:3 * DIM + 1]
 
 
@@ -441,7 +501,7 @@
             jax.ShapeDtypeStruct((groups, feat), F32),
             jax.ShapeDtypeStruct((2, 2 * DIM, WIDE), F32),
             jax.ShapeDtypeStruct((2, WIDE), F32),
-            jax.ShapeDtypeStruct((2, WIDE, DIM), F32),
+            jax.ShapeDtypeStruct((2, DIM, WIDE), F32),
         ],
         compiler_params=params(),
         cost_estimate=cost(1e6, 2 << 20),
@@ -454,7 +514,7 @@
     value = next_ref[...]
     for k in range(2):
         rows = slice(k * TILE, (k + 1) * TILE)
-        is_live = (tile == tiles_ref[1, k]) & (count_ref[1, 0] > k)
+        is_live = (tile == tiles_ref[1, k]) & (count_ref[0, 1] > k)
         value = jnp.where(is_live, live_ref[rows, :], value)
     for k in range(2):
         rows = slice(k * TILE, (k + 1) * TILE)
@@ -469,10 +529,6 @@
 def final_pass(tiles, count, quarter_id, after, live, parts, quarter):
     feat = after.shape[1]
     blocks = quarter // TILE
-
-    def whole(shape):
-        return pl.BlockSpec(shape, lambda i, *_: (0,) * len(shape))
-
     return pl.pallas_call(
         final_kernel,
         grid_spec=pltpu.PrefetchScalarGridSpec(
@@ -511,10 +567,9 @@
         ]
         return [part] + turned
 
-    def layer(index):
-        return update_in[index], update_bias[index][None, :], update_out[index]
-
     row = lambda values: values.reshape(1, edges)
+    count = jnp.swapaxes(frontier_count, 0, 1)
+    weights = (update_in, update_bias, jnp.swapaxes(update_out, 1, 2))
     request, ids = pl.pallas_call(
         functools.partial(slots_kernel, peers),
         in_specs=[VMEM] * 4,
@@ -523,40 +578,44 @@
             jax.ShapeDtypeStruct((peers, 1, 128), F32),
             jax.ShapeDtypeStruct((peers, 128), F32),
         ],
-        compiler_params=params(),
+        compiler_params=params(8 << 20),
         cost_estimate=cost(1e8, 1 << 20),
         name="slots",
     )(row(edge_owner), row(edge_target), row(edge_source), row(edge_relation))
     asked = exchange(request)
 
-    upstream_one, picked_two, sums_two = dense_pass(
-        False, capacity, frontier_tiles, frontier_count, aggregate_two, state_one, cotangent, *layer(1), asked
+    upstream_one, picked_two, sums_two = first_pass(
+        capacity, aggregate_two, state_one, cotangent, *weights, asked
     )
     answered_two = exchange(picked_two.reshape(peers, capacity, feat)).reshape(slots, feat)
-    after, rest, sums_rest = dense_pass(
-        True, capacity, frontier_tiles, frontier_count, aggregate_one, state_zero, upstream_one, *layer(0), asked
+    after, rest, sums_rest, live, *built = rest_pass(
+        capacity, frontier_tiles, count, aggregate_one, state_zero, upstream_one, *weights, asked
     )
-    edge_table, select_two, states_two, select_one, states_one, select_rel = slot_tables(
-        capacity, frontier_tiles, frontier_count, ids, relation_table, state_one, state_zero
+    edge_table, select_two = tables_two(capacity, frontier_tiles, count, ids, relation_table)
+    answered_two, rest, edge_table, select_two = lax.optimization_barrier(
+        (answered_two, rest, edge_table, select_two)
     )
     parts = over_rel(contribution(answered_two, edge_table, select_two))
     picked_one, after_live, sums_live = live_pass(
-        capacity, frontier_tiles, frontier_count, aggregate_one, state_zero, upstream_one, parts, *layer(0), asked, rest
+        frontier_tiles, count, aggregate_one, state_zero, upstream_one, parts, built, live, rest
     )
     answered_one = exchange(picked_one.reshape(peers, capacity, feat)).reshape(slots, feat)
-    relation_two = relation_part(answered_two, states_two, select_rel)
-
-    parts = over_rel(contribution(answered_one, edge_table, select_one))
-    packed = pack_sums(
-        answered_one, states_one, select_rel, relation_two, sums_two, sums_rest, sums_live, sum_rows
+    select_one, states_one, select_rel, relation_two = tables_one(
+        capacity, frontier_tiles, count, ids, answered_two, state_one, state_zero, groups
     )
+    part, packed = pack_sums(
+        answered_one, edge_table, select_one, states_one, select_rel, relation_two,
+        sums_two, sums_rest, sums_live, sum_rows,
+    )
+    parts = over_rel(part)
     scale_weights = 1.0 / math.sqrt(block_rows * peers * QUERIES)
     scale_relations = math.sqrt(groups * group_size / (edges * peers * group_size))
     chunks = exchange(packed.reshape(peers, 8, feat + TILE))
     gathered = exchange(combine(chunks, feat, scale_relations, scale_weights)).reshape(sum_rows, feat + TILE)
     quarter_id = lax.axis_index("rel").astype(jnp.int32).reshape(1)
-    grad_zero = final_pass(frontier_tiles, frontier_count, quarter_id, after, after_live, parts, quarter)
-    return (grad_zero,) + tuple(unpack(gathered, groups, feat))
+    grad_zero = final_pass(frontier_tiles, count, quarter_id, after, after_live, parts, quarter)
+    relation, grad_in, grad_bias, grad_out = unpack(gathered, groups, feat)
+    return grad_zero, relation, grad_in, grad_bias, jnp.swapaxes(grad_out, 1, 2)
 
 
 def solution(mesh):

time: 179 us -> 167 us (0.933)
  blocking collectives: 20.9 us -> 42.8 us
  Pallas kernels: 55.3 us -> 33.5 us
  local copies, waits for them, and re-layouts: 12.4 us -> 26 us
  waiting for transfers between devices: 48.3 us -> 34.7 us
  starting transfers between devices: 40.1 us -> 27.8 us
    all_to_all x1 -> x2, blocking collectives: 20.9 us -> 42.8 us  [exchange(): lax.all_to_all(chunks, 'ent', split_axis=0, concat_axis=0, tiled=True)]
    unnamed x24 -> x96, local copies, waits for them, and re-layouts: 8.93 us -> 26 us
    all_to_all x4 -> x3, waiting for transfers between devices: 40.2 us -> 25.1 us  [exchange(): lax.all_to_all(chunks, 'ent', split_axis=0, concat_axis=0, tiled=True)]
    all_to_all x4 -> x3, starting transfers between devices: 32.9 us -> 18.1 us  [exchange(): lax.all_to_all(chunks, 'ent', split_axis=0, concat_axis=0, tiled=True)]
    pallas_call x6, Pallas kernels: 41.6 us -> 29.6 us  [the longest x1 10.6 us: rest_pass(): pl.pallas_call(functools.partial(rest_kernel, capacity), grid=(rows // bl...]
    pallas_call x2 -> x1, Pallas kernels: 5.36 us -> 0.38 us  [contribution(): pl.pallas_call(contribution_kernel, in_specs=[VMEM] * 3, out_specs=VMEM,...]
    ppermute x6, starting transfers between devices: 7.18 us -> 9.67 us  [over_rel(): lax.ppermute(part, 'rel', [(i, (i + k) % group_size) for i in range(group...]
    slice x2 -> x0, local copies, waits for them, and re-layouts: 2.09 us -> none  [layer(): return (update_in[index], update_bias[index][None, :], update_out[index])]
  transfers between devices with their start and end apart: 10 -> 9, of which waited for: 6 -> 7; matrix products, arithmetic and copies ran while one was open for 4% -> 0% of each run, Pallas kernels for 15% -> 10%
where the time goes in v2:
time: 167 us; the launch traced here: 166 us
  blocking collectives  42.8 us (26%)
  waiting for transfers between devices  34.7 us (21%)
  Pallas kernels  33.5 us (20%)
  starting transfers between devices  27.8 us (17%)
  local copies, waits for them, and re-layouts  26 us (16%)
    all_to_all x2, blocking collectives, exchange(): lax.all_to_all(chunks, 'ent', split_axis=0, concat_axis=0, tiled=True)  42.8 us
    unnamed x96, local copies, waits for them, and re-layouts  26 us
    all_to_all x3, waiting for transfers between devices, exchange(): lax.all_to_all(chunks, 'ent', split_axis=0, concat_axis=0, tiled=True)  25.1 us
    all_to_all x3, starting transfers between devices, exchange(): lax.all_to_all(chunks, 'ent', split_axis=0, concat_axis=0, tiled=True)  18.1 us
    pallas_call x1, Pallas kernels, rest_pass(): pl.pallas_call(functools.partial(rest_kernel, capacity), grid=(rows // bl...  10.6 us
    pallas_call x1, Pallas kernels, first_pass(): pl.pallas_call(functools.partial(first_kernel, capacity), grid=(rows // b...  10.3 us
    ppermute x6, starting transfers between devices, over_rel(): lax.ppermute(part, 'rel', [(i, (i + k) % group_size) for i in range(group...  9.67 us
    ppermute x6, waiting for transfers between devices, over_rel(): lax.ppermute(part, 'rel', [(i, (i + k) % group_size) for i in range(group...  9.58 us
  transfers between devices with their start and end apart: 9, of which 7 were waited for; matrix products, arithmetic and copies ran while one was open for 0% of the time, Pallas kernels for 10%

profile of v2, /device:TPU:1, one launch (start us, length us, event | category | flops | bytes accessed | tf_op | source)
XLA Modules:
  0.0 165.8 jit_solution(4587204541501833567)
XLA Ops:
  3.8 22.1 %all_to_all.25.asked_ref = f32[64,1,128]{2,1,0:T(1,128)S(1)} all-to-all(f32[64,1,128]{2,1,0:T(1,128)S(1)} %get-tuple-element.36), channel_id=1, replica_groups=mesh['ent'=64,'rel'=4] {'ent'}, dimensions={0} | all-to-all | bytes 65536 | tf_op jit(solution)/shard_map/all_to_all | solution.py:561
  31.3 10.3 %first.1 = (f32[1024,256]{1,0:T(8,128)S(1)}, bf16[1536,256]{1,0:T(8,128)(2,1)}, f32[104,256]{1,0:T(8,128)S(1)}) custom-call(bf16[1024,256]{1,0:T(8,128)(2,1)S(1)} %copy-done.31, bf16[1024,256]{1,0:T(8,128)(2,1)S(1)} %copy-done.33, bf16[1024,256]{1,0:T(8,128)(2,1)S(1)} %copy-done.32, bf16[2,64,256]{2,1,0:T(8,128)(2,1)S(1)} %copy-done.36, ...), custom_call_target="tpu_custom_call" | custom-call | flops 5400000000 | bytes 4194304 | tf_op jit(solution)/shard_map/first/pallas_call | solution.py:226
  41.7 4.9 %all-to-all-start.1 = ((bf16[64,24,256]{2,1,0:T(8,128)(2,1)}), bf16[64,24,256]{2,1,0:T(8,128)(2,1)S(1)}, u32[]{:S(2)}, u32[]{:S(2)}) async-start(bf16[64,24,256]{2,1,0:T(8,128)(2,1)} %bitcast.7), calls=%async_computation.1 | async-start | bytes 1572864 | tf_op jit(solution)/shard_map/all_to_all | solution.py:561
  46.7 2.2 %tables_two.1 = (bf16[1536,256]{1,0:T(8,128)(2,1)S(1)}, bf16[256,1536]{1,0:T(8,128)(2,1)S(1)}) custom-call(s32[2,2]{1,0:T(2,128)S(1)} %copy-done.27, s32[1,2]{1,0:T(1,128)S(1)} %bitcast.20, f32[64,128]{1,0:T(8,128)S(1)} %get-tuple-element.41.ids_ref, bf16[328,256]{1,0:T(8,128)(2,1)S(1)} %copy-done.35), custom_call_target="tpu_custom_call" | custom-call | flops 1000000000 | bytes 2097152 | tf_op jit(solution)/shard_map/tables_two/pallas_call | solution.py:309
  49.8 10.6 %rest.1 = (f32[1024,256]{1,0:T(8,128)S(1)}, bf16[1536,256]{1,0:T(8,128)(2,1)S(1)}, f32[104,256]{1,0:T(8,128)S(1)}, bf16[1536,256]{1,0:T(8,128)(2,1)S(1)}, bf16[2...) custom-call(s32[2,2]{1,0:T(2,128)S(1)} %copy-done.27, s32[1,2]{1,0:T(1,128)S(1)} %bitcast.21, ...), custom_call_target="tpu_custom_call" | custom-call | flops 5400000000 | bytes 4194304 | tf_op jit(solution)/shard_map/rest/pallas_call | solution.py:275
  64.6 5.0 %all-to-all-done.1 = bf16[64,24,256]{2,1,0:T(8,128)(2,1)S(1)} async-done(((bf16[64,24,256]{2,1,0:T(8,128)(2,1)}), bf16[64,24,256]{2,1,0:T(8,128)(2,1)S(1)}, u32[]{:S(2)}, u32[]{:S(2)}) %all-to-all-start.1) | async-done | bytes 786464 | tf_op jit(solution)/shard_map/all_to_all | solution.py:561
  69.6 1.1 copy-done.17
  71.1 1.6 collective-permute-start
  72.7 2.6 %collective-permute-start.1 = (bf16[256,256]{1,0:T(8,128)(2,1)S(1)}, bf16[256,256]{1,0:T(8,128)(2,1)S(1)}, u32[]{:S(2)}, u32[]{:S(2)}) collective-permute-start(bf16[256,256]{1,0:T(8,128)(2,1)S(1)} %contribution.1.c0), channel_id=1, source_target_pairs={{0,2},{1,3},{2,0},{3,1},{4,6},{5,7},{6,4},{7,5},{8,10},{9,11},{10,... | collective-permute-start | bytes 393224 | tf_op jit(solution)/shard_map/ppermute | solution.py:565
  77.4 3.9 %collective-permute-done.1.c2 = bf16[256,256]{1,0:T(8,128)(2,1)S(1)} collective-permute-done((bf16[256,256]{1,0:T(8,128)(2,1)S(1)}, bf16[256,256]{1,0:T(8,128)(2,1)S(1)}, u32[]{:S(2)}, u32[]{:S(2)}) %collective-permute-start.1) | collective-permute-done | bytes 131104 | tf_op jit(solution)/shard_map/ppermute | solution.py:565
  82.4 2.9 %live.1 = (bf16[1536,256]{1,0:T(8,128)(2,1)S(1)}, f32[256,256]{1,0:T(8,128)S(1)}, f32[104,256]{1,0:T(8,128)S(1)}) custom-call(s32[2,2]{1,0:T(2,128)S(1)} %copy-done.27, s32[1,2]{1,0:T(1,128)S(1)} %bitcast.22, bf16[1024,256]{1,0:T(8,128)(2,1)S(1)} %copy-done, bf16[1024,256]{1,0:T(8,128)(2,1)S(1)} %copy-done, bf16[1024,256]{1,0:T(8,128)(2,1)S(1)} %copy-done.2, ...), custom_call_target="tpu_custom_call" | custom-call | flops 1600000000 | bytes 4194304 | tf_op jit(solution)/shard_map/live/pallas_call | solution.py:408
  87.5 7.0 %all-to-all-start.2 = ((bf16[64,24,256]{2,1,0:T(8,128)(2,1)}), bf16[64,24,256]{2,1,0:T(8,128)(2,1)S(1)}, u32[]{:S(2)}, u32[]{:S(2)}) async-start(bf16[64,24,256]{2,1,0:T(8,128)(2,1)} %bitcast.18), calls=%async_computation.2 | async-start | bytes 1572864 | tf_op jit(solution)/shard_map/all_to_all | solution.py:561
  95.6 2.9 %tables_one.1 = (bf16[256,1536]{1,0:T(8,128)(2,1)S(1)}, bf16[1536,256]{1,0:T(8,128)(2,1)S(1)}, bf16[384,1536]{1,0:T(8,128)(2,1)S(1)}, f32[384,256]{1,0:T(8,128)S(1)}) custom-call(s32[2,2]{1,0:T(2,128)S(1)} %copy-done.27, s32[1,2]{1,0:T(1,128)S(1)} %bitcast.23, f32[64,128]{1,0:T(8,128)S(1)} %copy-done.47, bf16[1536,256]{1,0:T(8,128)(2,1)S(1)} %bitcast.15, ...), custom_call_target="tpu_custom_call" | custom-call | flops 2000000000 | bytes 4194304 | tf_op jit(solution)/shard_map/tables_one/pallas_call | solution.py:346
  101.3 16.1 %all-to-all-done.2 = bf16[64,24,256]{2,1,0:T(8,128)(2,1)S(1)} async-done(((bf16[64,24,256]{2,1,0:T(8,128)(2,1)}), bf16[64,24,256]{2,1,0:T(8,128)(2,1)S(1)}, u32[]{:S(2)}, u32[]{:S(2)}) %all-to-all-start.2) | async-done | bytes 786464 | tf_op jit(solution)/shard_map/all_to_all | solution.py:561
  117.5 1.3 copy-done.5
  119.9 1.1 copy-done.15
  122.6 20.7 %all_to_all.26.in_ref = bf16[64,8,384]{2,1,0:T(8,128)(2,1)S(1)} all-to-all(bf16[64,8,384]{2,1,0:T(8,128)(2,1)S(1)} %bitcast.19), channel_id=1, replica_groups=mesh['ent'=64,'rel'=4] {'ent'}, dimensions={0} | all-to-all | bytes 786432 | tf_op jit(solution)/shard_map/all_to_all | solution.py:561
  144.2 6.2 %all-to-all-start.4 = ((bf16[64,8,384]{2,1,0:T(8,128)(2,1)}), bf16[64,8,384]{2,1,0:T(8,128)(2,1)S(1)}, u32[]{:S(2)}, u32[]{:S(2)}) async-start(bf16[64,8,384]{2,1,0:T(8,128)(2,1)} %combine.1), calls=%async_computation.4 | async-start | bytes 786432 | tf_op jit(solution)/shard_map/all_to_all | solution.py:561
  151.4 2.1 %collective-permute-start.4 = (bf16[256,256]{1,0:T(8,128)(2,1)S(1)}, bf16[256,256]{1,0:T(8,128)(2,1)S(1)}, u32[]{:S(2)}, u32[]{:S(2)}) collective-permute-start(bf16[256,256]{1,0:T(8,128)(2,1)S(1)} %get-tuple-element.61.c0), channel_id=1, source_target_pairs={{0,2},{1,3},{2,0},{3,1},{4,6},{5,7},{6,4},{7,5},{8,10},{9,11},{10,... | collective-permute-start | bytes 393224 | tf_op jit(solution)/shard_map/ppermute | solution.py:565
  153.6 1.3 collective-permute-start.5
  154.8 1.5 collective-permute-done.3.c1
  156.3 3.2 %collective-permute-done.4.c2 = bf16[256,256]{1,0:T(8,128)(2,1)S(1)} collective-permute-done((bf16[256,256]{1,0:T(8,128)(2,1)S(1)}, bf16[256,256]{1,0:T(8,128)(2,1)S(1)}, u32[]{:S(2)}, u32[]{:S(2)}) %collective-permute-start.4) | collective-permute-done | bytes 131104 | tf_op jit(solution)/shard_map/ppermute | solution.py:565
  159.5 1.4 final.1
  160.9 4.0 %all-to-all-done.4 = bf16[64,8,384]{2,1,0:T(8,128)(2,1)S(1)} async-done(((bf16[64,8,384]{2,1,0:T(8,128)(2,1)}), bf16[64,8,384]{2,1,0:T(8,128)(2,1)S(1)}, u32[]{:S(2)}, u32[]{:S(2)}) %all-to-all-start.4) | async-done | bytes 393248 | tf_op jit(solution)/shard_map/all_to_all | solution.py:561
  (103 shorter events, 28.7 us)
Async XLA Ops:
  3.8 42.7 %copy-start.46 = (f32[64,128]{1,0:T(8,128)}, f32[64,128]{1,0:T(8,128)S(1)}, u32[]{:S(2)}) copy-start(f32[64,128]{1,0:T(8,128)S(1)} %get-tuple-element.41.ids_ref) | copy-start | bytes 98308
  41.7 4.9 %copy-start.27 = (s32[2,2]{1,0:T(2,128)S(1)}, s32[2,2]{1,0:T(2,128)}, u32[]{:S(2)}) copy-start(s32[2,2]{1,0:T(2,128)} %tiles_ref.9) | copy-start | bytes 52
  41.7 4.9 %copy-start.28 = (s32[2,1]{0,1:T(1,128)S(1)}, s32[2,1]{0,1:T(1,128)}, u32[]{:S(2)}) copy-start(s32[2,1]{0,1:T(1,128)} %param.25) | copy-start | bytes 28
  41.7 4.9 %copy-start.35 = (bf16[328,256]{1,0:T(8,128)(2,1)S(1)}, bf16[328,256]{1,0:T(8,128)(2,1)}, u32[]{:S(2)}) copy-start(bf16[328,256]{1,0:T(8,128)(2,1)} %table_ref.1) | copy-start | bytes 503812
  41.7 27.9 %all-to-all-start.1 = ((bf16[64,24,256]{2,1,0:T(8,128)(2,1)}), bf16[64,24,256]{2,1,0:T(8,128)(2,1)S(1)}, u32[]{:S(2)}, u32[]{:S(2)}) async-start(bf16[64,24,256]{2,1,0:T(8,128)(2,1)} %bitcast.7), calls=%async_computation.1 | async-start | bytes 1572864 | tf_op jit(solution)/shard_map/all_to_all | solution.py:561
  46.6 3.2 %copy-start = (bf16[1024,256]{1,0:T(8,128)(2,1)S(1)}, bf16[1024,256]{1,0:T(8,128)(2,1)}, u32[]{:S(2)}) copy-start(bf16[1024,256]{1,0:T(8,128)(2,1)} %agg_b.1) | copy-start | bytes 1572868
  46.6 3.2 %copy-start.1 = (bf16[1024,256]{1,0:T(8,128)(2,1)S(1)}, bf16[1024,256]{1,0:T(8,128)(2,1)}, u32[]{:S(2)}) copy-start(bf16[1024,256]{1,0:T(8,128)(2,1)} %zero_b.1) | copy-start | bytes 1572868
  70.7 10.6 %copy-start.2 = (bf16[1024,256]{1,0:T(8,128)(2,1)S(1)}, bf16[1024,256]{1,0:T(8,128)(2,1)}, u32[]{:S(2)}) copy-start(bf16[1024,256]{1,0:T(8,128)(2,1)} %zero_b.1) | copy-start | bytes 1572868
  70.7 10.6 %copy-start.9 = (bf16[1536,256]{1,0:T(8,128)(2,1)S(1)}, bf16[1536,256]{1,0:T(8,128)(2,1)}, u32[]{:S(2)}) copy-start(bf16[1536,256]{1,0:T(8,128)(2,1)} %copy-done.8) | copy-start | bytes 2359300
  70.7 10.6 %copy-start.11 = (bf16[1536,256]{1,0:T(8,128)(2,1)S(1)}, bf16[1536,256]{1,0:T(8,128)(2,1)}, u32[]{:S(2)}) copy-start(bf16[1536,256]{1,0:T(8,128)(2,1)} %copy-done.10) | copy-start | bytes 2359300
  70.7 10.6 %copy-start.30 = (s32[2,1]{0,1:T(1,128)S(1)}, s32[2,1]{0,1:T(1,128)}, u32[]{:S(2)}) copy-start(s32[2,1]{0,1:T(1,128)} %param.25) | copy-start | bytes 28
  71.1 6.2 %collective-permute-start = (bf16[256,256]{1,0:T(8,128)(2,1)S(1)}, bf16[256,256]{1,0:T(8,128)(2,1)S(1)}, u32[]{:S(2)}, u32[]{:S(2)}) collective-permute-start(bf16[256,256]{1,0:T(8,128)(2,1)S(1)} %contribution.1.c0), channel_id=1, source_target_pairs={{0,1},{1,2},{2,3},{3,0},{4,5},{5,6},{6,7},{7,4},{8,9},{9,10},{10,1... | collective-permute-start | bytes 393224 | tf_op jit(solution)/shard_map/ppermute | solution.py:565
  72.7 8.6 %collective-permute-start.1 = (bf16[256,256]{1,0:T(8,128)(2,1)S(1)}, bf16[256,256]{1,0:T(8,128)(2,1)S(1)}, u32[]{:S(2)}, u32[]{:S(2)}) collective-permute-start(bf16[256,256]{1,0:T(8,128)(2,1)S(1)} %contribution.1.c0), channel_id=1, source_target_pairs={{0,2},{1,3},{2,0},{3,1},{4,6},{5,7},{6,4},{7,5},{8,10},{9,11},{10,... | collective-permute-start | bytes 393224 | tf_op jit(solution)/shard_map/ppermute | solution.py:565
  75.3 6.0 %collective-permute-start.2 = (bf16[256,256]{1,0:T(8,128)(2,1)S(1)}, bf16[256,256]{1,0:T(8,128)(2,1)S(1)}, u32[]{:S(2)}, u32[]{:S(2)}) collective-permute-start(bf16[256,256]{1,0:T(8,128)(2,1)S(1)} %contribution.1.c0), channel_id=1, source_target_pairs={{0,3},{1,0},{2,1},{3,2},{4,7},{5,4},{6,5},{7,6},{8,11},{9,8},{10,9... | collective-permute-start | bytes 393224 | tf_op jit(solution)/shard_map/ppermute | solution.py:565
  87.5 7.0 %copy-start.3 = (bf16[1024,256]{1,0:T(8,128)(2,1)S(1)}, bf16[1024,256]{1,0:T(8,128)(2,1)}, u32[]{:S(2)}) copy-start(bf16[1024,256]{1,0:T(8,128)(2,1)} %zero_b.1) | copy-start | bytes 1572868
  87.5 7.0 %copy-start.47 = (f32[64,128]{1,0:T(8,128)S(1)}, f32[64,128]{1,0:T(8,128)}, u32[]{:S(2)}) copy-start(f32[64,128]{1,0:T(8,128)} %copy-done.46) | copy-start | bytes 98308
  87.5 29.9 %all-to-all-start.2 = ((bf16[64,24,256]{2,1,0:T(8,128)(2,1)}), bf16[64,24,256]{2,1,0:T(8,128)(2,1)S(1)}, u32[]{:S(2)}, u32[]{:S(2)}) async-start(bf16[64,24,256]{2,1,0:T(8,128)(2,1)} %bitcast.18), calls=%async_computation.2 | async-start | bytes 1572864 | tf_op jit(solution)/shard_map/all_to_all | solution.py:561
  95.6 21.9 %copy-start.24 = (f32[104,256]{1,0:T(8,128)S(1)}, f32[104,256]{1,0:T(8,128)}, u32[]{:S(2)}) copy-start(f32[104,256]{1,0:T(8,128)} %copy-done.23) | copy-start | bytes 319492
  122.6 36.9 %copy-start.7 = (f32[1024,256]{1,0:T(8,128)S(1)}, f32[1024,256]{1,0:T(8,128)}, u32[]{:S(2)}) copy-start(f32[1024,256]{1,0:T(8,128)} %copy-done.6) | copy-start | bytes 3145732
  122.6 36.9 %copy-start.22 = (f32[256,256]{1,0:T(8,128)S(1)}, f32[256,256]{1,0:T(8,128)}, u32[]{:S(2)}) copy-start(f32[256,256]{1,0:T(8,128)} %copy-done.21) | copy-start | bytes 786436
  144.2 20.8 %all-to-all-start.4 = ((bf16[64,8,384]{2,1,0:T(8,128)(2,1)}), bf16[64,8,384]{2,1,0:T(8,128)(2,1)S(1)}, u32[]{:S(2)}, u32[]{:S(2)}) async-start(bf16[64,8,384]{2,1,0:T(8,128)(2,1)} %combine.1), calls=%async_computation.4 | async-start | bytes 786432 | tf_op jit(solution)/shard_map/all_to_all | solution.py:561
  150.4 5.9 %collective-permute-start.3 = (bf16[256,256]{1,0:T(8,128)(2,1)S(1)}, bf16[256,256]{1,0:T(8,128)(2,1)S(1)}, u32[]{:S(2)}, u32[]{:S(2)}) collective-permute-start(bf16[256,256]{1,0:T(8,128)(2,1)S(1)} %get-tuple-element.61.c0), channel_id=1, source_target_pairs={{0,1},{1,2},{2,3},{3,0},{4,5},{5,6},{6,7},{7,4},{8,9},{9,10},{10,1... | collective-permute-start | bytes 393224 | tf_op jit(solution)/shard_map/ppermute | solution.py:565
  151.4 8.1 %collective-permute-start.4 = (bf16[256,256]{1,0:T(8,128)(2,1)S(1)}, bf16[256,256]{1,0:T(8,128)(2,1)S(1)}, u32[]{:S(2)}, u32[]{:S(2)}) collective-permute-start(bf16[256,256]{1,0:T(8,128)(2,1)S(1)} %get-tuple-element.61.c0), channel_id=1, source_target_pairs={{0,2},{1,3},{2,0},{3,1},{4,6},{5,7},{6,4},{7,5},{8,10},{9,11},{10,... | collective-permute-start | bytes 393224 | tf_op jit(solution)/shard_map/ppermute | solution.py:565
  153.6 5.9 %collective-permute-start.5 = (bf16[256,256]{1,0:T(8,128)(2,1)S(1)}, bf16[256,256]{1,0:T(8,128)(2,1)S(1)}, u32[]{:S(2)}, u32[]{:S(2)}) collective-permute-start(bf16[256,256]{1,0:T(8,128)(2,1)S(1)} %get-tuple-element.61.c0), channel_id=1, source_target_pairs={{0,3},{1,0},{2,1},{3,2},{4,7},{5,4},{6,5},{7,6},{8,11},{9,8},{10,9... | collective-permute-start | bytes 393224 | tf_op jit(solution)/shard_map/ppermute | solution.py:565
  (33 other events, 38.5 us)

commit v3 on v2

--- a/solution.py
+++ b/solution.py
@@ -17,6 +17,11 @@
 BF16 = jnp.bfloat16
 VMEM = pl.BlockSpec(memory_space=pltpu.VMEM)
 SMEM = pl.BlockSpec(memory_space=pltpu.SMEM)
+HBM = pl.BlockSpec(memory_space=pltpu.HBM)
+
+
+def in_hbm(array):
+    return pltpu.with_memory_space_constraint(array, pltpu.HBM)
 
 
 def iota(shape, dim):
@@ -43,7 +48,14 @@
     return pl.CostEstimate(flops=int(flops), bytes_accessed=int(nbytes), transcendentals=int(trans))
 
 
-def slots_kernel(peers, owner_ref, target_ref, source_ref, relation_ref, request_ref, ids_ref):
+def slots_kernel(peers, owner_hbm, target_hbm, source_hbm, relation_hbm, request_ref, ids_ref,
+                 owner_ref, target_ref, source_ref, relation_ref, sems):
+    pairs = ((owner_hbm, owner_ref), (target_hbm, target_ref), (source_hbm, source_ref), (relation_hbm, relation_ref))
+    copies = [pltpu.make_async_copy(a, b, sems.at[i]) for i, (a, b) in enumerate(pairs)]
+    for copy in copies:
+        copy.start()
+    for copy in copies:
+        copy.wait()
     edges = owner_ref.shape[1]
     owner = owner_ref[...]
     hit = (iota((peers, edges), 0) == owner).astype(F32)
@@ -198,47 +210,56 @@
     next_ref[...] = up + jnp.concatenate(states, axis=1)
 
 
-def first_kernel(capacity, agg_ref, state_ref, up_ref, w_in_ref, w_bias_ref, w_out_ref, asked_ref,
-                 next_ref, picked_ref, sums_ref, wx, wu, wb, acc_in, acc_out, acc_bias, grad_agg):
-    step = pl.program_id(0)
-
-    @pl.when(step == 0)
-    def _():
-        build_weights(1, w_in_ref, w_bias_ref, w_out_ref, wx, wu, wb)
-        clear(acc_in, acc_out, acc_bias)
-
-    up_low = up_ref[...]
-    dense_step(step, agg_ref, state_ref, up_low.astype(F32), up_low, wx, wu, wb, acc_in, acc_out, acc_bias,
-               grad_agg, next_ref)
-
-    @pl.when(step == pl.num_programs(0) - 1)
-    def _():
-        store_sums(acc_in, acc_out, acc_bias, sums_ref)
-        asked = slot_columns(asked_ref[:, 0, :], capacity, (0,))[0]
-        pick_rows(asked, grad_agg, picked_ref)
+def first_kernel(capacity, blocks, agg_hbm, state_hbm, up_hbm, w_in_ref, w_bias_ref, w_out_ref, asked_ref,
+                 next_ref, picked_ref, sums_ref, wx, wu, wb, acc_in, acc_out, acc_bias, grad_agg,
+                 agg_buf, state_buf, up_buf, sems):
+    rows = agg_hbm.shape[0] // blocks
+
+    def copies(step):
+        part = pl.ds(pl.multiple_of(step * rows, rows), rows)
+        pairs = ((agg_hbm, agg_buf), (state_hbm, state_buf), (up_hbm, up_buf))
+        return [pltpu.make_async_copy(a.at[part], b.at[part], sems.at[step, i]) for i, (a, b) in enumerate(pairs)]
+
+    for step in range(blocks):
+        for copy in copies(step):
+            copy.start()
+    build_weights(1, w_in_ref, w_bias_ref, w_out_ref, wx, wu, wb)
+    clear(acc_in, acc_out, acc_bias)
+
+    @pl.loop(0, blocks)
+    def _(step):
+        for copy in copies(step):
+            copy.wait()
+        part = pl.ds(pl.multiple_of(step * rows, rows), rows)
+        up_low = up_buf[part, :]
+        dense_step(step, agg_buf.at[part], state_buf.at[part], up_low.astype(F32), up_low, wx, wu, wb,
+                   acc_in, acc_out, acc_bias, grad_agg, next_ref.at[part])
+
+    store_sums(acc_in, acc_out, acc_bias, sums_ref)
+    asked = slot_columns(asked_ref[:, 0, :], capacity, (0,))[0]
+    pick_rows(asked, grad_agg, picked_ref)
 
 
 def first_pass(capacity, agg, state, up, w_in, w_bias, w_out, asked):
     rows, feat = agg.shape
     slots = asked.shape[0] * capacity
-    block = 256
-    row_spec = pl.BlockSpec((block, feat), lambda i: (i, 0))
-    return pl.pallas_call(
-        functools.partial(first_kernel, capacity),
-        grid=(rows // block,),
-        in_specs=[row_spec, row_spec, row_spec, whole(w_in.shape), whole(w_bias.shape), whole(w_out.shape),
-                  whole(asked.shape)],
-        out_specs=[row_spec, whole((slots, feat)), whole((SUM_ROWS, WIDE))],
+    blocks = rows // 256
+    return pl.pallas_call(
+        functools.partial(first_kernel, capacity, blocks),
+        in_specs=[HBM, HBM, HBM, VMEM, VMEM, VMEM, VMEM],
+        out_specs=[VMEM] * 3,
         out_shape=[
             jax.ShapeDtypeStruct((rows, feat), F32),
             jax.ShapeDtypeStruct((slots, feat), BF16),
             jax.ShapeDtypeStruct((SUM_ROWS, WIDE), F32),
         ],
-        scratch_shapes=scratch(WEIGHT_SHAPES + SUM_SHAPES) + [pltpu.VMEM((rows, feat), BF16)],
+        scratch_shapes=scratch(WEIGHT_SHAPES + SUM_SHAPES)
+        + [pltpu.VMEM((rows, feat), BF16)] * 4
+        + [pltpu.SemaphoreType.DMA((blocks, 3))],
         compiler_params=params(),
         cost_estimate=cost(5.4e9, 4 << 20, 2 << 20),
         name="first",
-    )(agg, state, up, w_in, w_bias, w_out, asked)
+    )(in_hbm(agg), in_hbm(state), in_hbm(up), w_in, w_bias, w_out, asked)
 
 
 def rest_kernel(capacity, tiles_ref, count_ref, agg_ref, state_ref, up_ref, w_in_ref, w_bias_ref, w_out_ref,
@@ -277,30 +298,38 @@
         grid=(rows // block,),
         in_specs=[SMEM, SMEM, row_spec, row_spec, row_spec, whole(w_in.shape), whole(w_bias.shape),
                   whole(w_out.shape), whole(asked.shape)],
-        out_specs=[row_spec, whole((slots, feat)), whole((SUM_ROWS, WIDE)), whole((slots, 2 * TILE))]
-        + [whole(shape) for shape, _ in WEIGHT_SHAPES],
+        out_specs=[row_spec, whole((slots, feat)), whole((SUM_ROWS, WIDE)), whole((slots, 2 * TILE))],
         out_shape=[
             jax.ShapeDtypeStruct((rows, feat), F32),
             jax.ShapeDtypeStruct((slots, feat), BF16),
             jax.ShapeDtypeStruct((SUM_ROWS, WIDE), F32),
             jax.ShapeDtypeStruct((slots, 2 * TILE), BF16),
-        ]
-        + [jax.ShapeDtypeStruct(shape, dtype) for shape, dtype in WEIGHT_SHAPES],
-        scratch_shapes=scratch(SUM_SHAPES) + [pltpu.VMEM((rows, feat), BF16)],
+        ],
+        scratch_shapes=scratch(WEIGHT_SHAPES + SUM_SHAPES) + [pltpu.VMEM((rows, feat), BF16)],
         compiler_params=params(),
         cost_estimate=cost(5.4e9, 4 << 20, 2 << 20),
         name="rest",
     )(tiles, count, agg, state, up, w_in, w_bias, w_out, asked)
 
 
-def tables_two_kernel(capacity, tiles_ref, count_ref, ids_ref, table_ref, t_ref, s_ref):
+def as_row(column):
+    return jnp.broadcast_to(column.astype(F32), (column.shape[0], TILE)).T[0:8].astype(jnp.int32)
+
+
+def onehot_rows(row, width):
+    return (iota((width, row.shape[1]), 0) == row).astype(F32).astype(BF16)
+
+
+def tables_two_kernel(capacity, tiles_ref, count_ref, ids_ref, table_ref, t_ref, rows_ref):
     source, relation = slot_columns(ids_ref[...], capacity, (0, 64))
     width = -(-table_ref.shape[0] // TILE) * TILE
     pad = width - table_ref.shape[0]
     table = jnp.concatenate([table_ref[...], jnp.zeros((pad, table_ref.shape[1]), BF16)], axis=0)
     t_ref[...] = dot_nn(onehot(relation - 1, width), table).astype(BF16)
-    column = compact_column(source - 1, (tiles_ref[1, 0], tiles_ref[1, 1]), count_ref[0, 1])
-    s_ref[...] = onehot(column, 2 * TILE).T
+    rows_ref[0] = as_row(relation - 1)
+    for hop in range(2):
+        column = compact_column(source - 1, (tiles_ref[hop, 0], tiles_ref[hop, 1]), count_ref[0, hop])
+        rows_ref[1 + hop] = as_row(column)
 
 
 def tables_two(capacity, tiles, count, ids, table):
@@ -312,7 +341,7 @@
         out_specs=[VMEM, VMEM],
         out_shape=[
             jax.ShapeDtypeStruct((slots, feat), BF16),
-            jax.ShapeDtypeStruct((2 * TILE, slots), BF16),
+            jax.ShapeDtypeStruct((3, 8, slots), jnp.int32),
         ],
         compiler_params=params(),
         cost_estimate=cost(1e9, 2 << 20),
@@ -320,24 +349,19 @@
     )(tiles, count, ids, table)
 
 
-def tables_one_kernel(capacity, tiles_ref, count_ref, ids_ref, answer_ref, one_a, one_b, zero_a, zero_b,
-                      s_ref, h_ref, r_ref, total_ref):
-    source, relation = slot_columns(ids_ref[...], capacity, (0, 64))
+def tables_one_kernel(capacity, tiles_ref, count_ref, ids_ref, rows_ref, answer_ref, one_a, one_b, zero_a, zero_b,
+                      h_ref, total_ref):
+    source = slot_columns(ids_ref[...], capacity, (0,))[0] - 1
     columns = [
-        compact_column(source - 1, (tiles_ref[hop, 0], tiles_ref[hop, 1]), count_ref[0, hop]) for hop in range(2)
+        compact_column(source, (tiles_ref[hop, 0], tiles_ref[hop, 1]), count_ref[0, hop]) for hop in range(2)
     ]
-    select = onehot(columns[0], 2 * TILE)
-    s_ref[...] = select.T
-    h_ref[...] = dot_nn(select, jnp.concatenate([zero_a[...], zero_b[...]], axis=0)).astype(BF16)
+    h_ref[...] = dot_nn(onehot(columns[0], 2 * TILE), jnp.concatenate([zero_a[...], zero_b[...]], axis=0)).astype(BF16)
     states = dot_nn(onehot(columns[1], 2 * TILE), jnp.concatenate([one_a[...], one_b[...]], axis=0)).astype(BF16)
-    turned = onehot(relation - 1, r_ref.shape[0]).T
-    r_ref[...] = turned
-    total_ref[...] = dot_nn(turned, answer_ref[...] * states)
-
-
-def tables_one(capacity, tiles, count, ids, answer, state_one, state_zero, groups):
-    feat = answer.shape[1]
-    slots = ids.shape[0] * capacity
+    total_ref[...] = dot_nn(onehot_rows(rows_ref[0, 0:1, :], total_ref.shape[0]), answer_ref[...] * states)
+
+
+def tables_one(capacity, tiles, count, ids, rows, answer, state_one, state_zero, groups):
+    slots, feat = answer.shape
     width = -(-groups // TILE) * TILE
 
     def tile(hop, k):
@@ -348,39 +372,41 @@
         grid_spec=pltpu.PrefetchScalarGridSpec(
             num_scalar_prefetch=2,
             grid=(1,),
-            in_specs=[whole(ids.shape), whole(answer.shape), tile(1, 0), tile(1, 1), tile(0, 0), tile(0, 1)],
-            out_specs=[whole((2 * TILE, slots)), whole((slots, feat)), whole((width, slots)), whole((width, feat))],
+            in_specs=[whole(ids.shape), whole(rows.shape), whole(answer.shape), tile(1, 0), tile(1, 1), tile(0, 0),
+                      tile(0, 1)],
+            out_specs=[whole((slots, feat)), whole((width, feat))],
         ),
         out_shape=[
-            jax.ShapeDtypeStruct((2 * TILE, slots), BF16),
             jax.ShapeDtypeStruct((slots, feat), BF16),
-            jax.ShapeDtypeStruct((width, slots), BF16),
             jax.ShapeDtypeStruct((width, feat), F32),
         ],
-        compiler_params=params(24 << 20),
+        compiler_params=params(),
         cost_estimate=cost(2e9, 4 << 20),
         name="tables_one",
-    )(tiles, count, ids, answer, state_one, state_one, state_zero, state_zero)
-
-
-def contribution_kernel(answer_ref, t_ref, s_ref, out_ref):
-    out_ref[...] = dot_nn(s_ref[...], answer_ref[...] * t_ref[...]).astype(BF16)
-
-
-def contribution(answer, table, select):
+    )(tiles, count, ids, rows, answer, state_one, state_one, state_zero, state_zero)
+
+
+def contribution_kernel(answer_ref, t_ref, rows_ref, out_ref):
+    select = onehot_rows(rows_ref[2, 0:1, :], 2 * TILE)
+    out_ref[...] = dot_nn(select, answer_ref[...] * t_ref[...]).astype(BF16)
+
+
+def contribution(answer, table, rows):
     return pl.pallas_call(
         contribution_kernel,
         in_specs=[VMEM] * 3,
         out_specs=VMEM,
-        out_shape=jax.ShapeDtypeStruct((select.shape[0], answer.shape[1]), BF16),
+        out_shape=jax.ShapeDtypeStruct((2 * TILE, answer.shape[1]), BF16),
         compiler_params=params(8 << 20),
         cost_estimate=cost(2e8, 3 << 20),
         name="contribution",
-    )(answer, table, select)
+    )(answer, table, rows)
 
 
 def live_kernel(tiles_ref, count_ref, agg_a, agg_b, state_a, state_b, up_a, up_b, c0, c1, c2, c3,
-                wx, wu, wb, live_ref, rest_ref, picked_ref, next_ref, sums_ref, acc_in, acc_out, acc_bias):
+                w_in_ref, w_bias_ref, w_out_ref, live_ref, rest_ref, picked_ref, next_ref, sums_ref,
+                wx, wu, wb, acc_in, acc_out, acc_bias):
+    build_weights(0, w_in_ref, w_bias_ref, w_out_ref, wx, wu, wb)
     clear(acc_in, acc_out, acc_bias)
     source = (c0[...].astype(F32) + c1[...].astype(F32)) + (c2[...].astype(F32) + c3[...].astype(F32))
     up = jnp.concatenate([up_a[...], up_b[...]], axis=0) + source
@@ -413,7 +439,7 @@
             in_specs=[tile(0), tile(1)] * 3 + [whole(parts[0].shape)] * 4
             + [whole(w.shape) for w in weights] + [whole(live.shape), whole(rest.shape)],
             out_specs=[whole(rest.shape), whole((2 * TILE, feat)), whole((SUM_ROWS, WIDE))],
-            scratch_shapes=scratch(SUM_SHAPES),
+            scratch_shapes=scratch(WEIGHT_SHAPES + SUM_SHAPES),
         ),
         out_shape=[
             jax.ShapeDtypeStruct(rest.shape, BF16),
@@ -429,10 +455,11 @@
 GAP = SUM_ROWS
 
 
-def pack_kernel(answer_ref, t_ref, s_ref, h_ref, r_ref, before_ref, w2_ref, w1a_ref, w1b_ref, part_ref, out_ref):
+def pack_kernel(answer_ref, t_ref, h_ref, rows_ref, before_ref, w2_ref, w1a_ref, w1b_ref, part_ref, out_ref):
     answer = answer_ref[...]
-    part_ref[...] = dot_nn(s_ref[...], answer * t_ref[...]).astype(BF16)
-    total = before_ref[...] + dot_nn(r_ref[...], answer * h_ref[...])
+    part_ref[...] = dot_nn(onehot_rows(rows_ref[1, 0:1, :], 2 * TILE), answer * t_ref[...]).astype(BF16)
+    select = onehot_rows(rows_ref[0, 0:1, :], before_ref.shape[0])
+    total = before_ref[...] + dot_nn(select, answer * h_ref[...])
     used, feat = total.shape
     out_ref[used:, 0:feat] = jnp.zeros((out_ref.shape[0] - used, feat), BF16)
     out_ref[4 * GAP:, feat:feat + TILE] = jnp.zeros((out_ref.shape[0] - 4 * GAP, TILE), BF16)
@@ -444,20 +471,20 @@
     out_ref[0:4 * GAP, feat:feat + TILE] = jnp.concatenate(parts, axis=0).astype(BF16)
 
 
-def pack_sums(answer, table, select, states, select_rel, before, w2, w1a, w1b, rows):
+def pack_sums(answer, table, states, ids, before, w2, w1a, w1b, rows):
     feat = answer.shape[1]
     return pl.pallas_call(
         pack_kernel,
-        in_specs=[VMEM] * 9,
+        in_specs=[VMEM] * 8,
         out_specs=[VMEM, VMEM],
         out_shape=[
-            jax.ShapeDtypeStruct((select.shape[0], feat), BF16),
+            jax.ShapeDtypeStruct((2 * TILE, feat), BF16),
             jax.ShapeDtypeStruct((rows, feat + TILE), BF16),
         ],
         compiler_params=params(),
         cost_estimate=cost(4e8, 4 << 20),
         name="pack_sums",
-    )(answer, table, select, states, select_rel, before, w2, w1a, w1b)
+    )(answer, table, states, ids, before, w2, w1a, w1b)
 
 
 def combine_kernel(feat, scale_relations, scale_weights, in_ref, out_ref):
@@ -572,40 +599,40 @@
     weights = (update_in, update_bias, jnp.swapaxes(update_out, 1, 2))
     request, ids = pl.pallas_call(
         functools.partial(slots_kernel, peers),
-        in_specs=[VMEM] * 4,
+        in_specs=[HBM] * 4,
         out_specs=[VMEM] * 2,
         out_shape=[
             jax.ShapeDtypeStruct((peers, 1, 128), F32),
             jax.ShapeDtypeStruct((peers, 128), F32),
         ],
+        scratch_shapes=[pltpu.VMEM((1, edges), jnp.int32)] * 4 + [pltpu.SemaphoreType.DMA((4,))],
         compiler_params=params(8 << 20),
         cost_estimate=cost(1e8, 1 << 20),
         name="slots",
-    )(row(edge_owner), row(edge_target), row(edge_source), row(edge_relation))
+    )(*(in_hbm(row(values)) for values in (edge_owner, edge_target, edge_source, edge_relation)))
     asked = exchange(request)
 
     upstream_one, picked_two, sums_two = first_pass(
         capacity, aggregate_two, state_one, cotangent, *weights, asked
     )
+    sums_two = in_hbm(sums_two)
     answered_two = exchange(picked_two.reshape(peers, capacity, feat)).reshape(slots, feat)
-    after, rest, sums_rest, live, *built = rest_pass(
+    after, rest, sums_rest, live = rest_pass(
         capacity, frontier_tiles, count, aggregate_one, state_zero, upstream_one, *weights, asked
     )
-    edge_table, select_two = tables_two(capacity, frontier_tiles, count, ids, relation_table)
-    answered_two, rest, edge_table, select_two = lax.optimization_barrier(
-        (answered_two, rest, edge_table, select_two)
+    edge_table, rows = tables_two(capacity, frontier_tiles, count, ids, relation_table)
+    answered_two, rest, edge_table, rows = lax.optimization_barrier((answered_two, rest, edge_table, rows))
+    parts = over_rel(contribution(answered_two, edge_table, rows))
+    states_one, relation_two = tables_one(
+        capacity, frontier_tiles, count, ids, rows, answered_two, state_one, state_zero, groups
     )
-    parts = over_rel(contribution(answered_two, edge_table, select_two))
+    parts[0], rest, states_one, relation_two = lax.optimization_barrier((parts[0], rest, states_one, relation_two))
     picked_one, after_live, sums_live = live_pass(
-        frontier_tiles, count, aggregate_one, state_zero, upstream_one, parts, built, live, rest
+        frontier_tiles, count, aggregate_one, state_zero, upstream_one, parts, weights, live, rest
     )
     answered_one = exchange(picked_one.reshape(peers, capacity, feat)).reshape(slots, feat)
-    select_one, states_one, select_rel, relation_two = tables_one(
-        capacity, frontier_tiles, count, ids, answered_two, state_one, state_zero, groups
-    )
     part, packed = pack_sums(
-        answered_one, edge_table, select_one, states_one, select_rel, relation_two,
-        sums_two, sums_rest, sums_live, sum_rows,
+        answered_one, edge_table, states_one, rows, relation_two, sums_two, sums_rest, sums_live, sum_rows
     )
     parts = over_rel(part)
     scale_weights = 1.0 / math.sqrt(block_rows * peers * QUERIES)

time: 167 us -> 153 us (0.916)
  blocking collectives: 42.8 us -> 72.6 us
  local copies, waits for them, and re-layouts: 26 us -> 6.39 us
  waiting for transfers between devices: 34.7 us -> 15.5 us
  starting transfers between devices: 27.8 us -> 20.7 us
  Pallas kernels: 33.5 us -> 36.2 us
    all_to_all x2 -> x3, blocking collectives: 42.8 us -> 72.6 us  [exchange(): lax.all_to_all(chunks, 'ent', split_axis=0, concat_axis=0, tiled=True)]
    unnamed x96 -> x52, local copies, waits for them, and re-layouts: 26 us -> 6.39 us
    all_to_all x3 -> x2, waiting for transfers between devices: 25.1 us -> 8.44 us  [exchange(): lax.all_to_all(chunks, 'ent', split_axis=0, concat_axis=0, tiled=True)]
    all_to_all x3 -> x2, starting transfers between devices: 18.1 us -> 11 us  [exchange(): lax.all_to_all(chunks, 'ent', split_axis=0, concat_axis=0, tiled=True)]
    pallas_call x3, Pallas kernels: 11.4 us -> 14.4 us  [the longest x1 11.5 us: first_pass(): pl.pallas_call(functools.partial(first_kernel, capacity, blocks), in_spec...]
    ppermute x6, waiting for transfers between devices: 9.58 us -> 7.04 us  [over_rel(): lax.ppermute(part, 'rel', [(i, (i + k) % group_size) for i in range(group...]
  transfers between devices with their start and end apart: 9 -> 8, of which waited for: 7 -> 5; matrix products, arithmetic and copies ran while one was open for 0% -> 0% of each run, Pallas kernels for 10% -> 11%
where the time goes in v3:
time: 153 us; the launch traced here: 152 us
  blocking collectives  72.6 us (47%)
  Pallas kernels  36.2 us (24%)
  starting transfers between devices  20.7 us (14%)
  waiting for transfers between devices  15.5 us (10%)
  local copies, waits for them, and re-layouts  6.39 us (4%)
    all_to_all x3, blocking collectives, exchange(): lax.all_to_all(chunks, 'ent', split_axis=0, concat_axis=0, tiled=True)  72.6 us
    pallas_call x1, Pallas kernels, first_pass(): pl.pallas_call(functools.partial(first_kernel, capacity, blocks), in_spec...  11.5 us
    all_to_all x2, starting transfers between devices, exchange(): lax.all_to_all(chunks, 'ent', split_axis=0, concat_axis=0, tiled=True)  11 us
    pallas_call x1, Pallas kernels, rest_pass(): pl.pallas_call(functools.partial(rest_kernel, capacity), grid=(rows // bl...  10.6 us
    ppermute x6, starting transfers between devices, over_rel(): lax.ppermute(part, 'rel', [(i, (i + k) % group_size) for i in range(group...  9.68 us
    all_to_all x2, waiting for transfers between devices, exchange(): lax.all_to_all(chunks, 'ent', split_axis=0, concat_axis=0, tiled=True)  8.44 us
    ppermute x6, waiting for transfers between devices, over_rel(): lax.ppermute(part, 'rel', [(i, (i + k) % group_size) for i in range(group...  7.04 us
    unnamed x52, local copies, waits for them, and re-layouts  6.39 us
  transfers between devices with their start and end apart: 8, of which 5 were waited for; matrix products, arithmetic and copies ran while one was open for 0% of the time, Pallas kernels for 11%

profile of v3, /device:TPU:1, one launch (start us, length us, event | category | flops | bytes accessed | tf_op | source)
XLA Modules:
  0.0 152.2 jit_solution(2913478634735462904)
XLA Ops:
  0.6 1.2 slots.1
  1.9 22.2 %all_to_all.25.asked_ref = f32[64,1,128]{2,1,0:T(1,128)S(1)} all-to-all(f32[64,1,128]{2,1,0:T(1,128)S(1)} %get-tuple-element.35), channel_id=1, replica_groups=mesh['ent'=64,'rel'=4] {'ent'}, dimensions={0} | all-to-all | bytes 65536 | tf_op jit(solution)/shard_map/all_to_all | solution.py:588
  24.1 11.5 %first.1 = (f32[1024,256]{1,0:T(8,128)S(1)}, bf16[1536,256]{1,0:T(8,128)(2,1)}, f32[104,256]{1,0:T(8,128)S(1)}) custom-call(bf16[1024,256]{1,0:T(8,128)(2,1)} %agg_hbm.1, bf16[1024,256]{1,0:T(8,128)(2,1)} %one_b.1, bf16[1024,256]{1,0:T(8,128)(2,1)} %up_hbm.1, bf16[2,64,256]{2,1,0:T(8,128)(2,1)S(1)} %copy-done.12, f32[2,256]{1,0:T(2,128)S(1)} %copy-done.19, ...), custom_call_target="tpu_custom_call" | custom-call | flops 5400000000 | bytes 4194304 | tf_op jit(solution)/shard_map/first/pallas_call | solution.py:247
  36.3 4.7 %all-to-all-start.1 = ((bf16[64,24,256]{2,1,0:T(8,128)(2,1)}), bf16[64,24,256]{2,1,0:T(8,128)(2,1)S(1)}, u32[]{:S(2)}, u32[]{:S(2)}) async-start(bf16[64,24,256]{2,1,0:T(8,128)(2,1)} %bitcast.7), calls=%async_computation.1 | async-start | bytes 1572864 | tf_op jit(solution)/shard_map/all_to_all | solution.py:588
  42.7 2.3 %tables_two.1 = (bf16[1536,256]{1,0:T(8,128)(2,1)S(1)}, s32[3,8,1536]{2,1,0:T(8,128)S(1)}) custom-call(s32[2,2]{1,0:T(2,128)S(1)} %copy-done.16, s32[1,2]{1,0:T(1,128)S(1)} %bitcast.23, f32[64,128]{1,0:T(8,128)S(1)} %get-tuple-element.40.ids_ref, bf16[328,256]{1,0:T(8,128)(2,1)S(1)} %copy-done.25), custom_call_target="tpu_custom_call" | custom-call | flops 1000000000 | bytes 2097152 | tf_op jit(solution)/shard_map/tables_two/pallas_call | solution.py:338
  45.0 10.6 %rest.1 = (f32[1024,256]{1,0:T(8,128)S(1)}, bf16[1536,256]{1,0:T(8,128)(2,1)S(1)}, f32[104,256]{1,0:T(8,128)S(1)}, bf16[1536,256]{1,0:T(8,128)(2,1)S(1)}) custom-call(s32[2,2]{1,0:T(2,128)S(1)} %copy-done.16, s32[1,2]{1,0:T(1,128)S(1)} %bitcast.24, bf16[1024,256]{1,0:T(8,128)(2,1)S(1)} %copy-done, bf16[1024,256]{1,0:T(8,128)(2,1)S(1)} %copy-done.1, ...), custom_call_target="tpu_custom_call" | custom-call | flops 5400000000 | bytes 4194304 | tf_op jit(solution)/shard_map/rest/pallas_call | solution.py:296
  59.0 5.1 %all-to-all-done.1 = bf16[64,24,256]{2,1,0:T(8,128)(2,1)S(1)} async-done(((bf16[64,24,256]{2,1,0:T(8,128)(2,1)}), bf16[64,24,256]{2,1,0:T(8,128)(2,1)S(1)}, u32[]{:S(2)}, u32[]{:S(2)}) %all-to-all-start.1) | async-done | bytes 786464 | tf_op jit(solution)/shard_map/all_to_all | solution.py:588
  64.5 1.6 %collective-permute-start = (bf16[256,256]{1,0:T(8,128)(2,1)S(1)}, bf16[256,256]{1,0:T(8,128)(2,1)S(1)}, u32[]{:S(2)}, u32[]{:S(2)}) collective-permute-start(bf16[256,256]{1,0:T(8,128)(2,1)S(1)} %contribution.1.c0), channel_id=1, source_target_pairs={{0,1},{1,2},{2,3},{3,0},{4,5},{5,6},{6,7},{7,4},{8,9},{9,10},{10,1... | collective-permute-start | bytes 393224 | tf_op jit(solution)/shard_map/ppermute | solution.py:592
  66.1 2.6 %collective-permute-start.1 = (bf16[256,256]{1,0:T(8,128)(2,1)S(1)}, bf16[256,256]{1,0:T(8,128)(2,1)S(1)}, u32[]{:S(2)}, u32[]{:S(2)}) collective-permute-start(bf16[256,256]{1,0:T(8,128)(2,1)S(1)} %contribution.1.c0), channel_id=1, source_target_pairs={{0,2},{1,3},{2,0},{3,1},{4,6},{5,7},{6,4},{7,5},{8,10},{9,11},{10,... | collective-permute-start | bytes 393224 | tf_op jit(solution)/shard_map/ppermute | solution.py:592
  68.7 1.1 collective-permute-start.2
  69.8 2.5 %tables_one.1 = (bf16[1536,256]{1,0:T(8,128)(2,1)S(1)}, f32[384,256]{1,0:T(8,128)S(1)}) custom-call(s32[2,2]{1,0:T(2,128)S(1)} %copy-done.16, s32[1,2]{1,0:T(1,128)S(1)} %bitcast.25, f32[64,128]{1,0:T(8,128)S(1)} %get-tuple-element.40.ids_ref, s32[3,8,1536]{2,1,0:T(8,128)S(1)} %get-tuple-element.45.rows_ref, bf16[1536,256]{1,0:T(8,128)(2,1)S(1)} %bitcast.15, ...), custom_call_target="tpu_custom_call" | custom-call | flops 2000000000 | bytes 4194304 | tf_op jit(solution)/shard_map/tables_one/pallas_call | solution.py:370
  72.3 2.4 %collective-permute-done.1.c2 = bf16[256,256]{1,0:T(8,128)(2,1)S(1)} collective-permute-done((bf16[256,256]{1,0:T(8,128)(2,1)S(1)}, bf16[256,256]{1,0:T(8,128)(2,1)S(1)}, u32[]{:S(2)}, u32[]{:S(2)}) %collective-permute-start.1) | collective-permute-done | bytes 131104 | tf_op jit(solution)/shard_map/ppermute | solution.py:592
  74.8 2.9 %live.1 = (bf16[1536,256]{1,0:T(8,128)(2,1)S(1)}, f32[256,256]{1,0:T(8,128)S(1)}, f32[104,256]{1,0:T(8,128)S(1)}) custom-call(s32[2,2]{1,0:T(2,128)S(1)} %copy-done.17, s32[1,2]{1,0:T(1,128)S(1)} %bitcast.26, bf16[1024,256]{1,0:T(8,128)(2,1)S(1)} %copy-done, bf16[1024,256]{1,0:T(8,128)(2,1)S(1)} %copy-done, bf16[1024,256]{1,0:T(8,128)(2,1)S(1)} %copy-done.2, ...), custom_call_target="tpu_custom_call" | custom-call | flops 1600000000 | bytes 4194304 | tf_op jit(solution)/shard_map/live/pallas_call | solution.py:434
  77.7 29.7 %all_to_all.26 = bf16[64,24,256]{2,1,0:T(8,128)(2,1)S(1)} all-to-all(bf16[64,24,256]{2,1,0:T(8,128)(2,1)S(1)} %bitcast.18), channel_id=1, replica_groups=mesh['ent'=64,'rel'=4] {'ent'}, dimensions={0} | all-to-all | bytes 1572864 | tf_op jit(solution)/shard_map/all_to_all | solution.py:588
  107.4 1.6 %pack_sums.1 = (bf16[256,256]{1,0:T(8,128)(2,1)S(1)}, bf16[512,384]{1,0:T(8,128)(2,1)S(1)}) custom-call(bf16[1536,256]{1,0:T(8,128)(2,1)S(1)} %bitcast.16, bf16[1536,256]{1,0:T(8,128)(2,1)S(1)} %get-tuple-element.44.t_ref, bf16[1536,256]{1,0:T(8,128)(2,1)S(1)} %get-tuple-element.54.h_ref, s32[3,8,1536]{2,1,0:T(8,128)S(1)} %get-tuple-element.45.rows_ref, ...), custom_call_target="tpu_custom_call" | custom-call | flops 400000000 | bytes 4194304 | tf_op jit(solution)/shard_map/pack_sums/pallas_call | solution.py:476
  109.1 20.7 %all_to_all.27.in_ref = bf16[64,8,384]{2,1,0:T(8,128)(2,1)S(1)} all-to-all(bf16[64,8,384]{2,1,0:T(8,128)(2,1)S(1)} %bitcast.19), channel_id=1, replica_groups=mesh['ent'=64,'rel'=4] {'ent'}, dimensions={0} | all-to-all | bytes 786432 | tf_op jit(solution)/shard_map/all_to_all | solution.py:588
  130.6 6.2 %all-to-all-start.4 = ((bf16[64,8,384]{2,1,0:T(8,128)(2,1)}), bf16[64,8,384]{2,1,0:T(8,128)(2,1)S(1)}, u32[]{:S(2)}, u32[]{:S(2)}) async-start(bf16[64,8,384]{2,1,0:T(8,128)(2,1)} %combine.1), calls=%async_computation.4 | async-start | bytes 786432 | tf_op jit(solution)/shard_map/all_to_all | solution.py:588
  136.9 1.0 collective-permute-start.3
  137.9 2.1 %collective-permute-start.4 = (bf16[256,256]{1,0:T(8,128)(2,1)S(1)}, bf16[256,256]{1,0:T(8,128)(2,1)S(1)}, u32[]{:S(2)}, u32[]{:S(2)}) collective-permute-start(bf16[256,256]{1,0:T(8,128)(2,1)S(1)} %get-tuple-element.59.c0), channel_id=1, source_target_pairs={{0,2},{1,3},{2,0},{3,1},{4,6},{5,7},{6,4},{7,5},{8,10},{9,11},{10,... | collective-permute-start | bytes 393224 | tf_op jit(solution)/shard_map/ppermute | solution.py:592
  140.0 1.3 collective-permute-start.5
  141.3 1.5 collective-permute-done.3.c1
  142.8 3.2 %collective-permute-done.4.c2 = bf16[256,256]{1,0:T(8,128)(2,1)S(1)} collective-permute-done((bf16[256,256]{1,0:T(8,128)(2,1)S(1)}, bf16[256,256]{1,0:T(8,128)(2,1)S(1)}, u32[]{:S(2)}, u32[]{:S(2)}) %collective-permute-start.4) | collective-permute-done | bytes 131104 | tf_op jit(solution)/shard_map/ppermute | solution.py:592
  146.6 1.4 final.1
  148.1 3.4 %all-to-all-done.4 = bf16[64,8,384]{2,1,0:T(8,128)(2,1)S(1)} async-done(((bf16[64,8,384]{2,1,0:T(8,128)(2,1)}), bf16[64,8,384]{2,1,0:T(8,128)(2,1)S(1)}, u32[]{:S(2)}, u32[]{:S(2)}) %all-to-all-start.4) | async-done | bytes 393248 | tf_op jit(solution)/shard_map/all_to_all | solution.py:588
  (58 shorter events, 8.4 us)
Async XLA Ops:
  0.6 23.5 %copy-start.14 = (bf16[2,256,32]{1,2,0:T(8,128)(2,1)S(1)}, bf16[2,256,32]{1,2,0:T(8,128)(2,1)}, u32[]{:S(2)}) copy-start(bf16[2,256,32]{1,2,0:T(8,128)(2,1)} %param.23) | copy-start | bytes 98308
  1.9 22.2 %copy-start.12 = (bf16[2,64,256]{2,1,0:T(8,128)(2,1)S(1)}, bf16[2,64,256]{2,1,0:T(8,128)(2,1)}, u32[]{:S(2)}) copy-start(bf16[2,64,256]{2,1,0:T(8,128)(2,1)} %w_in_ref.5) | copy-start | bytes 196612
  1.9 22.2 %copy-start.19 = (f32[2,256]{1,0:T(2,128)S(1)}, f32[2,256]{1,0:T(2,128)}, u32[]{:S(2)}) copy-start(f32[2,256]{1,0:T(2,128)} %w_bias_ref.5) | copy-start | bytes 6148
  36.3 27.8 %all-to-all-start.1 = ((bf16[64,24,256]{2,1,0:T(8,128)(2,1)}), bf16[64,24,256]{2,1,0:T(8,128)(2,1)S(1)}, u32[]{:S(2)}, u32[]{:S(2)}) async-start(bf16[64,24,256]{2,1,0:T(8,128)(2,1)} %bitcast.7), calls=%async_computation.1 | async-start | bytes 1572864 | tf_op jit(solution)/shard_map/all_to_all | solution.py:588
  42.7 2.3 %copy-start = (bf16[1024,256]{1,0:T(8,128)(2,1)S(1)}, bf16[1024,256]{1,0:T(8,128)(2,1)}, u32[]{:S(2)}) copy-start(bf16[1024,256]{1,0:T(8,128)(2,1)} %agg_b.1) | copy-start | bytes 1572868
  42.7 2.3 %copy-start.1 = (bf16[1024,256]{1,0:T(8,128)(2,1)S(1)}, bf16[1024,256]{1,0:T(8,128)(2,1)}, u32[]{:S(2)}) copy-start(bf16[1024,256]{1,0:T(8,128)(2,1)} %state_b.1) | copy-start | bytes 1572868
  64.1 5.7 %copy-start.2 = (bf16[1024,256]{1,0:T(8,128)(2,1)S(1)}, bf16[1024,256]{1,0:T(8,128)(2,1)}, u32[]{:S(2)}) copy-start(bf16[1024,256]{1,0:T(8,128)(2,1)} %state_b.1) | copy-start | bytes 1572868
  64.1 5.7 %copy-start.24 = (bf16[1024,256]{1,0:T(8,128)(2,1)S(1)}, bf16[1024,256]{1,0:T(8,128)(2,1)}, u32[]{:S(2)}) copy-start(bf16[1024,256]{1,0:T(8,128)(2,1)} %one_b.1) | copy-start | bytes 1572868
  64.5 10.2 %copy-start.6 = (bf16[1536,256]{1,0:T(8,128)(2,1)S(1)}, bf16[1536,256]{1,0:T(8,128)(2,1)}, u32[]{:S(2)}) copy-start(bf16[1536,256]{1,0:T(8,128)(2,1)} %copy-done.5) | copy-start | bytes 2359300
  64.5 10.2 %copy-start.8 = (bf16[1536,256]{1,0:T(8,128)(2,1)S(1)}, bf16[1536,256]{1,0:T(8,128)(2,1)}, u32[]{:S(2)}) copy-start(bf16[1536,256]{1,0:T(8,128)(2,1)} %copy-done.7) | copy-start | bytes 2359300
  64.5 10.2 %copy-start.13 = (bf16[2,64,256]{2,1,0:T(8,128)(2,1)S(1)}, bf16[2,64,256]{2,1,0:T(8,128)(2,1)}, u32[]{:S(2)}) copy-start(bf16[2,64,256]{2,1,0:T(8,128)(2,1)} %w_in_ref.5) | copy-start | bytes 196612
  64.5 10.2 %copy-start.15 = (bf16[2,256,32]{1,2,0:T(8,128)(2,1)S(1)}, bf16[2,256,32]{1,2,0:T(8,128)(2,1)}, u32[]{:S(2)}) copy-start(bf16[2,256,32]{1,2,0:T(8,128)(2,1)} %param.23) | copy-start | bytes 98308
  64.5 7.8 %collective-permute-start = (bf16[256,256]{1,0:T(8,128)(2,1)S(1)}, bf16[256,256]{1,0:T(8,128)(2,1)S(1)}, u32[]{:S(2)}, u32[]{:S(2)}) collective-permute-start(bf16[256,256]{1,0:T(8,128)(2,1)S(1)} %contribution.1.c0), channel_id=1, source_target_pairs={{0,1},{1,2},{2,3},{3,0},{4,5},{5,6},{6,7},{7,4},{8,9},{9,10},{10,1... | collective-permute-start | bytes 393224 | tf_op jit(solution)/shard_map/ppermute | solution.py:592
  66.1 8.6 %collective-permute-start.1 = (bf16[256,256]{1,0:T(8,128)(2,1)S(1)}, bf16[256,256]{1,0:T(8,128)(2,1)S(1)}, u32[]{:S(2)}, u32[]{:S(2)}) collective-permute-start(bf16[256,256]{1,0:T(8,128)(2,1)S(1)} %contribution.1.c0), channel_id=1, source_target_pairs={{0,2},{1,3},{2,0},{3,1},{4,6},{5,7},{6,4},{7,5},{8,10},{9,11},{10,... | collective-permute-start | bytes 393224 | tf_op jit(solution)/shard_map/ppermute | solution.py:592
  68.7 6.0 %collective-permute-start.2 = (bf16[256,256]{1,0:T(8,128)(2,1)S(1)}, bf16[256,256]{1,0:T(8,128)(2,1)S(1)}, u32[]{:S(2)}, u32[]{:S(2)}) collective-permute-start(bf16[256,256]{1,0:T(8,128)(2,1)S(1)} %contribution.1.c0), channel_id=1, source_target_pairs={{0,3},{1,0},{2,1},{3,2},{4,7},{5,4},{6,5},{7,6},{8,11},{9,8},{10,9... | collective-permute-start | bytes 393224 | tf_op jit(solution)/shard_map/ppermute | solution.py:592
  72.3 2.5 %copy-start.20 = (f32[2,256]{1,0:T(2,128)S(1)}, f32[2,256]{1,0:T(2,128)}, u32[]{:S(2)}) copy-start(f32[2,256]{1,0:T(2,128)} %w_bias_ref.5) | copy-start | bytes 6148
  72.3 2.5 %copy-start.17 = (s32[2,2]{1,0:T(2,128)S(1)}, s32[2,2]{1,0:T(2,128)}, u32[]{:S(2)}) copy-start(s32[2,2]{1,0:T(2,128)} %tiles_ref.9) | copy-start | bytes 52
  72.3 2.5 %copy-start.22 = (s32[2,1]{0,1:T(1,128)S(1)}, s32[2,1]{0,1:T(1,128)}, u32[]{:S(2)}) copy-start(s32[2,1]{0,1:T(1,128)} %param.25) | copy-start | bytes 28
  77.7 29.7 %copy-start.11 = (f32[104,256]{1,0:T(8,128)S(1)}, f32[104,256]{1,0:T(8,128)}, u32[]{:S(2)}) copy-start(f32[104,256]{1,0:T(8,128)} %copy-done.10) | copy-start | bytes 319492
  109.1 36.9 %copy-start.4 = (f32[1024,256]{1,0:T(8,128)S(1)}, f32[1024,256]{1,0:T(8,128)}, u32[]{:S(2)}) copy-start(f32[1024,256]{1,0:T(8,128)} %copy-done.3) | copy-start | bytes 3145732
  130.6 20.8 %all-to-all-start.4 = ((bf16[64,8,384]{2,1,0:T(8,128)(2,1)}), bf16[64,8,384]{2,1,0:T(8,128)(2,1)S(1)}, u32[]{:S(2)}, u32[]{:S(2)}) async-start(bf16[64,8,384]{2,1,0:T(8,128)(2,1)} %combine.1), calls=%async_computation.4 | async-start | bytes 786432 | tf_op jit(solution)/shard_map/all_to_all | solution.py:588
  136.9 5.9 %collective-permute-start.3 = (bf16[256,256]{1,0:T(8,128)(2,1)S(1)}, bf16[256,256]{1,0:T(8,128)(2,1)S(1)}, u32[]{:S(2)}, u32[]{:S(2)}) collective-permute-start(bf16[256,256]{1,0:T(8,128)(2,1)S(1)} %get-tuple-element.59.c0), channel_id=1, source_target_pairs={{0,1},{1,2},{2,3},{3,0},{4,5},{5,6},{6,7},{7,4},{8,9},{9,10},{10,1... | collective-permute-start | bytes 393224 | tf_op jit(solution)/shard_map/ppermute | solution.py:592
  137.9 8.1 %collective-permute-start.4 = (bf16[256,256]{1,0:T(8,128)(2,1)S(1)}, bf16[256,256]{1,0:T(8,128)(2,1)S(1)}, u32[]{:S(2)}, u32[]{:S(2)}) collective-permute-start(bf16[256,256]{1,0:T(8,128)(2,1)S(1)} %get-tuple-element.59.c0), channel_id=1, source_target_pairs={{0,2},{1,3},{2,0},{3,1},{4,6},{5,7},{6,4},{7,5},{8,10},{9,11},{10,... | collective-permute-start | bytes 393224 | tf_op jit(solution)/shard_map/ppermute | solution.py:592
  140.0 5.9 %collective-permute-start.5 = (bf16[256,256]{1,0:T(8,128)(2,1)S(1)}, bf16[256,256]{1,0:T(8,128)(2,1)S(1)}, u32[]{:S(2)}, u32[]{:S(2)}) collective-permute-start(bf16[256,256]{1,0:T(8,128)(2,1)S(1)} %get-tuple-element.59.c0), channel_id=1, source_target_pairs={{0,3},{1,0},{2,1},{3,2},{4,7},{5,4},{6,5},{7,6},{8,11},{9,8},{10,9... | collective-permute-start | bytes 393224 | tf_op jit(solution)/shard_map/ppermute | solution.py:592
  (10 other events, 7.7 us)

commit v4 on v3

--- a/solution.py
+++ b/solution.py
@@ -125,49 +125,43 @@
     for q in range(HALF_Q):
         rows, cols = slice(q * DIM, (q + 1) * DIM), slice(q * WIDE, (q + 1) * WIDE)
         low = slice(TILE + q * DIM, TILE + (q + 1) * DIM)
-        wx_ref[rows, cols] = w_in_ref[layer, 0:DIM, :]
-        wx_ref[low, cols] = w_in_ref[layer, DIM:2 * DIM, :]
+        wx_ref[rows, cols] = 0.5 * w_in_ref[layer, 0:DIM, :]
+        wx_ref[low, cols] = 0.5 * w_in_ref[layer, DIM:2 * DIM, :]
         wu_ref[rows, cols] = w_out_ref[layer]
-        wb_ref[:, cols] = w_bias_ref[layer:layer + 1, :]
-
-
-def mlp_half(s, agg, state, up_low, wx, wu, bias, acc_in, acc_out, acc_bias):
+        wb_ref[:, cols] = 0.5 * w_bias_ref[layer:layer + 1, :]
+
+
+def mlp_half(s, agg, state, up_low, wx, wu, bias, acc_in, acc_out):
     lanes = slice(s * TILE, (s + 1) * TILE)
     x = jnp.concatenate([agg[:, lanes], state[:, lanes]], axis=1)
     up = up_low[:, lanes]
-    pre = dot_nn(x, wx[...]) + bias[...]
-    gate = 0.5 * jnp.tanh(0.5 * pre) + 0.5
-    act = pre * gate
-    slope = gate + act * (1.0 - gate)
-    grad_pre = dot_nn(up, wu[...]) * slope
-    low = grad_pre.astype(BF16)
-    acc_in[...] += dot_tn(x, low)
-    acc_out[...] += dot_tn(up, act.astype(BF16))
-    acc_bias[...] += jnp.sum(grad_pre, axis=0, keepdims=True)
-    return dot_nt(low, wx[...])
-
-
-def store_sums(acc_in, acc_out, acc_bias, sums_ref):
-    first = jnp.zeros((DIM, WIDE), F32)
-    second = jnp.zeros((DIM, WIDE), F32)
-    third = jnp.zeros((DIM, WIDE), F32)
-    fourth = jnp.zeros((1, WIDE), F32)
+    x_turned, up_turned = x.T, up.T
+    half = dot_nn(x, wx[...]) + bias[...]
+    bend = jnp.tanh(half)
+    above = 1.0 + bend
+    act_low = (half * above).astype(BF16)
+    slope = above * (1.0 + half * (1.0 - bend))
+    low = (dot_nn(up, wu[...]) * slope).astype(BF16)
+    ones = jnp.ones((16, x.shape[0]), BF16)
     for q in range(HALF_Q):
         cols = slice(q * WIDE, (q + 1) * WIDE)
-        first += acc_in[q * DIM:(q + 1) * DIM, cols]
-        second += acc_in[TILE + q * DIM:TILE + (q + 1) * DIM, cols]
-        third += acc_out[q * DIM:(q + 1) * DIM, cols]
-        fourth += acc_bias[:, cols]
-    sums_ref[0:DIM, :] = first
-    sums_ref[DIM:2 * DIM, :] = second
-    sums_ref[2 * DIM:3 * DIM, :] = third
-    sums_ref[3 * DIM:3 * DIM + 8, :] = jnp.concatenate([fourth, jnp.zeros((7, WIDE), F32)], axis=0)
-
-
-def clear(acc_in, acc_out, acc_bias):
+        rows = slice(q * DIM, (q + 1) * DIM)
+        low_rows = slice(TILE + q * DIM, TILE + (q + 1) * DIM)
+        own = jnp.concatenate([x_turned[rows], x_turned[low_rows], ones], axis=0)
+        acc_in[...] += dot_nn(own, low[:, cols])
+        acc_out[...] += dot_nn(up_turned[rows], act_low[:, cols])
+    return dot_nt(low, wx[...])
+
+
+def store_sums(acc_in, acc_out, sums_ref):
+    sums_ref[0:2 * DIM, :] = 0.5 * acc_in[0:2 * DIM, :]
+    sums_ref[2 * DIM:3 * DIM, :] = acc_out[...]
+    sums_ref[3 * DIM:3 * DIM + 8, :] = 0.5 * acc_in[2 * DIM:2 * DIM + 8, :]
+
+
+def clear(acc_in, acc_out):
     acc_in[...] = jnp.zeros_like(acc_in)
     acc_out[...] = jnp.zeros_like(acc_out)
-    acc_bias[...] = jnp.zeros_like(acc_bias)
 
 
 WEIGHT_SHAPES = [
@@ -175,11 +169,7 @@
     ((TILE, HALF_Q * WIDE), BF16),
     ((1, HALF_Q * WIDE), F32),
 ]
-SUM_SHAPES = [
-    ((2 * TILE, HALF_Q * WIDE), F32),
-    ((TILE, HALF_Q * WIDE), F32),
-    ((1, HALF_Q * WIDE), F32),
-]
+SUM_SHAPES = [((2 * DIM + 16, WIDE), F32), ((DIM, WIDE), F32)]
 SUM_ROWS = 3 * DIM + 8
 
 
@@ -199,19 +189,19 @@
         picked_ref[part, :] = dot_nn(onehot(asked[part], rows), grad_agg[...]).astype(BF16)
 
 
-def dense_step(step, agg_ref, state_ref, up, up_low, wx, wu, wb, acc_in, acc_out, acc_bias, grad_agg, next_ref):
+def dense_step(step, agg_ref, state_ref, up, up_low, wx, wu, wb, acc_in, acc_out, grad_agg, next_ref):
     rows = agg_ref.shape[0]
     aggs, states = [], []
     for s in range(2):
-        grad_x = mlp_half(s, agg_ref[...], state_ref[...], up_low, wx, wu, wb, acc_in, acc_out, acc_bias)
+        grad_x = mlp_half(s, agg_ref[...], state_ref[...], up_low, wx, wu, wb, acc_in, acc_out)
         aggs.append(grad_x[:, :TILE])
         states.append(grad_x[:, TILE:])
     grad_agg[pl.ds(pl.multiple_of(step * rows, rows), rows), :] = jnp.concatenate(aggs, axis=1).astype(BF16)
     next_ref[...] = up + jnp.concatenate(states, axis=1)
 
 
-def first_kernel(capacity, blocks, agg_hbm, state_hbm, up_hbm, w_in_ref, w_bias_ref, w_out_ref, asked_ref,
-                 next_ref, picked_ref, sums_ref, wx, wu, wb, acc_in, acc_out, acc_bias, grad_agg,
+def first_kernel(blocks, agg_hbm, state_hbm, up_hbm, w_in_ref, w_bias_ref, w_out_ref,
+                 next_ref, grad_agg, sums_hbm, wx, wu, wb, acc_in, acc_out, sums_ref,
                  agg_buf, state_buf, up_buf, sems):
     rows = agg_hbm.shape[0] // blocks
 
@@ -224,7 +214,7 @@
         for copy in copies(step):
             copy.start()
     build_weights(1, w_in_ref, w_bias_ref, w_out_ref, wx, wu, wb)
-    clear(acc_in, acc_out, acc_bias)
+    clear(acc_in, acc_out)
 
     @pl.loop(0, blocks)
     def _(step):
@@ -233,38 +223,57 @@
         part = pl.ds(pl.multiple_of(step * rows, rows), rows)
         up_low = up_buf[part, :]
         dense_step(step, agg_buf.at[part], state_buf.at[part], up_low.astype(F32), up_low, wx, wu, wb,
-                   acc_in, acc_out, acc_bias, grad_agg, next_ref.at[part])
-
-    store_sums(acc_in, acc_out, acc_bias, sums_ref)
+                   acc_in, acc_out, grad_agg, next_ref.at[part])
+
+    store_sums(acc_in, acc_out, sums_ref)
+    copy = pltpu.make_async_copy(sums_ref, sums_hbm, sems.at[0, 0])
+    copy.start()
+    copy.wait()
+
+
+def first_pass(agg, state, up, w_in, w_bias, w_out):
+    rows, feat = agg.shape
+    blocks = rows // 256
+    return pl.pallas_call(
+        functools.partial(first_kernel, blocks),
+        in_specs=[HBM, HBM, HBM, VMEM, VMEM, VMEM],
+        out_specs=[VMEM, VMEM, HBM],
+        out_shape=[
+            jax.ShapeDtypeStruct((rows, feat), F32),
+            jax.ShapeDtypeStruct((rows, feat), BF16),
+            pltpu.HBM((SUM_ROWS, WIDE), F32),
+        ],
+        scratch_shapes=scratch(WEIGHT_SHAPES + SUM_SHAPES)
+        + [pltpu.VMEM((SUM_ROWS, WIDE), F32)]
+        + [pltpu.VMEM((rows, feat), BF16)] * 3
+        + [pltpu.SemaphoreType.DMA((blocks, 3))],
+        compiler_params=params(),
+        cost_estimate=cost(5.4e9, 4 << 20, 2 << 20),
+        name="first",
+    )(in_hbm(agg), in_hbm(state), in_hbm(up), w_in, w_bias, w_out)
+
+
+def pick_kernel(capacity, asked_ref, grad_agg, picked_ref):
     asked = slot_columns(asked_ref[:, 0, :], capacity, (0,))[0]
     pick_rows(asked, grad_agg, picked_ref)
 
 
-def first_pass(capacity, agg, state, up, w_in, w_bias, w_out, asked):
-    rows, feat = agg.shape
-    slots = asked.shape[0] * capacity
-    blocks = rows // 256
-    return pl.pallas_call(
-        functools.partial(first_kernel, capacity, blocks),
-        in_specs=[HBM, HBM, HBM, VMEM, VMEM, VMEM, VMEM],
-        out_specs=[VMEM] * 3,
-        out_shape=[
-            jax.ShapeDtypeStruct((rows, feat), F32),
-            jax.ShapeDtypeStruct((slots, feat), BF16),
-            jax.ShapeDtypeStruct((SUM_ROWS, WIDE), F32),
-        ],
-        scratch_shapes=scratch(WEIGHT_SHAPES + SUM_SHAPES)
-        + [pltpu.VMEM((rows, feat), BF16)] * 4
-        + [pltpu.SemaphoreType.DMA((blocks, 3))],
-        compiler_params=params(),
-        cost_estimate=cost(5.4e9, 4 << 20, 2 << 20),
-        name="first",
-    )(in_hbm(agg), in_hbm(state), in_hbm(up), w_in, w_bias, w_out, asked)
+def pick(capacity, asked, grad_agg):
+    slots, feat = asked.shape[0] * capacity, grad_agg.shape[1]
+    return pl.pallas_call(
+        functools.partial(pick_kernel, capacity),
+        in_specs=[VMEM, VMEM],
+        out_specs=VMEM,
+        out_shape=jax.ShapeDtypeStruct((slots, feat), BF16),
+        compiler_params=params(12 << 20),
+        cost_estimate=cost(8e8, 1 << 20),
+        name="pick",
+    )(asked, grad_agg)
 
 
 def rest_kernel(capacity, tiles_ref, count_ref, agg_ref, state_ref, up_ref, w_in_ref, w_bias_ref, w_out_ref,
                 asked_ref, next_ref, picked_ref, sums_ref, live_ref, wx, wu, wb,
-                acc_in, acc_out, acc_bias, grad_agg):
+                acc_in, acc_out, grad_agg):
     step = pl.program_id(0)
     rows = agg_ref.shape[0]
     count = count_ref[0, 1]
@@ -272,17 +281,17 @@
     @pl.when(step == 0)
     def _():
         build_weights(0, w_in_ref, w_bias_ref, w_out_ref, wx, wu, wb)
-        clear(acc_in, acc_out, acc_bias)
+        clear(acc_in, acc_out)
 
     up = up_ref[...]
     tile = lax.shift_right_logical(iota((rows, 1), 0) + step * rows, 7)
     dead = (tile == tiles_ref[1, 0]) | ((tile == tiles_ref[1, 1]) & (count > 1))
     up_low = jnp.where(dead, 0.0, up).astype(BF16)
-    dense_step(step, agg_ref, state_ref, up, up_low, wx, wu, wb, acc_in, acc_out, acc_bias, grad_agg, next_ref)
+    dense_step(step, agg_ref, state_ref, up, up_low, wx, wu, wb, acc_in, acc_out, grad_agg, next_ref)
 
     @pl.when(step == pl.num_programs(0) - 1)
     def _():
-        store_sums(acc_in, acc_out, acc_bias, sums_ref)
+        store_sums(acc_in, acc_out, sums_ref)
         asked = slot_columns(asked_ref[:, 0, :], capacity, (0,))[0]
         live_ref[...] = onehot(compact_column(asked, (tiles_ref[1, 0], tiles_ref[1, 1]), count), 2 * TILE)
         pick_rows(asked, grad_agg, picked_ref)
@@ -300,10 +309,10 @@
                   whole(w_out.shape), whole(asked.shape)],
         out_specs=[row_spec, whole((slots, feat)), whole((SUM_ROWS, WIDE)), whole((slots, 2 * TILE))],
         out_shape=[
-            jax.ShapeDtypeStruct((rows, feat), F32),
-            jax.ShapeDtypeStruct((slots, feat), BF16),
-            jax.ShapeDtypeStruct((SUM_ROWS, WIDE), F32),
-            jax.ShapeDtypeStruct((slots, 2 * TILE), BF16),
+            pltpu.HBM((rows, feat), F32),
+            pltpu.HBM((slots, feat), BF16),
+            pltpu.HBM((SUM_ROWS, WIDE), F32),
+            pltpu.HBM((slots, 2 * TILE), BF16),
         ],
         scratch_shapes=scratch(WEIGHT_SHAPES + SUM_SHAPES) + [pltpu.VMEM((rows, feat), BF16)],
         compiler_params=params(),
@@ -405,9 +414,9 @@
 
 def live_kernel(tiles_ref, count_ref, agg_a, agg_b, state_a, state_b, up_a, up_b, c0, c1, c2, c3,
                 w_in_ref, w_bias_ref, w_out_ref, live_ref, rest_ref, picked_ref, next_ref, sums_ref,
-                wx, wu, wb, acc_in, acc_out, acc_bias):
+                wx, wu, wb, acc_in, acc_out):
     build_weights(0, w_in_ref, w_bias_ref, w_out_ref, wx, wu, wb)
-    clear(acc_in, acc_out, acc_bias)
+    clear(acc_in, acc_out)
     source = (c0[...].astype(F32) + c1[...].astype(F32)) + (c2[...].astype(F32) + c3[...].astype(F32))
     up = jnp.concatenate([up_a[...], up_b[...]], axis=0) + source
     keep = (iota((2 * TILE, 1), 0) < TILE) | (count_ref[0, 1] > 1)
@@ -416,12 +425,12 @@
     state = jnp.concatenate([state_a[...], state_b[...]], axis=0)
     aggs, states = [], []
     for s in range(2):
-        grad_x = mlp_half(s, agg, state, up_low, wx, wu, wb, acc_in, acc_out, acc_bias)
+        grad_x = mlp_half(s, agg, state, up_low, wx, wu, wb, acc_in, acc_out)
         aggs.append(grad_x[:, :TILE])
         states.append(grad_x[:, TILE:])
     grad_agg = jnp.concatenate(aggs, axis=1).astype(BF16)
     next_ref[...] = up + jnp.concatenate(states, axis=1)
-    store_sums(acc_in, acc_out, acc_bias, sums_ref)
+    store_sums(acc_in, acc_out, sums_ref)
     picked_ref[...] = (dot_nn(live_ref[...], grad_agg) + rest_ref[...].astype(F32)).astype(BF16)
 
 
@@ -612,10 +621,8 @@
     )(*(in_hbm(row(values)) for values in (edge_owner, edge_target, edge_source, edge_relation)))
     asked = exchange(request)
 
-    upstream_one, picked_two, sums_two = first_pass(
-        capacity, aggregate_two, state_one, cotangent, *weights, asked
-    )
-    sums_two = in_hbm(sums_two)
+    upstream_one, grad_agg, sums_two = first_pass(aggregate_two, state_one, cotangent, *weights)
+    picked_two = pick(capacity, asked, grad_agg)
     answered_two = exchange(picked_two.reshape(peers, capacity, feat)).reshape(slots, feat)
     after, rest, sums_rest, live = rest_pass(
         capacity, frontier_tiles, count, aggregate_one, state_zero, upstream_one, *weights, asked

time: 153 us -> 147 us (0.961)
  blocking collectives: 72.6 us -> 50.4 us
  starting transfers between devices: 20.7 us -> 38.2 us
  waiting for transfers between devices: 15.5 us -> 19.9 us
  local copies, waits for them, and re-layouts: 6.39 us -> 2.35 us
  Pallas kernels: 36.2 us -> 34.6 us
    all_to_all x3 -> x2, blocking collectives: 72.6 us -> 50.4 us  [exchange(): lax.all_to_all(chunks, 'ent', split_axis=0, concat_axis=0, tiled=True)]
    all_to_all x2 -> x3, starting transfers between devices: 11 us -> 28.7 us  [exchange(): lax.all_to_all(chunks, 'ent', split_axis=0, concat_axis=0, tiled=True)]
    all_to_all x2 -> x3, waiting for transfers between devices: 8.44 us -> 12.7 us  [exchange(): lax.all_to_all(chunks, 'ent', split_axis=0, concat_axis=0, tiled=True)]
    unnamed x52 -> x44, local copies, waits for them, and re-layouts: 6.39 us -> 2.35 us
    pallas_call x1 -> x2, Pallas kernels: 11.5 us -> 10.6 us  [the longest x1 8.26 us: first_pass(): pl.pallas_call(functools.partial(first_kernel, blocks), in_specs=[HBM, HB...]
  transfers between devices with their start and end apart: 8 -> 9, of which waited for: 5 -> 6; matrix products, arithmetic and copies ran while one was open for 0% -> 0% of each run, Pallas kernels for 11% -> 17%
where the time goes in v4:
time: 147 us; the launch traced here: 146 us
  blocking collectives  50.4 us (34%)
  starting transfers between devices  38.2 us (26%)
  Pallas kernels  34.6 us (24%)
  waiting for transfers between devices  19.9 us (14%)
  local copies, waits for them, and re-layouts  2.35 us (2%)
    all_to_all x2, blocking collectives, exchange(): lax.all_to_all(chunks, 'ent', split_axis=0, concat_axis=0, tiled=True)  50.4 us
    all_to_all x3, starting transfers between devices, exchange(): lax.all_to_all(chunks, 'ent', split_axis=0, concat_axis=0, tiled=True)  28.7 us
    all_to_all x3, waiting for transfers between devices, exchange(): lax.all_to_all(chunks, 'ent', split_axis=0, concat_axis=0, tiled=True)  12.7 us
    pallas_call x1, Pallas kernels, rest_pass(): pl.pallas_call(functools.partial(rest_kernel, capacity), grid=(rows // bl...  10.4 us
    ppermute x6, starting transfers between devices, over_rel(): lax.ppermute(part, 'rel', [(i, (i + k) % group_size) for i in range(group...  9.5 us
    pallas_call x1, Pallas kernels, first_pass(): pl.pallas_call(functools.partial(first_kernel, blocks), in_specs=[HBM, HB...  8.26 us
    ppermute x6, waiting for transfers between devices, over_rel(): lax.ppermute(part, 'rel', [(i, (i + k) % group_size) for i in range(group...  7.21 us
  transfers between devices with their start and end apart: 9, of which 6 were waited for; matrix products, arithmetic and copies ran while one was open for 0% of the time, Pallas kernels for 17%

profile of v4, /device:TPU:1, one launch (start us, length us, event | category | flops | bytes accessed | tf_op | source)
XLA Modules:
  0.0 146.4 jit_solution(16728978125838518854)
XLA Ops:
  0.6 1.8 %slots.1 = (f32[64,1,128]{2,1,0:T(1,128)}, f32[64,128]{1,0:T(8,128)S(1)}) custom-call(s32[1,1024]{1,0:T(1,128)} %bitcast.29, s32[1,1024]{1,0:T(1,128)} %bitcast.30, s32[1,1024]{1,0:T(1,128)} %bitcast.31, s32[1,1024]{1,0:T(1,128)} %bitcast.32), custom_call_target="tpu_custom_call" | custom-call | flops 100000000 | bytes 1048576 | tf_op jit(solution)/shard_map/slots/pallas_call | solution.py:609
  2.5 13.1 %all-to-all-start = ((f32[64,1,128]{2,1,0:T(1,128)}), f32[64,1,128]{2,1,0:T(1,128)S(1)}, u32[]{:S(2)}, u32[]{:S(2)}) async-start(f32[64,1,128]{2,1,0:T(1,128)} %get-tuple-element.36), calls=%async_computation | async-start | bytes 65536 | tf_op jit(solution)/shard_map/all_to_all | solution.py:597
  15.6 8.3 %first.1 = (f32[1024,256]{1,0:T(8,128)S(1)}, bf16[1024,256]{1,0:T(8,128)(2,1)S(1)}, f32[104,256]{1,0:T(8,128)}) custom-call(bf16[1024,256]{1,0:T(8,128)(2,1)} %agg_hbm.1, bf16[1024,256]{1,0:T(8,128)(2,1)} %one_b.1, bf16[1024,256]{1,0:T(8,128)(2,1)} %up_hbm.1, bf16[2,64,256]{2,1,0:T(8,128)(2,1)S(1)} %copy-done.8, f32[2,256]{1,0:T(2,128)S(1)} %copy-done.15, ...), custom_call_target="tpu_custom_call" | custom-call | flops 5400000000 | bytes 4194304 | tf_op jit(solution)/shard_map/first/pallas_call | solution.py:237
  24.8 2.4 %pick.1 = bf16[1536,256]{1,0:T(8,128)(2,1)} custom-call(f32[64,1,128]{2,1,0:T(1,128)S(1)} %all-to-all-done.asked_ref, bf16[1024,256]{1,0:T(8,128)(2,1)S(1)} %get-tuple-element.38.grad_agg), custom_call_target="tpu_custom_call" | custom-call | flops 800000000 | bytes 1048576 | tf_op jit(solution)/shard_map/pick/pallas_call | solution.py:263
  27.2 9.4 %all-to-all-start.1 = ((bf16[64,24,256]{2,1,0:T(8,128)(2,1)}), bf16[64,24,256]{2,1,0:T(8,128)(2,1)S(1)}, u32[]{:S(2)}, u32[]{:S(2)}) async-start(bf16[64,24,256]{2,1,0:T(8,128)(2,1)} %bitcast.7), calls=%async_computation.1 | async-start | bytes 1572864 | tf_op jit(solution)/shard_map/all_to_all | solution.py:597
  38.2 2.3 %tables_two.1 = (bf16[1536,256]{1,0:T(8,128)(2,1)S(1)}, s32[3,8,1536]{2,1,0:T(8,128)S(1)}) custom-call(s32[2,2]{1,0:T(2,128)S(1)} %copy-done.12, s32[1,2]{1,0:T(1,128)S(1)} %bitcast.23, f32[64,128]{1,0:T(8,128)S(1)} %get-tuple-element.40.ids_ref, bf16[328,256]{1,0:T(8,128)(2,1)S(1)} %copy-done.21), custom_call_target="tpu_custom_call" | custom-call | flops 1000000000 | bytes 2097152 | tf_op jit(solution)/shard_map/tables_two/pallas_call | solution.py:347
  40.5 10.4 %rest.1 = (f32[1024,256]{1,0:T(8,128)}, bf16[1536,256]{1,0:T(8,128)(2,1)}, f32[104,256]{1,0:T(8,128)}, bf16[1536,256]{1,0:T(8,128)(2,1)}) custom-call(s32[2,2]{1,0:T(2,128)S(1)} %copy-done.12, s32[1,2]{1,0:T(1,128)S(1)} %bitcast.24, bf16[1024,256]{1,0:T(8,128)(2,1)S(1)} %copy-done, bf16[1024,256]{1,0:T(8,128)(2,1)S(1)} %copy-done.1, ...), custom_call_target="tpu_custom_call" | custom-call | flops 5400000000 | bytes 4194304 | tf_op jit(solution)/shard_map/rest/pallas_call | solution.py:305
  50.9 8.6 %all-to-all-done.1 = bf16[64,24,256]{2,1,0:T(8,128)(2,1)S(1)} async-done(((bf16[64,24,256]{2,1,0:T(8,128)(2,1)}), bf16[64,24,256]{2,1,0:T(8,128)(2,1)S(1)}, u32[]{:S(2)}, u32[]{:S(2)}) %all-to-all-start.1) | async-done | bytes 786464 | tf_op jit(solution)/shard_map/all_to_all | solution.py:597
  59.9 1.4 collective-permute-start
  61.3 2.6 %collective-permute-start.1 = (bf16[256,256]{1,0:T(8,128)(2,1)S(1)}, bf16[256,256]{1,0:T(8,128)(2,1)S(1)}, u32[]{:S(2)}, u32[]{:S(2)}) collective-permute-start(bf16[256,256]{1,0:T(8,128)(2,1)S(1)} %contribution.1.c0), channel_id=1, source_target_pairs={{0,2},{1,3},{2,0},{3,1},{4,6},{5,7},{6,4},{7,5},{8,10},{9,11},{10,... | collective-permute-start | bytes 393224 | tf_op jit(solution)/shard_map/ppermute | solution.py:601
  63.9 1.1 collective-permute-start.2
  65.0 2.5 %tables_one.1 = (bf16[1536,256]{1,0:T(8,128)(2,1)S(1)}, f32[384,256]{1,0:T(8,128)S(1)}) custom-call(s32[2,2]{1,0:T(2,128)S(1)} %copy-done.12, s32[1,2]{1,0:T(1,128)S(1)} %bitcast.25, f32[64,128]{1,0:T(8,128)S(1)} %get-tuple-element.40.ids_ref, s32[3,8,1536]{2,1,0:T(8,128)S(1)} %get-tuple-element.45.rows_ref, bf16[1536,256]{1,0:T(8,128)(2,1)S(1)} %bitcast.15, ...), custom_call_target="tpu_custom_call" | custom-call | flops 2000000000 | bytes 4194304 | tf_op jit(solution)/shard_map/tables_one/pallas_call | solution.py:379
  67.5 2.4 %collective-permute-done.1.c2 = bf16[256,256]{1,0:T(8,128)(2,1)S(1)} collective-permute-done((bf16[256,256]{1,0:T(8,128)(2,1)S(1)}, bf16[256,256]{1,0:T(8,128)(2,1)S(1)}, u32[]{:S(2)}, u32[]{:S(2)}) %collective-permute-start.1) | collective-permute-done | bytes 131104 | tf_op jit(solution)/shard_map/ppermute | solution.py:601
  70.0 2.8 %live.1 = (bf16[1536,256]{1,0:T(8,128)(2,1)S(1)}, f32[256,256]{1,0:T(8,128)S(1)}, f32[104,256]{1,0:T(8,128)S(1)}) custom-call(s32[2,2]{1,0:T(2,128)S(1)} %copy-done.13, s32[1,2]{1,0:T(1,128)S(1)} %bitcast.26, bf16[1024,256]{1,0:T(8,128)(2,1)S(1)} %copy-done, bf16[1024,256]{1,0:T(8,128)(2,1)S(1)} %copy-done, bf16[1024,256]{1,0:T(8,128)(2,1)S(1)} %copy-done.2, ...), custom_call_target="tpu_custom_call" | custom-call | flops 1600000000 | bytes 4194304 | tf_op jit(solution)/shard_map/live/pallas_call | solution.py:443
  72.8 29.7 %all_to_all.25 = bf16[64,24,256]{2,1,0:T(8,128)(2,1)S(1)} all-to-all(bf16[64,24,256]{2,1,0:T(8,128)(2,1)S(1)} %bitcast.18), channel_id=1, replica_groups=mesh['ent'=64,'rel'=4] {'ent'}, dimensions={0} | all-to-all | bytes 1572864 | tf_op jit(solution)/shard_map/all_to_all | solution.py:597
  103.3 20.7 %all_to_all.26.in_ref = bf16[64,8,384]{2,1,0:T(8,128)(2,1)S(1)} all-to-all(bf16[64,8,384]{2,1,0:T(8,128)(2,1)S(1)} %bitcast.19), channel_id=1, replica_groups=mesh['ent'=64,'rel'=4] {'ent'}, dimensions={0} | all-to-all | bytes 786432 | tf_op jit(solution)/shard_map/all_to_all | solution.py:597
  124.8 6.2 %all-to-all-start.4 = ((bf16[64,8,384]{2,1,0:T(8,128)(2,1)}), bf16[64,8,384]{2,1,0:T(8,128)(2,1)S(1)}, u32[]{:S(2)}, u32[]{:S(2)}) async-start(bf16[64,8,384]{2,1,0:T(8,128)(2,1)} %combine.1), calls=%async_computation.4 | async-start | bytes 786432 | tf_op jit(solution)/shard_map/all_to_all | solution.py:597
  131.1 1.2 collective-permute-start.3
  132.3 2.1 %collective-permute-start.4 = (bf16[256,256]{1,0:T(8,128)(2,1)S(1)}, bf16[256,256]{1,0:T(8,128)(2,1)S(1)}, u32[]{:S(2)}, u32[]{:S(2)}) collective-permute-start(bf16[256,256]{1,0:T(8,128)(2,1)S(1)} %get-tuple-element.59.c0), channel_id=1, source_target_pairs={{0,2},{1,3},{2,0},{3,1},{4,6},{5,7},{6,4},{7,5},{8,10},{9,11},{10,... | collective-permute-start | bytes 393224 | tf_op jit(solution)/shard_map/ppermute | solution.py:601
  134.4 1.1 collective-permute-start.5
  135.5 1.5 collective-permute-done.3.c1
  137.0 3.4 %collective-permute-done.4.c2 = bf16[256,256]{1,0:T(8,128)(2,1)S(1)} collective-permute-done((bf16[256,256]{1,0:T(8,128)(2,1)S(1)}, bf16[256,256]{1,0:T(8,128)(2,1)S(1)}, u32[]{:S(2)}, u32[]{:S(2)}) %collective-permute-start.4) | collective-permute-done | bytes 131104 | tf_op jit(solution)/shard_map/ppermute | solution.py:601
  141.0 1.4 final.1
  142.4 3.2 %all-to-all-done.4 = bf16[64,8,384]{2,1,0:T(8,128)(2,1)S(1)} async-done(((bf16[64,8,384]{2,1,0:T(8,128)(2,1)}), bf16[64,8,384]{2,1,0:T(8,128)(2,1)S(1)}, u32[]{:S(2)}, u32[]{:S(2)}) %all-to-all-start.4) | async-done | bytes 393248 | tf_op jit(solution)/shard_map/all_to_all | solution.py:597
  (52 shorter events, 6.0 us)
Async XLA Ops:
  0.6 15.0 %copy-start.10 = (bf16[2,256,32]{1,2,0:T(8,128)(2,1)S(1)}, bf16[2,256,32]{1,2,0:T(8,128)(2,1)}, u32[]{:S(2)}) copy-start(bf16[2,256,32]{1,2,0:T(8,128)(2,1)} %param.23) | copy-start | bytes 98308
  2.4 13.2 %copy-start.8 = (bf16[2,64,256]{2,1,0:T(8,128)(2,1)S(1)}, bf16[2,64,256]{2,1,0:T(8,128)(2,1)}, u32[]{:S(2)}) copy-start(bf16[2,64,256]{2,1,0:T(8,128)(2,1)} %w_in_ref.5) | copy-start | bytes 196612
  2.4 13.2 %copy-start.15 = (f32[2,256]{1,0:T(2,128)S(1)}, f32[2,256]{1,0:T(2,128)}, u32[]{:S(2)}) copy-start(f32[2,256]{1,0:T(2,128)} %w_bias_ref.5) | copy-start | bytes 6148
  2.5 22.4 %all-to-all-start = ((f32[64,1,128]{2,1,0:T(1,128)}), f32[64,1,128]{2,1,0:T(1,128)S(1)}, u32[]{:S(2)}, u32[]{:S(2)}) async-start(f32[64,1,128]{2,1,0:T(1,128)} %get-tuple-element.36), calls=%async_computation | async-start | bytes 65536 | tf_op jit(solution)/shard_map/all_to_all | solution.py:597
  27.2 32.3 %all-to-all-start.1 = ((bf16[64,24,256]{2,1,0:T(8,128)(2,1)}), bf16[64,24,256]{2,1,0:T(8,128)(2,1)S(1)}, u32[]{:S(2)}, u32[]{:S(2)}) async-start(bf16[64,24,256]{2,1,0:T(8,128)(2,1)} %bitcast.7), calls=%async_computation.1 | async-start | bytes 1572864 | tf_op jit(solution)/shard_map/all_to_all | solution.py:597
  59.5 5.5 %copy-start.2 = (bf16[1024,256]{1,0:T(8,128)(2,1)S(1)}, bf16[1024,256]{1,0:T(8,128)(2,1)}, u32[]{:S(2)}) copy-start(bf16[1024,256]{1,0:T(8,128)(2,1)} %state_b.1) | copy-start | bytes 1572868
  59.5 5.5 %copy-start.20 = (bf16[1024,256]{1,0:T(8,128)(2,1)S(1)}, bf16[1024,256]{1,0:T(8,128)(2,1)}, u32[]{:S(2)}) copy-start(bf16[1024,256]{1,0:T(8,128)(2,1)} %one_b.1) | copy-start | bytes 1572868
  59.9 10.0 %copy-start.4 = (bf16[1536,256]{1,0:T(8,128)(2,1)S(1)}, bf16[1536,256]{1,0:T(8,128)(2,1)}, u32[]{:S(2)}) copy-start(bf16[1536,256]{1,0:T(8,128)(2,1)} %get-tuple-element.51.rest_ref) | copy-start | bytes 2359300
  59.9 10.0 %copy-start.5 = (bf16[1536,256]{1,0:T(8,128)(2,1)S(1)}, bf16[1536,256]{1,0:T(8,128)(2,1)}, u32[]{:S(2)}) copy-start(bf16[1536,256]{1,0:T(8,128)(2,1)} %get-tuple-element.50.live_ref) | copy-start | bytes 2359300
  59.9 10.0 %copy-start.9 = (bf16[2,64,256]{2,1,0:T(8,128)(2,1)S(1)}, bf16[2,64,256]{2,1,0:T(8,128)(2,1)}, u32[]{:S(2)}) copy-start(bf16[2,64,256]{2,1,0:T(8,128)(2,1)} %w_in_ref.5) | copy-start | bytes 196612
  59.9 10.0 %copy-start.11 = (bf16[2,256,32]{1,2,0:T(8,128)(2,1)S(1)}, bf16[2,256,32]{1,2,0:T(8,128)(2,1)}, u32[]{:S(2)}) copy-start(bf16[2,256,32]{1,2,0:T(8,128)(2,1)} %param.23) | copy-start | bytes 98308
  59.9 7.6 %collective-permute-start = (bf16[256,256]{1,0:T(8,128)(2,1)S(1)}, bf16[256,256]{1,0:T(8,128)(2,1)S(1)}, u32[]{:S(2)}, u32[]{:S(2)}) collective-permute-start(bf16[256,256]{1,0:T(8,128)(2,1)S(1)} %contribution.1.c0), channel_id=1, source_target_pairs={{0,1},{1,2},{2,3},{3,0},{4,5},{5,6},{6,7},{7,4},{8,9},{9,10},{10,1... | collective-permute-start | bytes 393224 | tf_op jit(solution)/shard_map/ppermute | solution.py:601
  61.3 8.6 %collective-permute-start.1 = (bf16[256,256]{1,0:T(8,128)(2,1)S(1)}, bf16[256,256]{1,0:T(8,128)(2,1)S(1)}, u32[]{:S(2)}, u32[]{:S(2)}) collective-permute-start(bf16[256,256]{1,0:T(8,128)(2,1)S(1)} %contribution.1.c0), channel_id=1, source_target_pairs={{0,2},{1,3},{2,0},{3,1},{4,6},{5,7},{6,4},{7,5},{8,10},{9,11},{10,... | collective-permute-start | bytes 393224 | tf_op jit(solution)/shard_map/ppermute | solution.py:601
  63.9 6.0 %collective-permute-start.2 = (bf16[256,256]{1,0:T(8,128)(2,1)S(1)}, bf16[256,256]{1,0:T(8,128)(2,1)S(1)}, u32[]{:S(2)}, u32[]{:S(2)}) collective-permute-start(bf16[256,256]{1,0:T(8,128)(2,1)S(1)} %contribution.1.c0), channel_id=1, source_target_pairs={{0,3},{1,0},{2,1},{3,2},{4,7},{5,4},{6,5},{7,6},{8,11},{9,8},{10,9... | collective-permute-start | bytes 393224 | tf_op jit(solution)/shard_map/ppermute | solution.py:601
  67.5 2.5 %copy-start.16 = (f32[2,256]{1,0:T(2,128)S(1)}, f32[2,256]{1,0:T(2,128)}, u32[]{:S(2)}) copy-start(f32[2,256]{1,0:T(2,128)} %w_bias_ref.5) | copy-start | bytes 6148
  67.5 2.5 %copy-start.13 = (s32[2,2]{1,0:T(2,128)S(1)}, s32[2,2]{1,0:T(2,128)}, u32[]{:S(2)}) copy-start(s32[2,2]{1,0:T(2,128)} %tiles_ref.9) | copy-start | bytes 52
  67.5 2.5 %copy-start.18 = (s32[2,1]{0,1:T(1,128)S(1)}, s32[2,1]{0,1:T(1,128)}, u32[]{:S(2)}) copy-start(s32[2,1]{0,1:T(1,128)} %param.25) | copy-start | bytes 28
  72.8 29.7 %copy-start.6 = (f32[104,256]{1,0:T(8,128)S(1)}, f32[104,256]{1,0:T(8,128)}, u32[]{:S(2)}) copy-start(f32[104,256]{1,0:T(8,128)} %get-tuple-element.56.w2_ref) | copy-start | bytes 319492
  72.8 29.7 %copy-start.7 = (f32[104,256]{1,0:T(8,128)S(1)}, f32[104,256]{1,0:T(8,128)}, u32[]{:S(2)}) copy-start(f32[104,256]{1,0:T(8,128)} %get-tuple-element.57.w1a_ref) | copy-start | bytes 319492
  103.3 37.1 %copy-start.3 = (f32[1024,256]{1,0:T(8,128)S(1)}, f32[1024,256]{1,0:T(8,128)}, u32[]{:S(2)}) copy-start(f32[1024,256]{1,0:T(8,128)} %get-tuple-element.37.next_ref) | copy-start | bytes 3145732
  124.8 20.8 %all-to-all-start.4 = ((bf16[64,8,384]{2,1,0:T(8,128)(2,1)}), bf16[64,8,384]{2,1,0:T(8,128)(2,1)S(1)}, u32[]{:S(2)}, u32[]{:S(2)}) async-start(bf16[64,8,384]{2,1,0:T(8,128)(2,1)} %combine.1), calls=%async_computation.4 | async-start | bytes 786432 | tf_op jit(solution)/shard_map/all_to_all | solution.py:597
  131.1 5.9 %collective-permute-start.3 = (bf16[256,256]{1,0:T(8,128)(2,1)S(1)}, bf16[256,256]{1,0:T(8,128)(2,1)S(1)}, u32[]{:S(2)}, u32[]{:S(2)}) collective-permute-start(bf16[256,256]{1,0:T(8,128)(2,1)S(1)} %get-tuple-element.59.c0), channel_id=1, source_target_pairs={{0,1},{1,2},{2,3},{3,0},{4,5},{5,6},{6,7},{7,4},{8,9},{9,10},{10,1... | collective-permute-start | bytes 393224 | tf_op jit(solution)/shard_map/ppermute | solution.py:601
  132.3 8.1 %collective-permute-start.4 = (bf16[256,256]{1,0:T(8,128)(2,1)S(1)}, bf16[256,256]{1,0:T(8,128)(2,1)S(1)}, u32[]{:S(2)}, u32[]{:S(2)}) collective-permute-start(bf16[256,256]{1,0:T(8,128)(2,1)S(1)} %get-tuple-element.59.c0), channel_id=1, source_target_pairs={{0,2},{1,3},{2,0},{3,1},{4,6},{5,7},{6,4},{7,5},{8,10},{9,11},{10,... | collective-permute-start | bytes 393224 | tf_op jit(solution)/shard_map/ppermute | solution.py:601
  134.4 5.9 %collective-permute-start.5 = (bf16[256,256]{1,0:T(8,128)(2,1)S(1)}, bf16[256,256]{1,0:T(8,128)(2,1)S(1)}, u32[]{:S(2)}, u32[]{:S(2)}) collective-permute-start(bf16[256,256]{1,0:T(8,128)(2,1)S(1)} %get-tuple-element.59.c0), channel_id=1, source_target_pairs={{0,3},{1,0},{2,1},{3,2},{4,7},{5,4},{6,5},{7,6},{8,11},{9,8},{10,9... | collective-permute-start | bytes 393224 | tf_op jit(solution)/shard_map/ppermute | solution.py:601
  (7 other events, 8.3 us)

commit v5 on v4

--- a/solution.py
+++ b/solution.py
@@ -48,7 +48,7 @@
     return pl.CostEstimate(flops=int(flops), bytes_accessed=int(nbytes), transcendentals=int(trans))
 
 
-def slots_kernel(peers, owner_hbm, target_hbm, source_hbm, relation_hbm, request_ref, ids_ref,
+def slots_kernel(peers, tiles_ref, count_ref, owner_hbm, target_hbm, source_hbm, relation_hbm, request_ref, ids_ref,
                  owner_ref, target_ref, source_ref, relation_ref, sems):
     pairs = ((owner_hbm, owner_ref), (target_hbm, target_ref), (source_hbm, source_ref), (relation_hbm, relation_ref))
     copies = [pltpu.make_async_copy(a, b, sems.at[i]) for i, (a, b) in enumerate(pairs)]
@@ -57,35 +57,41 @@
     for copy in copies:
         copy.wait()
     edges = owner_ref.shape[1]
-    owner = owner_ref[...]
-    hit = (iota((peers, edges), 0) == owner).astype(F32)
-    hit_low = hit.astype(BF16)
+    hit = (iota((peers, edges), 0) == owner_ref[...]).astype(F32)
     below = (iota((TILE, TILE), 0) < iota((TILE, TILE), 1)).astype(BF16)
-    offset = jnp.zeros((peers, 1), F32)
-    pieces = []
-    for b in range(edges // TILE):
-        block = hit_low[:, b * TILE:(b + 1) * TILE]
-        pieces.append(dot_nn(block, below) + offset)
-        offset = offset + jnp.sum(hit[:, b * TILE:(b + 1) * TILE], axis=1, keepdims=True)
-    before = jnp.concatenate(pieces, axis=1)
-    earlier = jnp.sum(before * hit, axis=0, keepdims=True).astype(jnp.int32)
-    place = (iota((32, edges), 0) == earlier).astype(F32)
-
-    def spread(values):
-        high = lax.shift_right_logical(values, 5)
-        low = values & 31
-        return [place * high.astype(F32), place * low.astype(F32)]
-
-    zero = jnp.zeros((64, edges), F32)
-    first = jnp.concatenate(spread(target_ref[...]) + [zero], axis=0).astype(BF16)
-    request_ref[:, 0, :] = dot_nt(hit_low, first)
-    second = jnp.concatenate(
-        spread(source_ref[...] + 1) + spread(relation_ref[...] + 1), axis=0
-    ).astype(BF16)
-    ids_ref[...] = dot_nt(hit_low, second)
-
-
-def slot_columns(table, capacity, bases):
+    tile = lax.shift_right_logical(source_ref[...], 7)
+    request, tops = [], []
+    for hop in (1, 0):
+        live = (tile == tiles_ref[hop, 0]) | ((tile == tiles_ref[hop, 1]) & (count_ref[0, hop] > 1))
+        own = jnp.where(live, hit, 0.0)
+        own_low = own.astype(BF16)
+        offset = jnp.zeros((peers, 1), F32)
+        pieces = []
+        for b in range(edges // TILE):
+            block = slice(b * TILE, (b + 1) * TILE)
+            pieces.append(dot_nn(own_low[:, block], below) + offset)
+            offset = offset + jnp.sum(own[:, block], axis=1, keepdims=True)
+        earlier = jnp.sum(jnp.concatenate(pieces, axis=1) * own, axis=0, keepdims=True).astype(jnp.int32)
+        place = jnp.where((iota((32, edges), 0) == earlier) & live, 1.0, 0.0)
+
+        def spread(values):
+            high = lax.shift_right_logical(values, 5)
+            low = values & 31
+            return [place * high.astype(F32), place * low.astype(F32)]
+
+        request += spread(target_ref[...])
+        tops.append(jnp.max(offset, axis=0, keepdims=True))
+        second = jnp.concatenate(
+            spread(source_ref[...] + 1) + spread(relation_ref[...] + 1), axis=0
+        ).astype(BF16)
+        ids_ref[hop] = dot_nt(own_low, second)
+    lane = iota((peers, 128), 1)
+    sent = dot_nt(hit.astype(BF16), jnp.concatenate(request, axis=0).astype(BF16))
+    sent = jnp.where(lane == 31, tops[0], sent)
+    request_ref[:, 0, :] = jnp.where(lane == 95, tops[1], sent)
+
+
+def slot_columns(table, capacity, bases, skip=0):
     peers = table.shape[0]
     slots = peers * capacity
     row = iota((slots, peers), 0)
@@ -94,7 +100,7 @@
     spread = dot_nn(expand, table.astype(BF16))
     row = iota((slots, 128), 0)
     group = ((row.astype(F32) + 0.5) * (1.0 / capacity)).astype(jnp.int32)
-    place = row - group * capacity
+    place = row - group * capacity + skip
     lane = iota((slots, 128), 1)
     columns = []
     for base in bases:
@@ -116,7 +122,10 @@
 
 
 def onehot(column, width):
-    return (iota((column.shape[0], width), 1) == column).astype(F32).astype(BF16)
+    shape = (column.shape[0], width)
+    lane = lax.broadcasted_iota(jnp.int16, shape, 1)
+    hit = lane == jnp.broadcast_to(column, shape).astype(jnp.int16)
+    return jnp.where(hit, jnp.ones((), BF16), jnp.zeros((), BF16))
 
 
 def build_weights(layer, w_in_ref, w_bias_ref, w_out_ref, wx_ref, wu_ref, wb_ref):
@@ -233,7 +242,7 @@
 
 def first_pass(agg, state, up, w_in, w_bias, w_out):
     rows, feat = agg.shape
-    blocks = rows // 256
+    blocks = rows // 512
     return pl.pallas_call(
         functools.partial(first_kernel, blocks),
         in_specs=[HBM, HBM, HBM, VMEM, VMEM, VMEM],
@@ -253,15 +262,15 @@
     )(in_hbm(agg), in_hbm(state), in_hbm(up), w_in, w_bias, w_out)
 
 
-def pick_kernel(capacity, asked_ref, grad_agg, picked_ref):
-    asked = slot_columns(asked_ref[:, 0, :], capacity, (0,))[0]
+def pick_kernel(capacity, skip, base, asked_ref, grad_agg, picked_ref):
+    asked = slot_columns(asked_ref[:, 0, :], capacity, (base,), skip)[0]
     pick_rows(asked, grad_agg, picked_ref)
 
 
-def pick(capacity, asked, grad_agg):
+def pick(capacity, skip, base, asked, grad_agg):
     slots, feat = asked.shape[0] * capacity, grad_agg.shape[1]
     return pl.pallas_call(
-        functools.partial(pick_kernel, capacity),
+        functools.partial(pick_kernel, capacity, skip, base),
         in_specs=[VMEM, VMEM],
         out_specs=VMEM,
         out_shape=jax.ShapeDtypeStruct((slots, feat), BF16),
@@ -272,8 +281,8 @@
 
 
 def rest_kernel(capacity, tiles_ref, count_ref, agg_ref, state_ref, up_ref, w_in_ref, w_bias_ref, w_out_ref,
-                asked_ref, next_ref, picked_ref, sums_ref, live_ref, wx, wu, wb,
-                acc_in, acc_out, grad_agg):
+                asked_ref, next_ref, picked_ref, sums_ref, live_ref, grad_agg, wx, wu, wb,
+                acc_in, acc_out):
     step = pl.program_id(0)
     rows = agg_ref.shape[0]
     count = count_ref[0, 1]
@@ -292,7 +301,7 @@
     @pl.when(step == pl.num_programs(0) - 1)
     def _():
         store_sums(acc_in, acc_out, sums_ref)
-        asked = slot_columns(asked_ref[:, 0, :], capacity, (0,))[0]
+        asked = slot_columns(asked_ref[:, 0, :], capacity, (64,))[0]
         live_ref[...] = onehot(compact_column(asked, (tiles_ref[1, 0], tiles_ref[1, 1]), count), 2 * TILE)
         pick_rows(asked, grad_agg, picked_ref)
 
@@ -307,14 +316,16 @@
         grid=(rows // block,),
         in_specs=[SMEM, SMEM, row_spec, row_spec, row_spec, whole(w_in.shape), whole(w_bias.shape),
                   whole(w_out.shape), whole(asked.shape)],
-        out_specs=[row_spec, whole((slots, feat)), whole((SUM_ROWS, WIDE)), whole((slots, 2 * TILE))],
+        out_specs=[row_spec, whole((slots, feat)), whole((SUM_ROWS, WIDE)), whole((slots, 2 * TILE)),
+                   whole((rows, feat))],
         out_shape=[
             pltpu.HBM((rows, feat), F32),
             pltpu.HBM((slots, feat), BF16),
             pltpu.HBM((SUM_ROWS, WIDE), F32),
             pltpu.HBM((slots, 2 * TILE), BF16),
+            pltpu.HBM((rows, feat), BF16),
         ],
-        scratch_shapes=scratch(WEIGHT_SHAPES + SUM_SHAPES) + [pltpu.VMEM((rows, feat), BF16)],
+        scratch_shapes=scratch(WEIGHT_SHAPES + SUM_SHAPES),
         compiler_params=params(),
         cost_estimate=cost(5.4e9, 4 << 20, 2 << 20),
         name="rest",
@@ -329,28 +340,33 @@
     return (iota((width, row.shape[1]), 0) == row).astype(F32).astype(BF16)
 
 
-def tables_two_kernel(capacity, tiles_ref, count_ref, ids_ref, table_ref, t_ref, rows_ref):
-    source, relation = slot_columns(ids_ref[...], capacity, (0, 64))
+def relation_rows(relation, table_ref):
     width = -(-table_ref.shape[0] // TILE) * TILE
     pad = width - table_ref.shape[0]
     table = jnp.concatenate([table_ref[...], jnp.zeros((pad, table_ref.shape[1]), BF16)], axis=0)
-    t_ref[...] = dot_nn(onehot(relation - 1, width), table).astype(BF16)
-    rows_ref[0] = as_row(relation - 1)
+    return dot_nn(onehot(relation, width), table).astype(BF16)
+
+
+def tables_two_kernel(capacity, tiles_ref, count_ref, ids_ref, table_ref, t_ref, rows_ref):
     for hop in range(2):
+        source, relation = slot_columns(ids_ref[hop], capacity, (0, 64))
+        if hop == 1:
+            t_ref[...] = relation_rows(relation - 1, table_ref)
+        rows_ref[hop] = as_row(relation - 1)
         column = compact_column(source - 1, (tiles_ref[hop, 0], tiles_ref[hop, 1]), count_ref[0, hop])
-        rows_ref[1 + hop] = as_row(column)
+        rows_ref[2 + hop] = as_row(column)
 
 
 def tables_two(capacity, tiles, count, ids, table):
     feat = table.shape[1]
-    slots = ids.shape[0] * capacity
+    slots = ids.shape[1] * capacity
     return pl.pallas_call(
         functools.partial(tables_two_kernel, capacity),
         in_specs=[SMEM, SMEM, VMEM, VMEM],
         out_specs=[VMEM, VMEM],
         out_shape=[
             jax.ShapeDtypeStruct((slots, feat), BF16),
-            jax.ShapeDtypeStruct((3, 8, slots), jnp.int32),
+            jax.ShapeDtypeStruct((4, 8, slots), jnp.int32),
         ],
         compiler_params=params(),
         cost_estimate=cost(1e9, 2 << 20),
@@ -358,20 +374,22 @@
     )(tiles, count, ids, table)
 
 
-def tables_one_kernel(capacity, tiles_ref, count_ref, ids_ref, rows_ref, answer_ref, one_a, one_b, zero_a, zero_b,
-                      h_ref, total_ref):
-    source = slot_columns(ids_ref[...], capacity, (0,))[0] - 1
-    columns = [
-        compact_column(source, (tiles_ref[hop, 0], tiles_ref[hop, 1]), count_ref[0, hop]) for hop in range(2)
-    ]
-    h_ref[...] = dot_nn(onehot(columns[0], 2 * TILE), jnp.concatenate([zero_a[...], zero_b[...]], axis=0)).astype(BF16)
-    states = dot_nn(onehot(columns[1], 2 * TILE), jnp.concatenate([one_a[...], one_b[...]], axis=0)).astype(BF16)
-    total_ref[...] = dot_nn(onehot_rows(rows_ref[0, 0:1, :], total_ref.shape[0]), answer_ref[...] * states)
-
-
-def tables_one(capacity, tiles, count, ids, rows, answer, state_one, state_zero, groups):
+def tables_one_kernel(capacity, tiles_ref, count_ref, ids_ref, rows_ref, table_ref, answer_ref,
+                      one_a, one_b, zero_a, zero_b, t_ref, h_ref, total_ref):
+    states = []
+    for hop, a, b in ((0, zero_a, zero_b), (1, one_a, one_b)):
+        source, relation = slot_columns(ids_ref[hop], capacity, (0, 64))
+        column = compact_column(source - 1, (tiles_ref[hop, 0], tiles_ref[hop, 1]), count_ref[0, hop])
+        states.append(dot_nn(onehot(column, 2 * TILE), jnp.concatenate([a[...], b[...]], axis=0)).astype(BF16))
+        if hop == 0:
+            t_ref[...] = relation_rows(relation - 1, table_ref)
+    h_ref[...] = states[0]
+    total_ref[...] = dot_nn(onehot_rows(rows_ref[1, 0:1, :], total_ref.shape[0]), answer_ref[...] * states[1])
+
+
+def tables_one(capacity, tiles, count, ids, rows, table, answer, state_one, state_zero):
     slots, feat = answer.shape
-    width = -(-groups // TILE) * TILE
+    width = -(-table.shape[0] // TILE) * TILE
 
     def tile(hop, k):
         return pl.BlockSpec((TILE, feat), lambda i, tiles, count: (tiles[hop, k], 0))
@@ -381,22 +399,57 @@
         grid_spec=pltpu.PrefetchScalarGridSpec(
             num_scalar_prefetch=2,
             grid=(1,),
-            in_specs=[whole(ids.shape), whole(rows.shape), whole(answer.shape), tile(1, 0), tile(1, 1), tile(0, 0),
-                      tile(0, 1)],
-            out_specs=[whole((slots, feat)), whole((width, feat))],
+            in_specs=[whole(ids.shape), whole(rows.shape), whole(table.shape), whole(answer.shape), tile(1, 0),
+                      tile(1, 1), tile(0, 0), tile(0, 1)],
+            out_specs=[whole((slots, feat)), whole((slots, feat)), whole((width, feat))],
         ),
         out_shape=[
             jax.ShapeDtypeStruct((slots, feat), BF16),
+            jax.ShapeDtypeStruct((slots, feat), BF16),
             jax.ShapeDtypeStruct((width, feat), F32),
         ],
         compiler_params=params(),
         cost_estimate=cost(2e9, 4 << 20),
         name="tables_one",
-    )(tiles, count, ids, rows, answer, state_one, state_one, state_zero, state_zero)
+    )(tiles, count, ids, rows, table, answer, state_one, state_one, state_zero, state_zero)
+
+
+def extra_kernel(hop, capacity, skip, tiles_ref, count_ref, ids_ref, table_ref, answer_ref, state_a, state_b,
+                 part_ref, out_ref, total_ref):
+    source, relation = slot_columns(ids_ref[hop], capacity, (0, 64), skip)
+    column = compact_column(source - 1, (tiles_ref[hop, 0], tiles_ref[hop, 1]), count_ref[0, hop])
+    select = onehot(column, 2 * TILE)
+    answer = answer_ref[...]
+    more = dot_nn(onehot_rows(as_row(column)[0:1], 2 * TILE), answer * relation_rows(relation - 1, table_ref))
+    out_ref[...] = (part_ref[...].astype(F32) + more).astype(BF16)
+    states = dot_nn(select, jnp.concatenate([state_a[...], state_b[...]], axis=0)).astype(BF16)
+    total_ref[...] = dot_nn(onehot_rows(as_row(relation - 1)[0:1], total_ref.shape[0]), answer * states)
+
+
+def extra(hop, capacity, skip, tiles, count, ids, table, answer, state, part):
+    feat = answer.shape[1]
+    width = -(-table.shape[0] // TILE) * TILE
+
+    def tile(k):
+        return pl.BlockSpec((TILE, feat), lambda i, tiles, count: (tiles[hop, k], 0))
+
+    return pl.pallas_call(
+        functools.partial(extra_kernel, hop, capacity, skip),
+        grid_spec=pltpu.PrefetchScalarGridSpec(
+            num_scalar_prefetch=2,
+            grid=(1,),
+            in_specs=[whole(ids.shape), whole(table.shape), whole(answer.shape), tile(0), tile(1), whole(part.shape)],
+            out_specs=[whole(part.shape), whole((width, feat))],
+        ),
+        out_shape=[jax.ShapeDtypeStruct(part.shape, BF16), jax.ShapeDtypeStruct((width, feat), F32)],
+        compiler_params=params(),
+        cost_estimate=cost(1e9, 2 << 20),
+        name="extra",
+    )(tiles, count, ids, table, answer, state, state, part)
 
 
 def contribution_kernel(answer_ref, t_ref, rows_ref, out_ref):
-    select = onehot_rows(rows_ref[2, 0:1, :], 2 * TILE)
+    select = onehot_rows(rows_ref[3, 0:1, :], 2 * TILE)
     out_ref[...] = dot_nn(select, answer_ref[...] * t_ref[...]).astype(BF16)
 
 
@@ -413,7 +466,7 @@
 
 
 def live_kernel(tiles_ref, count_ref, agg_a, agg_b, state_a, state_b, up_a, up_b, c0, c1, c2, c3,
-                w_in_ref, w_bias_ref, w_out_ref, live_ref, rest_ref, picked_ref, next_ref, sums_ref,
+                w_in_ref, w_bias_ref, w_out_ref, live_ref, rest_ref, picked_ref, next_ref, sums_ref, grad_ref,
                 wx, wu, wb, acc_in, acc_out):
     build_weights(0, w_in_ref, w_bias_ref, w_out_ref, wx, wu, wb)
     clear(acc_in, acc_out)
@@ -431,6 +484,7 @@
     grad_agg = jnp.concatenate(aggs, axis=1).astype(BF16)
     next_ref[...] = up + jnp.concatenate(states, axis=1)
     store_sums(acc_in, acc_out, sums_ref)
+    grad_ref[...] = grad_agg
     picked_ref[...] = (dot_nn(live_ref[...], grad_agg) + rest_ref[...].astype(F32)).astype(BF16)
 
 
@@ -447,13 +501,14 @@
             grid=(1,),
             in_specs=[tile(0), tile(1)] * 3 + [whole(parts[0].shape)] * 4
             + [whole(w.shape) for w in weights] + [whole(live.shape), whole(rest.shape)],
-            out_specs=[whole(rest.shape), whole((2 * TILE, feat)), whole((SUM_ROWS, WIDE))],
+            out_specs=[whole(rest.shape), whole((2 * TILE, feat)), whole((SUM_ROWS, WIDE)), whole((2 * TILE, feat))],
             scratch_shapes=scratch(WEIGHT_SHAPES + SUM_SHAPES),
         ),
         out_shape=[
             jax.ShapeDtypeStruct(rest.shape, BF16),
             jax.ShapeDtypeStruct((2 * TILE, feat), F32),
             jax.ShapeDtypeStruct((SUM_ROWS, WIDE), F32),
+            jax.ShapeDtypeStruct((2 * TILE, feat), BF16),
         ],
         compiler_params=params(),
         cost_estimate=cost(1.6e9, 4 << 20, 1 << 19),
@@ -461,12 +516,32 @@
     )(tiles, count, agg, agg, state, state, up, up, *parts, *weights, live, rest)
 
 
+def late_kernel(capacity, skip, tiles_ref, count_ref, asked_ref, rest_ref, live_ref, picked_ref):
+    asked = slot_columns(asked_ref[:, 0, :], capacity, (64,), skip)[0]
+    column = compact_column(asked, (tiles_ref[1, 0], tiles_ref[1, 1]), count_ref[0, 1])
+    rest = dot_nn(onehot(asked, rest_ref.shape[0]), rest_ref[...])
+    picked_ref[...] = (dot_nn(onehot(column, 2 * TILE), live_ref[...]) + rest).astype(BF16)
+
+
+def late_pick(capacity, skip, tiles, count, asked, rest, live):
+    slots, feat = asked.shape[0] * capacity, rest.shape[1]
+    return pl.pallas_call(
+        functools.partial(late_kernel, capacity, skip),
+        in_specs=[SMEM, SMEM, VMEM, VMEM, VMEM],
+        out_specs=VMEM,
+        out_shape=jax.ShapeDtypeStruct((slots, feat), BF16),
+        compiler_params=params(),
+        cost_estimate=cost(8e8, 1 << 20),
+        name="late_pick",
+    )(tiles, count, asked, rest, live)
+
+
 GAP = SUM_ROWS
 
 
 def pack_kernel(answer_ref, t_ref, h_ref, rows_ref, before_ref, w2_ref, w1a_ref, w1b_ref, part_ref, out_ref):
     answer = answer_ref[...]
-    part_ref[...] = dot_nn(onehot_rows(rows_ref[1, 0:1, :], 2 * TILE), answer * t_ref[...]).astype(BF16)
+    part_ref[...] = dot_nn(onehot_rows(rows_ref[2, 0:1, :], 2 * TILE), answer * t_ref[...]).astype(BF16)
     select = onehot_rows(rows_ref[0, 0:1, :], before_ref.shape[0])
     total = before_ref[...] + dot_nn(select, answer * h_ref[...])
     used, feat = total.shape
@@ -590,7 +665,9 @@
     quarter = block_rows // group_size
     edges = edge_source.shape[0]
     capacity = 3 * edges // (2 * peers)
-    slots = peers * capacity
+    regular = 2 * capacity // 3
+    over = capacity - regular
+    slots = peers * regular
     sum_rows = 8 * peers
 
     def exchange(chunks):
@@ -608,39 +685,65 @@
     weights = (update_in, update_bias, jnp.swapaxes(update_out, 1, 2))
     request, ids = pl.pallas_call(
         functools.partial(slots_kernel, peers),
-        in_specs=[HBM] * 4,
+        in_specs=[SMEM] * 2 + [HBM] * 4,
         out_specs=[VMEM] * 2,
         out_shape=[
             jax.ShapeDtypeStruct((peers, 1, 128), F32),
-            jax.ShapeDtypeStruct((peers, 128), F32),
+            jax.ShapeDtypeStruct((2, peers, 128), F32),
         ],
         scratch_shapes=[pltpu.VMEM((1, edges), jnp.int32)] * 4 + [pltpu.SemaphoreType.DMA((4,))],
         compiler_params=params(8 << 20),
         cost_estimate=cost(1e8, 1 << 20),
         name="slots",
-    )(*(in_hbm(row(values)) for values in (edge_owner, edge_target, edge_source, edge_relation)))
+    )(frontier_tiles, count, *(in_hbm(row(values)) for values in (edge_owner, edge_target, edge_source, edge_relation)))
     asked = exchange(request)
+    more_two = jnp.max(asked[:, 0, 31]) > regular
+    more_any = jnp.maximum(jnp.max(asked[:, 0, 31]), jnp.max(asked[:, 0, 95])) > regular
 
     upstream_one, grad_agg, sums_two = first_pass(aggregate_two, state_one, cotangent, *weights)
-    picked_two = pick(capacity, asked, grad_agg)
-    answered_two = exchange(picked_two.reshape(peers, capacity, feat)).reshape(slots, feat)
-    after, rest, sums_rest, live = rest_pass(
-        capacity, frontier_tiles, count, aggregate_one, state_zero, upstream_one, *weights, asked
+    picked_two = pick(regular, 0, 0, asked, grad_agg)
+    answered_two = exchange(picked_two.reshape(peers, regular, feat)).reshape(slots, feat)
+    after, rest, sums_rest, live, grad_rest = rest_pass(
+        regular, frontier_tiles, count, aggregate_one, state_zero, upstream_one, *weights, asked
     )
-    edge_table, rows = tables_two(capacity, frontier_tiles, count, ids, relation_table)
-    answered_two, rest, edge_table, rows = lax.optimization_barrier((answered_two, rest, edge_table, rows))
-    parts = over_rel(contribution(answered_two, edge_table, rows))
-    states_one, relation_two = tables_one(
-        capacity, frontier_tiles, count, ids, rows, answered_two, state_one, state_zero, groups
+    edge_table, rows = tables_two(regular, frontier_tiles, count, ids, relation_table)
+    answered_two, rest, edge_table, rows, more_two, more_any = lax.optimization_barrier(
+        (answered_two, rest, edge_table, rows, more_two, more_any)
     )
-    parts[0], rest, states_one, relation_two = lax.optimization_barrier((parts[0], rest, states_one, relation_two))
-    picked_one, after_live, sums_live = live_pass(
+
+    def over_two(part):
+        picked = pick(over, regular, 0, asked, grad_agg)
+        answer = exchange(picked.reshape(peers, over, feat)).reshape(peers * over, feat)
+        return extra(1, over, regular, frontier_tiles, count, ids, relation_table, answer, state_one, part)
+
+    part = contribution(answered_two, edge_table, rows)
+    part = lax.cond(more_two, lambda part: over_two(part)[0], lambda part: part, part)
+    parts = over_rel(part)
+    table_one, states_one, relation_two = tables_one(
+        regular, frontier_tiles, count, ids, rows, relation_table, answered_two, state_one, state_zero
+    )
+    parts[0], rest, table_one, states_one, relation_two = lax.optimization_barrier(
+        (parts[0], rest, table_one, states_one, relation_two)
+    )
+    picked_one, after_live, sums_live, grad_live = live_pass(
         frontier_tiles, count, aggregate_one, state_zero, upstream_one, parts, weights, live, rest
     )
-    answered_one = exchange(picked_one.reshape(peers, capacity, feat)).reshape(slots, feat)
+    answered_one = exchange(picked_one.reshape(peers, regular, feat)).reshape(slots, feat)
+    answered_one, more_any = lax.optimization_barrier((answered_one, more_any))
     part, packed = pack_sums(
-        answered_one, edge_table, states_one, rows, relation_two, sums_two, sums_rest, sums_live, sum_rows
+        answered_one, table_one, states_one, rows, relation_two, sums_two, sums_rest, sums_live, sum_rows
     )
+
+    def over_any(part, packed):
+        first = over_two(part)[1]
+        picked = late_pick(over, regular, frontier_tiles, count, asked, grad_rest, grad_live)
+        answer = exchange(picked.reshape(peers, over, feat)).reshape(peers * over, feat)
+        part, second = extra(0, over, regular, frontier_tiles, count, ids, relation_table, answer, state_zero, part)
+        used = first.shape[0]
+        total = packed[:used, :feat].astype(F32) + (first + second)
+        return part, packed.at[:used, :feat].set(total.astype(BF16))
+
+    part, packed = lax.cond(more_any, over_any, lambda part, packed: (part, packed), part, packed)
     parts = over_rel(part)
     scale_weights = 1.0 / math.sqrt(block_rows * peers * QUERIES)
     scale_relations = math.sqrt(groups * group_size / (edges * peers * group_size))

time: 147 us -> 142 us (0.966)
  waiting for transfers between devices: 19.9 us -> 12.2 us
  blocking collectives: 50.4 us -> 47.8 us
  between operations: 0.92 us -> 2.84 us
  local copies, waits for them, and re-layouts: 2.35 us -> 4.21 us
    all_to_all x3, waiting for transfers between devices: 12.7 us -> 5.93 us  [exchange(): lax.all_to_all(chunks, 'ent', split_axis=0, concat_axis=0, tiled=True)]
    all_to_all x2, blocking collectives: 50.4 us -> 47.8 us  [exchange(): lax.all_to_all(chunks, 'ent', split_axis=0, concat_axis=0, tiled=True)]
    unnamed x44, local copies, waits for them, and re-layouts: 2.35 us -> 4.2 us
  transfers between devices with their start and end apart: 9 -> 9, of which waited for: 6 -> 6; matrix products, arithmetic and copies ran while one was open for 0% -> 1% of each run, Pallas kernels for 17% -> 17%
where the time goes in v5:
time: 142 us; the launch traced here: 141 us
  blocking collectives  47.8 us (34%)
  starting transfers between devices  38.6 us (27%)
  Pallas kernels  34.2 us (24%)
  waiting for transfers between devices  12.2 us (9%)
  local copies, waits for them, and re-layouts  4.21 us (3%)
  between operations  2.84 us (2%)
    all_to_all x2, blocking collectives, exchange(): lax.all_to_all(chunks, 'ent', split_axis=0, concat_axis=0, tiled=True)  47.8 us
    all_to_all x3, starting transfers between devices, exchange(): lax.all_to_all(chunks, 'ent', split_axis=0, concat_axis=0, tiled=True)  29.1 us
    pallas_call x1, Pallas kernels, rest_pass(): pl.pallas_call(functools.partial(rest_kernel, capacity), grid=(rows // bl...  9.86 us
    ppermute x6, starting transfers between devices, over_rel(): lax.ppermute(part, 'rel', [(i, (i + k) % group_size) for i in range(group...  9.5 us
    pallas_call x1, Pallas kernels, first_pass(): pl.pallas_call(functools.partial(first_kernel, blocks), in_specs=[HBM, HB...  7.58 us
    ppermute x6, waiting for transfers between devices, over_rel(): lax.ppermute(part, 'rel', [(i, (i + k) % group_size) for i in range(group...  6.32 us
    all_to_all x3, waiting for transfers between devices, exchange(): lax.all_to_all(chunks, 'ent', split_axis=0, concat_axis=0, tiled=True)  5.93 us
    unnamed x44, local copies, waits for them, and re-layouts  4.2 us
  transfers between devices with their start and end apart: 9, of which 6 were waited for; matrix products, arithmetic and copies ran while one was open for 1% of the time, Pallas kernels for 17%

profile of v5, /device:TPU:1, one launch (start us, length us, event | category | flops | bytes accessed | tf_op | source)
XLA Modules:
  0.0 141.0 jit_solution(1016905378210097799)
XLA Ops:
  1.3 2.5 %slots.1 = (f32[64,1,128]{2,1,0:T(1,128)}, f32[2,64,128]{2,1,0:T(8,128)S(1)}) custom-call(s32[2,2]{1,0:T(2,128)S(1)} %copy-done.12, s32[1,2]{1,0:T(1,128)S(1)} %bitcast.32, s32[1,1024]{1,0:T(1,128)} %bitcast.41, s32[1,1024]{1,0:T(1,128)} %bitcast.42, s32[1,1024]{1,0:T(1,128)} %bitcast.43, s32[1,1024]{1,0:T(1,128)} %bitcast.44), custom_call_target="tpu_custom_call" | custom-call | flops 100000000 | bytes 1048576 | tf_op jit(solution)/shard_map/slots/pallas_call | solution.py:686
  3.9 13.1 %all-to-all-start.3 = ((f32[64,1,128]{2,1,0:T(1,128)}), f32[64,1,128]{2,1,0:T(1,128)S(1)}, u32[]{:S(2)}, u32[]{:S(2)}) async-start(f32[64,1,128]{2,1,0:T(1,128)} %get-tuple-element.130), calls=%async_computation.3 | async-start | bytes 65536 | tf_op jit(solution)/shard_map/all_to_all | solution.py:674
  17.0 7.6 %first.1 = (f32[1024,256]{1,0:T(8,128)S(1)}, bf16[1024,256]{1,0:T(8,128)(2,1)S(1)}, f32[104,256]{1,0:T(8,128)}) custom-call(bf16[1024,256]{1,0:T(8,128)(2,1)} %agg_hbm.1, bf16[1024,256]{1,0:T(8,128)(2,1)} %one_b.1, bf16[1024,256]{1,0:T(8,128)(2,1)} %up_hbm.1, bf16[2,64,256]{2,1,0:T(8,128)(2,1)S(1)} %copy-done.4, f32[2,256]{1,0:T(2,128)S(1)} %copy-done.6, ...), custom_call_target="tpu_custom_call" | custom-call | flops 5400000000 | bytes 4194304 | tf_op jit(solution)/shard_map/first/pallas_call | solution.py:246
  26.2 1.8 %pick.5 = bf16[1024,256]{1,0:T(8,128)(2,1)} custom-call(f32[64,1,128]{2,1,0:T(1,128)S(1)} %all-to-all-done.3.asked_ref, bf16[1024,256]{1,0:T(8,128)(2,1)S(1)} %get-tuple-element.132.grad_agg), custom_call_target="tpu_custom_call" | custom-call | flops 800000000 | bytes 1048576 | tf_op jit(solution)/shard_map/pick/pallas_call | solution.py:272
  28.1 9.8 %all-to-all-start.4 = ((bf16[64,16,256]{2,1,0:T(8,128)(2,1)}), bf16[64,16,256]{2,1,0:T(8,128)(2,1)S(1)}, u32[]{:S(2)}, u32[]{:S(2)}) async-start(bf16[64,16,256]{2,1,0:T(8,128)(2,1)} %bitcast.13), calls=%async_computation.4 | async-start | bytes 1048576 | tf_op jit(solution)/shard_map/all_to_all | solution.py:674
  37.9 2.2 %tables_two.1 = (bf16[1024,256]{1,0:T(8,128)(2,1)S(1)}, s32[4,8,1024]{2,1,0:T(8,128)S(1)}) custom-call(s32[2,2]{1,0:T(2,128)S(1)} %copy-done.12, s32[1,2]{1,0:T(1,128)S(1)} %bitcast.33, f32[2,64,128]{2,1,0:T(8,128)S(1)} %get-tuple-element.134.ids_ref, bf16[328,256]{1,0:T(8,128)(2,1)S(1)} %copy-done.19), custom_call_target="tpu_custom_call" | custom-call | flops 1000000000 | bytes 2097152 | tf_op jit(solution)/shard_map/tables_two/pallas_call | solution.py:363
  42.8 1.2 copy-done.8
  44.0 9.9 %rest.1 = (f32[1024,256]{1,0:T(8,128)}, bf16[1024,256]{1,0:T(8,128)(2,1)}, f32[104,256]{1,0:T(8,128)}, bf16[1024,256]{1,0:T(8,128)(2,1)}, bf16[1024,256]{1,0:T(8,128)(2,1)}) custom-call(s32[2,2]{1,0:T(2,128)S(1)} %copy-done.12, s32[1,2]{1,0:T(1,128)S(1)} %bitcast.34, bf16[1024,256]{1,0:T(8,128)(2,1)S(1)} %copy-done.3, bf16[1024,256]{1,0:T(8,128)(2,1)S(1)} %copy-done.14, ...), custom_call_target="tpu_custom_call" | custom-call | flops 5400000000 | bytes 4194304 | tf_op jit(solution)/shard_map/rest/pallas_call | solution.py:314
  53.9 1.2 all-to-all-done.4
  56.2 1.4 collective-permute-start
  57.6 2.6 %collective-permute-start.1 = (bf16[256,256]{1,0:T(8,128)(2,1)S(1)}, bf16[256,256]{1,0:T(8,128)(2,1)S(1)}, u32[]{:S(2)}, u32[]{:S(2)}) collective-permute-start(bf16[256,256]{1,0:T(8,128)(2,1)S(1)} %get-tuple-element.175.c0), channel_id=1, source_target_pairs={{0,2},{1,3},{2,0},{3,1},{4,6},{5,7},{6,4},{7,5},{8,10},{9,11},{10,... | collective-permute-start | bytes 393224 | tf_op jit(solution)/shard_map/ppermute | solution.py:678
  60.2 1.1 collective-permute-start.2
  61.3 3.4 %tables_one.1 = (bf16[1024,256]{1,0:T(8,128)(2,1)S(1)}, bf16[1024,256]{1,0:T(8,128)(2,1)S(1)}, f32[384,256]{1,0:T(8,128)S(1)}) custom-call(s32[2,2]{1,0:T(2,128)S(1)} %copy-done.12, s32[1,2]{1,0:T(1,128)S(1)} %bitcast.36, f32[2,64,128]{2,1,0:T(8,128)S(1)} %get-tuple-element.134.ids_ref, s32[4,8,1024]{2,1,0:T(8,128)S(1)} %get-tuple-element.140.rows_ref, ...), custom_call_target="tpu_custom_call" | custom-call | flops 2000000000 | bytes 4194304 | tf_op jit(solution)/shard_map/tables_one/pallas_call | solution.py:397
  64.7 1.7 %collective-permute-done.1.c2 = bf16[256,256]{1,0:T(8,128)(2,1)S(1)} collective-permute-done((bf16[256,256]{1,0:T(8,128)(2,1)S(1)}, bf16[256,256]{1,0:T(8,128)(2,1)S(1)}, u32[]{:S(2)}, u32[]{:S(2)}) %collective-permute-start.1) | collective-permute-done | bytes 131104 | tf_op jit(solution)/shard_map/ppermute | solution.py:678
  66.4 3.0 %live.1 = (bf16[1024,256]{1,0:T(8,128)(2,1)S(1)}, f32[256,256]{1,0:T(8,128)S(1)}, f32[104,256]{1,0:T(8,128)S(1)}, bf16[256,256]{1,0:T(8,128)(2,1)}) custom-call(s32[2,2]{1,0:T(2,128)S(1)} %copy-done.12, s32[1,2]{1,0:T(1,128)S(1)} %bitcast.37, bf16[1024,256]{1,0:T(8,128)(2,1)S(1)} %copy-done.3, bf16[1024,256]{1,0:T(8,128)(2,1)S(1)} %copy-done.3, ...), custom_call_target="tpu_custom_call" | custom-call | flops 1600000000 | bytes 4194304 | tf_op jit(solution)/shard_map/live/pallas_call | solution.py:497
  69.4 27.0 %all_to_all.37 = bf16[64,16,256]{2,1,0:T(8,128)(2,1)S(1)} all-to-all(bf16[64,16,256]{2,1,0:T(8,128)(2,1)S(1)} %bitcast.24), channel_id=1, replica_groups=mesh['ent'=64,'rel'=4] {'ent'}, dimensions={0} | all-to-all | bytes 1048576 | tf_op jit(solution)/shard_map/all_to_all | solution.py:674
  97.7 20.8 %all_to_all.38.in_ref = bf16[64,8,384]{2,1,0:T(8,128)(2,1)S(1)} all-to-all(bf16[64,8,384]{2,1,0:T(8,128)(2,1)S(1)} %bitcast.31), channel_id=1, replica_groups=mesh['ent'=64,'rel'=4] {'ent'}, dimensions={0} | all-to-all | bytes 786432 | tf_op jit(solution)/shard_map/all_to_all | solution.py:674
  119.4 6.2 %all-to-all-start.7 = ((bf16[64,8,384]{2,1,0:T(8,128)(2,1)}), bf16[64,8,384]{2,1,0:T(8,128)(2,1)S(1)}, u32[]{:S(2)}, u32[]{:S(2)}) async-start(bf16[64,8,384]{2,1,0:T(8,128)(2,1)} %combine.1), calls=%async_computation.7 | async-start | bytes 786432 | tf_op jit(solution)/shard_map/all_to_all | solution.py:674
  126.6 2.1 %collective-permute-start.4 = (bf16[256,256]{1,0:T(8,128)(2,1)S(1)}, bf16[256,256]{1,0:T(8,128)(2,1)S(1)}, u32[]{:S(2)}, u32[]{:S(2)}) collective-permute-start(bf16[256,256]{1,0:T(8,128)(2,1)S(1)} %get-tuple-element.163.c0), channel_id=1, source_target_pairs={{0,2},{1,3},{2,0},{3,1},{4,6},{5,7},{6,4},{7,5},{8,10},{9,11},{10,... | collective-permute-start | bytes 393224 | tf_op jit(solution)/shard_map/ppermute | solution.py:678
  128.7 1.3 collective-permute-start.5
  130.0 1.5 %collective-permute-done.3.c1 = bf16[256,256]{1,0:T(8,128)(2,1)S(1)} collective-permute-done((bf16[256,256]{1,0:T(8,128)(2,1)S(1)}, bf16[256,256]{1,0:T(8,128)(2,1)S(1)}, u32[]{:S(2)}, u32[]{:S(2)}) %collective-permute-start.3) | collective-permute-done | bytes 131104 | tf_op jit(solution)/shard_map/ppermute | solution.py:678
  131.5 3.2 %collective-permute-done.4.c2 = bf16[256,256]{1,0:T(8,128)(2,1)S(1)} collective-permute-done((bf16[256,256]{1,0:T(8,128)(2,1)S(1)}, bf16[256,256]{1,0:T(8,128)(2,1)S(1)}, u32[]{:S(2)}, u32[]{:S(2)}) %collective-permute-start.4) | collective-permute-done | bytes 131104 | tf_op jit(solution)/shard_map/ppermute | solution.py:678
  134.7 1.4 %final.1 = bf16[256,256]{1,0:T(8,128)(2,1)} custom-call(s32[2,2]{1,0:T(2,128)S(1)} %copy-done.12, s32[1,2]{1,0:T(1,128)S(1)} %bitcast.39, s32[1]{0:T(128)} %bitcast.7.quarter_ref, f32[1024,256]{1,0:T(8,128)S(1)} %copy-done, f32[256,256]{1,0:T(8,128)S(1)} %get-tuple-element.148.live_ref, bf16[256,256]{1,0:T(8,128)(2,1)S(1)} %get-tuple-element.163.c0, ...), custom_call_target="tpu_custom_call" | custom-call | flops 1000000 | bytes 1048576 | tf_op jit(solution)/shard_map/final/pallas_call | solution.py:643
  136.1 4.0 %all-to-all-done.7 = bf16[64,8,384]{2,1,0:T(8,128)(2,1)S(1)} async-done(((bf16[64,8,384]{2,1,0:T(8,128)(2,1)}), bf16[64,8,384]{2,1,0:T(8,128)(2,1)S(1)}, u32[]{:S(2)}, u32[]{:S(2)}) %all-to-all-start.7) | async-done | bytes 393248 | tf_op jit(solution)/shard_map/all_to_all | solution.py:674
  (56 shorter events, 8.3 us)
Async XLA Ops:
  1.3 15.7 %copy-start.5 = (bf16[2,256,32]{1,2,0:T(8,128)(2,1)S(1)}, bf16[2,256,32]{1,2,0:T(8,128)(2,1)}, u32[]{:S(2)}) copy-start(bf16[2,256,32]{1,2,0:T(8,128)(2,1)} %param.29) | copy-start | bytes 98308
  3.8 57.4 %copy-start.21 = (f32[2,64,128]{2,1,0:T(8,128)}, f32[2,64,128]{2,1,0:T(8,128)S(1)}, u32[]{:S(2)}) copy-start(f32[2,64,128]{2,1,0:T(8,128)S(1)} %get-tuple-element.134.ids_ref) | copy-start | bytes 196612
  3.8 13.2 %copy-start.4 = (bf16[2,64,256]{2,1,0:T(8,128)(2,1)S(1)}, bf16[2,64,256]{2,1,0:T(8,128)(2,1)}, u32[]{:S(2)}) copy-start(bf16[2,64,256]{2,1,0:T(8,128)(2,1)} %w_in_ref.5) | copy-start | bytes 196612
  3.9 13.2 %copy-start.6 = (f32[2,256]{1,0:T(2,128)S(1)}, f32[2,256]{1,0:T(2,128)}, u32[]{:S(2)}) copy-start(f32[2,256]{1,0:T(2,128)} %w_bias_ref.5) | copy-start | bytes 6148
  3.9 22.4 %all-to-all-start.3 = ((f32[64,1,128]{2,1,0:T(1,128)}), f32[64,1,128]{2,1,0:T(1,128)S(1)}, u32[]{:S(2)}, u32[]{:S(2)}) async-start(f32[64,1,128]{2,1,0:T(1,128)} %get-tuple-element.130), calls=%async_computation.3 | async-start | bytes 65536 | tf_op jit(solution)/shard_map/all_to_all | solution.py:674
  25.6 2.5 %copy-start.23 = (bf16[1024,256]{1,0:T(8,128)(2,1)}, bf16[1024,256]{1,0:T(8,128)(2,1)S(1)}, u32[]{:S(2)}) copy-start(bf16[1024,256]{1,0:T(8,128)(2,1)S(1)} %get-tuple-element.132.grad_agg) | copy-start | bytes 1572868
  28.0 9.8 %copy-start.19 = (bf16[328,256]{1,0:T(8,128)(2,1)S(1)}, bf16[328,256]{1,0:T(8,128)(2,1)}, u32[]{:S(2)}) copy-start(bf16[328,256]{1,0:T(8,128)(2,1)} %table_ref.3) | copy-start | bytes 503812
  28.1 27.1 %all-to-all-start.4 = ((bf16[64,16,256]{2,1,0:T(8,128)(2,1)}), bf16[64,16,256]{2,1,0:T(8,128)(2,1)S(1)}, u32[]{:S(2)}, u32[]{:S(2)}) async-start(bf16[64,16,256]{2,1,0:T(8,128)(2,1)} %bitcast.13), calls=%async_computation.4 | async-start | bytes 1048576 | tf_op jit(solution)/shard_map/all_to_all | solution.py:674
  37.9 4.9 %copy-start.3 = (bf16[1024,256]{1,0:T(8,128)(2,1)S(1)}, bf16[1024,256]{1,0:T(8,128)(2,1)}, u32[]{:S(2)}) copy-start(bf16[1024,256]{1,0:T(8,128)(2,1)} %agg_b.1) | copy-start | bytes 1572868
  37.9 4.9 %copy-start.14 = (bf16[1024,256]{1,0:T(8,128)(2,1)S(1)}, bf16[1024,256]{1,0:T(8,128)(2,1)}, u32[]{:S(2)}) copy-start(bf16[1024,256]{1,0:T(8,128)(2,1)} %state_b.1) | copy-start | bytes 1572868
  56.2 10.2 %copy-start.9 = (f32[1024,256]{1,0:T(8,128)S(1)}, f32[1024,256]{1,0:T(8,128)}, u32[]{:S(2)}) copy-start(f32[1024,256]{1,0:T(8,128)} %copy-done.7) | copy-start | bytes 3145732
  56.2 10.2 %copy-start.10 = (bf16[1024,256]{1,0:T(8,128)(2,1)S(1)}, bf16[1024,256]{1,0:T(8,128)(2,1)}, u32[]{:S(2)}) copy-start(bf16[1024,256]{1,0:T(8,128)(2,1)} %get-tuple-element.147.rest_ref) | copy-start | bytes 1572868
  56.2 10.2 %copy-start.11 = (bf16[1024,256]{1,0:T(8,128)(2,1)S(1)}, bf16[1024,256]{1,0:T(8,128)(2,1)}, u32[]{:S(2)}) copy-start(bf16[1024,256]{1,0:T(8,128)(2,1)} %get-tuple-element.146.live_ref) | copy-start | bytes 1572868
  56.2 10.2 %copy-start.15 = (bf16[1024,256]{1,0:T(8,128)(2,1)S(1)}, bf16[1024,256]{1,0:T(8,128)(2,1)}, u32[]{:S(2)}) copy-start(bf16[1024,256]{1,0:T(8,128)(2,1)} %state_b.1) | copy-start | bytes 1572868
  56.2 8.5 %collective-permute-start = (bf16[256,256]{1,0:T(8,128)(2,1)S(1)}, bf16[256,256]{1,0:T(8,128)(2,1)S(1)}, u32[]{:S(2)}, u32[]{:S(2)}) collective-permute-start(bf16[256,256]{1,0:T(8,128)(2,1)S(1)} %get-tuple-element.175.c0), channel_id=1, source_target_pairs={{0,1},{1,2},{2,3},{3,0},{4,5},{5,6},{6,7},{7,4},{8,9},{9,10},{10,1... | collective-permute-start | bytes 393224 | tf_op jit(solution)/shard_map/ppermute | solution.py:678
  57.6 8.8 %collective-permute-start.1 = (bf16[256,256]{1,0:T(8,128)(2,1)S(1)}, bf16[256,256]{1,0:T(8,128)(2,1)S(1)}, u32[]{:S(2)}, u32[]{:S(2)}) collective-permute-start(bf16[256,256]{1,0:T(8,128)(2,1)S(1)} %get-tuple-element.175.c0), channel_id=1, source_target_pairs={{0,2},{1,3},{2,0},{3,1},{4,6},{5,7},{6,4},{7,5},{8,10},{9,11},{10,... | collective-permute-start | bytes 393224 | tf_op jit(solution)/shard_map/ppermute | solution.py:678
  60.2 6.2 %collective-permute-start.2 = (bf16[256,256]{1,0:T(8,128)(2,1)S(1)}, bf16[256,256]{1,0:T(8,128)(2,1)S(1)}, u32[]{:S(2)}, u32[]{:S(2)}) collective-permute-start(bf16[256,256]{1,0:T(8,128)(2,1)S(1)} %get-tuple-element.175.c0), channel_id=1, source_target_pairs={{0,3},{1,0},{2,1},{3,2},{4,7},{5,4},{6,5},{7,6},{8,11},{9,8},{10,9... | collective-permute-start | bytes 393224 | tf_op jit(solution)/shard_map/ppermute | solution.py:678
  69.4 27.0 %copy-start.1 = (f32[104,256]{1,0:T(8,128)S(1)}, f32[104,256]{1,0:T(8,128)}, u32[]{:S(2)}) copy-start(f32[104,256]{1,0:T(8,128)} %get-tuple-element.156.w2_ref) | copy-start | bytes 319492
  69.4 27.0 %copy-start.2 = (f32[104,256]{1,0:T(8,128)S(1)}, f32[104,256]{1,0:T(8,128)}, u32[]{:S(2)}) copy-start(f32[104,256]{1,0:T(8,128)} %get-tuple-element.157.w1a_ref) | copy-start | bytes 319492
  97.7 37.0 %copy-start = (f32[1024,256]{1,0:T(8,128)S(1)}, f32[1024,256]{1,0:T(8,128)}, u32[]{:S(2)}) copy-start(f32[1024,256]{1,0:T(8,128)} %get-tuple-element.131.next_ref) | copy-start | bytes 3145732
  119.4 20.8 %all-to-all-start.7 = ((bf16[64,8,384]{2,1,0:T(8,128)(2,1)}), bf16[64,8,384]{2,1,0:T(8,128)(2,1)S(1)}, u32[]{:S(2)}, u32[]{:S(2)}) async-start(bf16[64,8,384]{2,1,0:T(8,128)(2,1)} %combine.1), calls=%async_computation.7 | async-start | bytes 786432 | tf_op jit(solution)/shard_map/all_to_all | solution.py:674
  125.6 5.9 %collective-permute-start.3 = (bf16[256,256]{1,0:T(8,128)(2,1)S(1)}, bf16[256,256]{1,0:T(8,128)(2,1)S(1)}, u32[]{:S(2)}, u32[]{:S(2)}) collective-permute-start(bf16[256,256]{1,0:T(8,128)(2,1)S(1)} %get-tuple-element.163.c0), channel_id=1, source_target_pairs={{0,1},{1,2},{2,3},{3,0},{4,5},{5,6},{6,7},{7,4},{8,9},{9,10},{10,1... | collective-permute-start | bytes 393224 | tf_op jit(solution)/shard_map/ppermute | solution.py:678
  126.6 8.1 %collective-permute-start.4 = (bf16[256,256]{1,0:T(8,128)(2,1)S(1)}, bf16[256,256]{1,0:T(8,128)(2,1)S(1)}, u32[]{:S(2)}, u32[]{:S(2)}) collective-permute-start(bf16[256,256]{1,0:T(8,128)(2,1)S(1)} %get-tuple-element.163.c0), channel_id=1, source_target_pairs={{0,2},{1,3},{2,0},{3,1},{4,6},{5,7},{6,4},{7,5},{8,10},{9,11},{10,... | collective-permute-start | bytes 393224 | tf_op jit(solution)/shard_map/ppermute | solution.py:678
  128.7 5.9 %collective-permute-start.5 = (bf16[256,256]{1,0:T(8,128)(2,1)S(1)}, bf16[256,256]{1,0:T(8,128)(2,1)S(1)}, u32[]{:S(2)}, u32[]{:S(2)}) collective-permute-start(bf16[256,256]{1,0:T(8,128)(2,1)S(1)} %get-tuple-element.163.c0), channel_id=1, source_target_pairs={{0,3},{1,0},{2,1},{3,2},{4,7},{5,4},{6,5},{7,6},{8,11},{9,8},{10,9... | collective-permute-start | bytes 393224 | tf_op jit(solution)/shard_map/ppermute | solution.py:678
  (7 other events, 6.6 us)

commit v6 on v5

--- a/solution.py
+++ b/solution.py
@@ -210,8 +210,8 @@
 
 
 def first_kernel(blocks, agg_hbm, state_hbm, up_hbm, w_in_ref, w_bias_ref, w_out_ref,
-                 next_ref, grad_agg, sums_hbm, wx, wu, wb, acc_in, acc_out, sums_ref,
-                 agg_buf, state_buf, up_buf, sems):
+                 next_hbm, grad_agg, grad_hbm, sums_hbm, wx, wu, wb, acc_in, acc_out, sums_ref,
+                 agg_buf, state_buf, up_buf, next_buf, sems, out_sems):
     rows = agg_hbm.shape[0] // blocks
 
     def copies(step):
@@ -232,12 +232,15 @@
         part = pl.ds(pl.multiple_of(step * rows, rows), rows)
         up_low = up_buf[part, :]
         dense_step(step, agg_buf.at[part], state_buf.at[part], up_low.astype(F32), up_low, wx, wu, wb,
-                   acc_in, acc_out, grad_agg, next_ref.at[part])
+                   acc_in, acc_out, grad_agg, next_buf.at[part])
 
     store_sums(acc_in, acc_out, sums_ref)
-    copy = pltpu.make_async_copy(sums_ref, sums_hbm, sems.at[0, 0])
-    copy.start()
-    copy.wait()
+    pairs = ((next_buf, next_hbm), (grad_agg, grad_hbm), (sums_ref, sums_hbm))
+    copies = [pltpu.make_async_copy(a, b, out_sems.at[i]) for i, (a, b) in enumerate(pairs)]
+    for copy in copies:
+        copy.start()
+    for copy in copies:
+        copy.wait()
 
 
 def first_pass(agg, state, up, w_in, w_bias, w_out):
@@ -246,23 +249,27 @@
     return pl.pallas_call(
         functools.partial(first_kernel, blocks),
         in_specs=[HBM, HBM, HBM, VMEM, VMEM, VMEM],
-        out_specs=[VMEM, VMEM, HBM],
-        out_shape=[
-            jax.ShapeDtypeStruct((rows, feat), F32),
+        out_specs=[HBM, VMEM, HBM, HBM],
+        out_shape=[
+            pltpu.HBM((rows, feat), F32),
             jax.ShapeDtypeStruct((rows, feat), BF16),
+            pltpu.HBM((rows, feat), BF16),
             pltpu.HBM((SUM_ROWS, WIDE), F32),
         ],
         scratch_shapes=scratch(WEIGHT_SHAPES + SUM_SHAPES)
         + [pltpu.VMEM((SUM_ROWS, WIDE), F32)]
         + [pltpu.VMEM((rows, feat), BF16)] * 3
-        + [pltpu.SemaphoreType.DMA((blocks, 3))],
+        + [pltpu.VMEM((rows, feat), F32), pltpu.SemaphoreType.DMA((blocks, 3)), pltpu.SemaphoreType.DMA((3,))],
         compiler_params=params(),
         cost_estimate=cost(5.4e9, 4 << 20, 2 << 20),
         name="first",
     )(in_hbm(agg), in_hbm(state), in_hbm(up), w_in, w_bias, w_out)
 
 
-def pick_kernel(capacity, skip, base, asked_ref, grad_agg, picked_ref):
+def pick_kernel(capacity, skip, base, asked_ref, grad_agg, picked_ref, two_ref, any_ref):
+    two, one = jnp.max(asked_ref[:, 0, 31:32]), jnp.max(asked_ref[:, 0, 95:96])
+    two_ref[0] = (two > capacity).astype(jnp.int32)
+    any_ref[0] = (jnp.maximum(two, one) > capacity).astype(jnp.int32)
     asked = slot_columns(asked_ref[:, 0, :], capacity, (base,), skip)[0]
     pick_rows(asked, grad_agg, picked_ref)
 
@@ -272,8 +279,12 @@
     return pl.pallas_call(
         functools.partial(pick_kernel, capacity, skip, base),
         in_specs=[VMEM, VMEM],
-        out_specs=VMEM,
-        out_shape=jax.ShapeDtypeStruct((slots, feat), BF16),
+        out_specs=[VMEM, SMEM, SMEM],
+        out_shape=[
+            jax.ShapeDtypeStruct((slots, feat), BF16),
+            jax.ShapeDtypeStruct((1,), jnp.int32),
+            jax.ShapeDtypeStruct((1,), jnp.int32),
+        ],
         compiler_params=params(12 << 20),
         cost_estimate=cost(8e8, 1 << 20),
         name="pick",
@@ -309,7 +320,7 @@
 def rest_pass(capacity, tiles, count, agg, state, up, w_in, w_bias, w_out, asked):
     rows, feat = agg.shape
     slots = asked.shape[0] * capacity
-    block = 256
+    block = 512
     row_spec = pl.BlockSpec((block, feat), lambda i: (i, 0))
     return pl.pallas_call(
         functools.partial(rest_kernel, capacity),
@@ -329,7 +340,7 @@
         compiler_params=params(),
         cost_estimate=cost(5.4e9, 4 << 20, 2 << 20),
         name="rest",
-    )(tiles, count, agg, state, up, w_in, w_bias, w_out, asked)
+    )(tiles, count, in_hbm(agg), in_hbm(state), in_hbm(up), w_in, w_bias, w_out, asked)
 
 
 def as_row(column):
@@ -508,7 +519,7 @@
             jax.ShapeDtypeStruct(rest.shape, BF16),
             jax.ShapeDtypeStruct((2 * TILE, feat), F32),
             jax.ShapeDtypeStruct((SUM_ROWS, WIDE), F32),
-            jax.ShapeDtypeStruct((2 * TILE, feat), BF16),
+            pltpu.HBM((2 * TILE, feat), BF16),
         ],
         compiler_params=params(),
         cost_estimate=cost(1.6e9, 4 << 20, 1 << 19),
@@ -695,13 +706,12 @@
         compiler_params=params(8 << 20),
         cost_estimate=cost(1e8, 1 << 20),
         name="slots",
-    )(frontier_tiles, count, *(in_hbm(row(values)) for values in (edge_owner, edge_target, edge_source, edge_relation)))
+    )(in_hbm(frontier_tiles), in_hbm(count), *(in_hbm(row(values)) for values in (edge_owner, edge_target, edge_source, edge_relation)))
     asked = exchange(request)
-    more_two = jnp.max(asked[:, 0, 31]) > regular
-    more_any = jnp.maximum(jnp.max(asked[:, 0, 31]), jnp.max(asked[:, 0, 95])) > regular
-
-    upstream_one, grad_agg, sums_two = first_pass(aggregate_two, state_one, cotangent, *weights)
-    picked_two = pick(regular, 0, 0, asked, grad_agg)
+
+    upstream_one, grad_agg, grad_kept, sums_two = first_pass(aggregate_two, state_one, cotangent, *weights)
+    picked_two, more_two, more_any = pick(regular, 0, 0, asked, grad_agg)
+    more_two, more_any = more_two[0], more_any[0]
     answered_two = exchange(picked_two.reshape(peers, regular, feat)).reshape(slots, feat)
     after, rest, sums_rest, live, grad_rest = rest_pass(
         regular, frontier_tiles, count, aggregate_one, state_zero, upstream_one, *weights, asked
@@ -712,12 +722,14 @@
     )
 
     def over_two(part):
-        picked = pick(over, regular, 0, asked, grad_agg)
+        picked = pick(over, regular, 0, asked, in_hbm(grad_kept))[0]
         answer = exchange(picked.reshape(peers, over, feat)).reshape(peers * over, feat)
-        return extra(1, over, regular, frontier_tiles, count, ids, relation_table, answer, state_one, part)
+        return extra(
+            1, over, regular, frontier_tiles, count, in_hbm(ids), in_hbm(relation_table), answer, in_hbm(state_one), part
+        )
 
     part = contribution(answered_two, edge_table, rows)
-    part = lax.cond(more_two, lambda part: over_two(part)[0], lambda part: part, part)
+    part = lax.switch(more_two, (lambda part: part, lambda part: over_two(part)[0]), part)
     parts = over_rel(part)
     table_one, states_one, relation_two = tables_one(
         regular, frontier_tiles, count, ids, rows, relation_table, answered_two, state_one, state_zero
@@ -736,14 +748,16 @@
 
     def over_any(part, packed):
         first = over_two(part)[1]
-        picked = late_pick(over, regular, frontier_tiles, count, asked, grad_rest, grad_live)
+        picked = late_pick(over, regular, frontier_tiles, count, asked, in_hbm(grad_rest), in_hbm(grad_live))
         answer = exchange(picked.reshape(peers, over, feat)).reshape(peers * over, feat)
-        part, second = extra(0, over, regular, frontier_tiles, count, ids, relation_table, answer, state_zero, part)
+        part, second = extra(
+            0, over, regular, frontier_tiles, count, in_hbm(ids), in_hbm(relation_table), answer, in_hbm(state_zero), part
+        )
         used = first.shape[0]
         total = packed[:used, :feat].astype(F32) + (first + second)
         return part, packed.at[:used, :feat].set(total.astype(BF16))
 
-    part, packed = lax.cond(more_any, over_any, lambda part, packed: (part, packed), part, packed)
+    part, packed = lax.switch(more_any, (lambda part, packed: (part, packed), over_any), part, packed)
     parts = over_rel(part)
     scale_weights = 1.0 / math.sqrt(block_rows * peers * QUERIES)
     scale_relations = math.sqrt(groups * group_size / (edges * peers * group_size))

time: 142 us -> 138 us (0.972)
  waiting for transfers between devices: 12.2 us -> 16.1 us
  local copies, waits for them, and re-layouts: 4.21 us -> 0.74 us
  blocking collectives: 47.8 us -> 44.7 us
    all_to_all x3, waiting for transfers between devices: 5.93 us -> 9.71 us  [exchange(): lax.all_to_all(chunks, 'ent', split_axis=0, concat_axis=0, tiled=True)]
    unnamed x44 -> x30, local copies, waits for them, and re-layouts: 4.2 us -> 0.72 us
    all_to_all x2, blocking collectives: 47.8 us -> 44.7 us  [exchange(): lax.all_to_all(chunks, 'ent', split_axis=0, concat_axis=0, tiled=True)]
  transfers between devices with their start and end apart: 9 -> 9, of which waited for: 6 -> 6; matrix products, arithmetic and copies ran while one was open for 1% -> 0% of each run, Pallas kernels for 17% -> 18%
where the time goes in v6:
time: 138 us; the launch traced here: 137 us
  blocking collectives  44.7 us (32%)
  starting transfers between devices  38.3 us (28%)
  Pallas kernels  35 us (25%)
  waiting for transfers between devices  16.1 us (12%)
  between operations  2.15 us (2%)
    all_to_all x2, blocking collectives, exchange(): lax.all_to_all(chunks, 'ent', split_axis=0, concat_axis=0, tiled=True)  44.7 us
    all_to_all x3, starting transfers between devices, exchange(): lax.all_to_all(chunks, 'ent', split_axis=0, concat_axis=0, tiled=True)  28.8 us
    pallas_call x1, Pallas kernels, rest_pass(): pl.pallas_call(functools.partial(rest_kernel, capacity), grid=(rows // bl...  9.77 us
    all_to_all x3, waiting for transfers between devices, exchange(): lax.all_to_all(chunks, 'ent', split_axis=0, concat_axis=0, tiled=True)  9.71 us
    ppermute x6, starting transfers between devices, over_rel(): lax.ppermute(part, 'rel', [(i, (i + k) % group_size) for i in range(group...  9.51 us
    pallas_call x1, Pallas kernels, first_pass(): pl.pallas_call(functools.partial(first_kernel, blocks), in_specs=[HBM, HB...  8.21 us
    ppermute x6, waiting for transfers between devices, over_rel(): lax.ppermute(part, 'rel', [(i, (i + k) % group_size) for i in range(group...  6.37 us
    pallas_call x1, Pallas kernels, tables_one(): pl.pallas_call(functools.partial(tables_one_kernel, capacity), grid_spec=...  3.37 us
  transfers between devices with their start and end apart: 9, of which 6 were waited for; matrix products, arithmetic and copies ran while one was open for 0% of the time, Pallas kernels for 18%

profile of v6, /device:TPU:1, one launch (start us, length us, event | category | flops | bytes accessed | tf_op | source)
XLA Modules:
  0.0 137.0 jit_solution(502573552859386497)
XLA Ops:
  0.6 2.8 %slots.1 = (f32[64,1,128]{2,1,0:T(1,128)}, f32[2,64,128]{2,1,0:T(8,128)S(1)}) custom-call(s32[2,2]{1,0:T(2,128)} %tiles_ref.11, s32[1,2]{1,0:T(1,128)} %bitcast.34, s32[1,1024]{1,0:T(1,128)} %bitcast.43, s32[1,1024]{1,0:T(1,128)} %bitcast.44, s32[1,1024]{1,0:T(1,128)} %bitcast.45, s32[1,1024]{1,0:T(1,128)} %bitcast.46), custom_call_target="tpu_custom_call" | custom-call | flops 100000000 | bytes 1048576 | tf_op jit(solution)/shard_map/slots/pallas_call | solution.py:697
  3.5 13.1 %all-to-all-start.3 = ((f32[64,1,128]{2,1,0:T(1,128)}), f32[64,1,128]{2,1,0:T(1,128)S(1)}, u32[]{:S(2)}, u32[]{:S(2)}) async-start(f32[64,1,128]{2,1,0:T(1,128)} %get-tuple-element.136), calls=%async_computation.3 | async-start | bytes 65536 | tf_op jit(solution)/shard_map/all_to_all | solution.py:685
  16.6 8.2 %first.1 = (f32[1024,256]{1,0:T(8,128)}, bf16[1024,256]{1,0:T(8,128)(2,1)S(1)}, bf16[1024,256]{1,0:T(8,128)(2,1)}, f32[104,256]{1,0:T(8,128)}) custom-call(bf16[1024,256]{1,0:T(8,128)(2,1)} %agg_hbm.1, bf16[1024,256]{1,0:T(8,128)(2,1)} %one_b.1, bf16[1024,256]{1,0:T(8,128)(2,1)} %up_hbm.1, bf16[2,64,256]{2,1,0:T(8,128)(2,1)S(1)} %copy-done.4, ...), custom_call_target="tpu_custom_call" | custom-call | flops 5400000000 | bytes 4194304 | tf_op jit(solution)/shard_map/first/pallas_call | solution.py:249
  25.8 1.8 %pick.5 = (bf16[1024,256]{1,0:T(8,128)(2,1)}, s32[1]{0:T(128)}, s32[1]{0:T(128)}) custom-call(f32[64,1,128]{2,1,0:T(1,128)S(1)} %all-to-all-done.3.asked_ref, bf16[1024,256]{1,0:T(8,128)(2,1)S(1)} %get-tuple-element.138.grad_agg), custom_call_target="tpu_custom_call" | custom-call | flops 800000000 | bytes 1048576 | tf_op jit(solution)/shard_map/pick/pallas_call | solution.py:279
  27.7 9.5 %all-to-all-start.4 = ((bf16[64,16,256]{2,1,0:T(8,128)(2,1)}), bf16[64,16,256]{2,1,0:T(8,128)(2,1)S(1)}, u32[]{:S(2)}, u32[]{:S(2)}) async-start(bf16[64,16,256]{2,1,0:T(8,128)(2,1)} %bitcast.13), calls=%async_computation.4 | async-start | bytes 1048576 | tf_op jit(solution)/shard_map/all_to_all | solution.py:685
  37.9 2.1 %tables_two.1 = (bf16[1024,256]{1,0:T(8,128)(2,1)S(1)}, s32[4,8,1024]{2,1,0:T(8,128)S(1)}) custom-call(s32[2,2]{1,0:T(2,128)S(1)} %copy-done.10, s32[1,2]{1,0:T(1,128)S(1)} %bitcast.35, f32[2,64,128]{2,1,0:T(8,128)S(1)} %get-tuple-element.141.ids_ref, bf16[328,256]{1,0:T(8,128)(2,1)S(1)} %copy-done.13), custom_call_target="tpu_custom_call" | custom-call | flops 1000000000 | bytes 2097152 | tf_op jit(solution)/shard_map/tables_two/pallas_call | solution.py:374
  40.0 9.8 %rest.1 = (f32[1024,256]{1,0:T(8,128)}, bf16[1024,256]{1,0:T(8,128)(2,1)}, f32[104,256]{1,0:T(8,128)}, bf16[1024,256]{1,0:T(8,128)(2,1)}, bf16[1024,256]{1,0:T(8,128)(2,1)}) custom-call(s32[2,2]{1,0:T(2,128)S(1)} %copy-done.10, s32[1,2]{1,0:T(1,128)S(1)} %bitcast.36, bf16[1024,256]{1,0:T(8,128)(2,1)} %agg_b.1, bf16[1024,256]{1,0:T(8,128)(2,1)} %state_b.1, ...), custom_call_target="tpu_custom_call" | custom-call | flops 5400000000 | bytes 4194304 | tf_op jit(solution)/shard_map/rest/pallas_call | solution.py:325
  49.8 4.7 %all-to-all-done.4 = bf16[64,16,256]{2,1,0:T(8,128)(2,1)S(1)} async-done(((bf16[64,16,256]{2,1,0:T(8,128)(2,1)}), bf16[64,16,256]{2,1,0:T(8,128)(2,1)S(1)}, u32[]{:S(2)}, u32[]{:S(2)}) %all-to-all-start.4) | async-done | bytes 524320 | tf_op jit(solution)/shard_map/all_to_all | solution.py:685
  55.5 1.4 %collective-permute-start = (bf16[256,256]{1,0:T(8,128)(2,1)S(1)}, bf16[256,256]{1,0:T(8,128)(2,1)S(1)}, u32[]{:S(2)}, u32[]{:S(2)}) collective-permute-start(bf16[256,256]{1,0:T(8,128)(2,1)S(1)} %get-tuple-element.183.c0), channel_id=1, source_target_pairs={{0,1},{1,2},{2,3},{3,0},{4,5},{5,6},{6,7},{7,4},{8,9},{9,10},{10,1... | collective-permute-start | bytes 393224 | tf_op jit(solution)/shard_map/ppermute | solution.py:689
  56.9 2.6 %collective-permute-start.1 = (bf16[256,256]{1,0:T(8,128)(2,1)S(1)}, bf16[256,256]{1,0:T(8,128)(2,1)S(1)}, u32[]{:S(2)}, u32[]{:S(2)}) collective-permute-start(bf16[256,256]{1,0:T(8,128)(2,1)S(1)} %get-tuple-element.183.c0), channel_id=1, source_target_pairs={{0,2},{1,3},{2,0},{3,1},{4,6},{5,7},{6,4},{7,5},{8,10},{9,11},{10,... | collective-permute-start | bytes 393224 | tf_op jit(solution)/shard_map/ppermute | solution.py:689
  59.5 1.1 collective-permute-start.2
  60.6 3.4 %tables_one.1 = (bf16[1024,256]{1,0:T(8,128)(2,1)S(1)}, bf16[1024,256]{1,0:T(8,128)(2,1)S(1)}, f32[384,256]{1,0:T(8,128)S(1)}) custom-call(s32[2,2]{1,0:T(2,128)S(1)} %copy-done.10, s32[1,2]{1,0:T(1,128)S(1)} %bitcast.38, f32[2,64,128]{2,1,0:T(8,128)S(1)} %get-tuple-element.141.ids_ref, s32[4,8,1024]{2,1,0:T(8,128)S(1)} %get-tuple-element.149.rows_ref, ...), custom_call_target="tpu_custom_call" | custom-call | flops 2000000000 | bytes 4194304 | tf_op jit(solution)/shard_map/tables_one/pallas_call | solution.py:408
  64.0 1.7 %collective-permute-done.1.c2 = bf16[256,256]{1,0:T(8,128)(2,1)S(1)} collective-permute-done((bf16[256,256]{1,0:T(8,128)(2,1)S(1)}, bf16[256,256]{1,0:T(8,128)(2,1)S(1)}, u32[]{:S(2)}, u32[]{:S(2)}) %collective-permute-start.1) | collective-permute-done | bytes 131104 | tf_op jit(solution)/shard_map/ppermute | solution.py:689
  65.7 3.0 %live.1 = (bf16[1024,256]{1,0:T(8,128)(2,1)S(1)}, f32[256,256]{1,0:T(8,128)S(1)}, f32[104,256]{1,0:T(8,128)S(1)}, bf16[256,256]{1,0:T(8,128)(2,1)}) custom-call(s32[2,2]{1,0:T(2,128)S(1)} %copy-done.10, s32[1,2]{1,0:T(1,128)S(1)} %bitcast.39, bf16[1024,256]{1,0:T(8,128)(2,1)S(1)} %copy-done.3, bf16[1024,256]{1,0:T(8,128)(2,1)S(1)} %copy-done.3, ...), custom_call_target="tpu_custom_call" | custom-call | flops 1600000000 | bytes 4194304 | tf_op jit(solution)/shard_map/live/pallas_call | solution.py:508
  68.7 23.9 %all_to_all.37 = bf16[64,16,256]{2,1,0:T(8,128)(2,1)S(1)} all-to-all(bf16[64,16,256]{2,1,0:T(8,128)(2,1)S(1)} %bitcast.26), channel_id=1, replica_groups=mesh['ent'=64,'rel'=4] {'ent'}, dimensions={0} | all-to-all | bytes 1048576 | tf_op jit(solution)/shard_map/all_to_all | solution.py:685
  93.8 20.8 %all_to_all.38.in_ref = bf16[64,8,384]{2,1,0:T(8,128)(2,1)S(1)} all-to-all(bf16[64,8,384]{2,1,0:T(8,128)(2,1)S(1)} %bitcast.33), channel_id=1, replica_groups=mesh['ent'=64,'rel'=4] {'ent'}, dimensions={0} | all-to-all | bytes 786432 | tf_op jit(solution)/shard_map/all_to_all | solution.py:685
  115.4 6.2 %all-to-all-start.7 = ((bf16[64,8,384]{2,1,0:T(8,128)(2,1)}), bf16[64,8,384]{2,1,0:T(8,128)(2,1)S(1)}, u32[]{:S(2)}, u32[]{:S(2)}) async-start(bf16[64,8,384]{2,1,0:T(8,128)(2,1)} %combine.1), calls=%async_computation.7 | async-start | bytes 786432 | tf_op jit(solution)/shard_map/all_to_all | solution.py:685
  121.6 1.0 collective-permute-start.3
  122.7 2.1 %collective-permute-start.4 = (bf16[256,256]{1,0:T(8,128)(2,1)S(1)}, bf16[256,256]{1,0:T(8,128)(2,1)S(1)}, u32[]{:S(2)}, u32[]{:S(2)}) collective-permute-start(bf16[256,256]{1,0:T(8,128)(2,1)S(1)} %get-tuple-element.173.c0), channel_id=1, source_target_pairs={{0,2},{1,3},{2,0},{3,1},{4,6},{5,7},{6,4},{7,5},{8,10},{9,11},{10,... | collective-permute-start | bytes 393224 | tf_op jit(solution)/shard_map/ppermute | solution.py:689
  124.8 1.3 collective-permute-start.5
  126.1 1.4 %collective-permute-done.3.c1 = bf16[256,256]{1,0:T(8,128)(2,1)S(1)} collective-permute-done((bf16[256,256]{1,0:T(8,128)(2,1)S(1)}, bf16[256,256]{1,0:T(8,128)(2,1)S(1)}, u32[]{:S(2)}, u32[]{:S(2)}) %collective-permute-start.3) | collective-permute-done | bytes 131104 | tf_op jit(solution)/shard_map/ppermute | solution.py:689
  127.5 3.2 %collective-permute-done.4.c2 = bf16[256,256]{1,0:T(8,128)(2,1)S(1)} collective-permute-done((bf16[256,256]{1,0:T(8,128)(2,1)S(1)}, bf16[256,256]{1,0:T(8,128)(2,1)S(1)}, u32[]{:S(2)}, u32[]{:S(2)}) %collective-permute-start.4) | collective-permute-done | bytes 131104 | tf_op jit(solution)/shard_map/ppermute | solution.py:689
  130.7 1.4 %final.1 = bf16[256,256]{1,0:T(8,128)(2,1)} custom-call(s32[2,2]{1,0:T(2,128)S(1)} %copy-done.10, s32[1,2]{1,0:T(1,128)S(1)} %bitcast.41, s32[1]{0:T(128)} %bitcast.7.quarter_ref, f32[1024,256]{1,0:T(8,128)S(1)} %copy-done, f32[256,256]{1,0:T(8,128)S(1)} %get-tuple-element.158.live_ref, bf16[256,256]{1,0:T(8,128)(2,1)S(1)} %get-tuple-element.173.c0, ...), custom_call_target="tpu_custom_call" | custom-call | flops 1000000 | bytes 1048576 | tf_op jit(solution)/shard_map/final/pallas_call | solution.py:654
  132.2 4.0 %all-to-all-done.7 = bf16[64,8,384]{2,1,0:T(8,128)(2,1)S(1)} async-done(((bf16[64,8,384]{2,1,0:T(8,128)(2,1)}), bf16[64,8,384]{2,1,0:T(8,128)(2,1)S(1)}, u32[]{:S(2)}, u32[]{:S(2)}) %all-to-all-start.7) | async-done | bytes 393248 | tf_op jit(solution)/shard_map/all_to_all | solution.py:685
  (41 shorter events, 4.3 us)
Async XLA Ops:
  0.6 16.0 %copy-start.5 = (bf16[2,256,32]{1,2,0:T(8,128)(2,1)S(1)}, bf16[2,256,32]{1,2,0:T(8,128)(2,1)}, u32[]{:S(2)}) copy-start(bf16[2,256,32]{1,2,0:T(8,128)(2,1)} %param.29) | copy-start | bytes 98308
  3.4 57.1 %copy-start.15 = (f32[2,64,128]{2,1,0:T(8,128)}, f32[2,64,128]{2,1,0:T(8,128)S(1)}, u32[]{:S(2)}) copy-start(f32[2,64,128]{2,1,0:T(8,128)S(1)} %get-tuple-element.141.ids_ref) | copy-start | bytes 196612
  3.4 13.2 %copy-start.4 = (bf16[2,64,256]{2,1,0:T(8,128)(2,1)S(1)}, bf16[2,64,256]{2,1,0:T(8,128)(2,1)}, u32[]{:S(2)}) copy-start(bf16[2,64,256]{2,1,0:T(8,128)(2,1)} %w_in_ref.5) | copy-start | bytes 196612
  3.5 13.2 %copy-start.6 = (f32[2,256]{1,0:T(2,128)S(1)}, f32[2,256]{1,0:T(2,128)}, u32[]{:S(2)}) copy-start(f32[2,256]{1,0:T(2,128)} %w_bias_ref.5) | copy-start | bytes 6148
  3.5 22.4 %all-to-all-start.3 = ((f32[64,1,128]{2,1,0:T(1,128)}), f32[64,1,128]{2,1,0:T(1,128)S(1)}, u32[]{:S(2)}, u32[]{:S(2)}) async-start(f32[64,1,128]{2,1,0:T(1,128)} %get-tuple-element.136), calls=%async_computation.3 | async-start | bytes 65536 | tf_op jit(solution)/shard_map/all_to_all | solution.py:685
  27.7 9.5 %copy-start.13 = (bf16[328,256]{1,0:T(8,128)(2,1)S(1)}, bf16[328,256]{1,0:T(8,128)(2,1)}, u32[]{:S(2)}) copy-start(bf16[328,256]{1,0:T(8,128)(2,1)} %table_ref.3) | copy-start | bytes 503812
  27.7 26.8 %all-to-all-start.4 = ((bf16[64,16,256]{2,1,0:T(8,128)(2,1)}), bf16[64,16,256]{2,1,0:T(8,128)(2,1)S(1)}, u32[]{:S(2)}, u32[]{:S(2)}) async-start(bf16[64,16,256]{2,1,0:T(8,128)(2,1)} %bitcast.13), calls=%async_computation.4 | async-start | bytes 1048576 | tf_op jit(solution)/shard_map/all_to_all | solution.py:685
  37.2 0.7 copy-start.10
  37.2 0.7 copy-start.11
  55.4 5.1 %copy-start.12 = (bf16[1024,256]{1,0:T(8,128)(2,1)S(1)}, bf16[1024,256]{1,0:T(8,128)(2,1)}, u32[]{:S(2)}) copy-start(bf16[1024,256]{1,0:T(8,128)(2,1)} %state_b.1) | copy-start | bytes 1572868
  55.5 10.2 %copy-start.3 = (bf16[1024,256]{1,0:T(8,128)(2,1)S(1)}, bf16[1024,256]{1,0:T(8,128)(2,1)}, u32[]{:S(2)}) copy-start(bf16[1024,256]{1,0:T(8,128)(2,1)} %agg_b.1) | copy-start | bytes 1572868
  55.5 10.2 %copy-start.7 = (f32[1024,256]{1,0:T(8,128)S(1)}, f32[1024,256]{1,0:T(8,128)}, u32[]{:S(2)}) copy-start(f32[1024,256]{1,0:T(8,128)} %get-tuple-element.135.up_ref.up_a.up_b) | copy-start | bytes 3145732
  55.5 10.2 %copy-start.8 = (bf16[1024,256]{1,0:T(8,128)(2,1)S(1)}, bf16[1024,256]{1,0:T(8,128)(2,1)}, u32[]{:S(2)}) copy-start(bf16[1024,256]{1,0:T(8,128)(2,1)} %get-tuple-element.157.rest_ref) | copy-start | bytes 1572868
  55.5 10.2 %copy-start.9 = (bf16[1024,256]{1,0:T(8,128)(2,1)S(1)}, bf16[1024,256]{1,0:T(8,128)(2,1)}, u32[]{:S(2)}) copy-start(bf16[1024,256]{1,0:T(8,128)(2,1)} %get-tuple-element.156.live_ref) | copy-start | bytes 1572868
  55.5 8.4 %collective-permute-start = (bf16[256,256]{1,0:T(8,128)(2,1)S(1)}, bf16[256,256]{1,0:T(8,128)(2,1)S(1)}, u32[]{:S(2)}, u32[]{:S(2)}) collective-permute-start(bf16[256,256]{1,0:T(8,128)(2,1)S(1)} %get-tuple-element.183.c0), channel_id=1, source_target_pairs={{0,1},{1,2},{2,3},{3,0},{4,5},{5,6},{6,7},{7,4},{8,9},{9,10},{10,1... | collective-permute-start | bytes 393224 | tf_op jit(solution)/shard_map/ppermute | solution.py:689
  56.9 8.8 %collective-permute-start.1 = (bf16[256,256]{1,0:T(8,128)(2,1)S(1)}, bf16[256,256]{1,0:T(8,128)(2,1)S(1)}, u32[]{:S(2)}, u32[]{:S(2)}) collective-permute-start(bf16[256,256]{1,0:T(8,128)(2,1)S(1)} %get-tuple-element.183.c0), channel_id=1, source_target_pairs={{0,2},{1,3},{2,0},{3,1},{4,6},{5,7},{6,4},{7,5},{8,10},{9,11},{10,... | collective-permute-start | bytes 393224 | tf_op jit(solution)/shard_map/ppermute | solution.py:689
  59.5 6.2 %collective-permute-start.2 = (bf16[256,256]{1,0:T(8,128)(2,1)S(1)}, bf16[256,256]{1,0:T(8,128)(2,1)S(1)}, u32[]{:S(2)}, u32[]{:S(2)}) collective-permute-start(bf16[256,256]{1,0:T(8,128)(2,1)S(1)} %get-tuple-element.183.c0), channel_id=1, source_target_pairs={{0,3},{1,0},{2,1},{3,2},{4,7},{5,4},{6,5},{7,6},{8,11},{9,8},{10,9... | collective-permute-start | bytes 393224 | tf_op jit(solution)/shard_map/ppermute | solution.py:689
  68.7 24.5 %copy-start.1 = (f32[104,256]{1,0:T(8,128)S(1)}, f32[104,256]{1,0:T(8,128)}, u32[]{:S(2)}) copy-start(f32[104,256]{1,0:T(8,128)} %get-tuple-element.166.w2_ref) | copy-start | bytes 319492
  68.7 24.5 %copy-start.2 = (f32[104,256]{1,0:T(8,128)S(1)}, f32[104,256]{1,0:T(8,128)}, u32[]{:S(2)}) copy-start(f32[104,256]{1,0:T(8,128)} %get-tuple-element.167.w1a_ref) | copy-start | bytes 319492
  93.8 37.0 %copy-start = (f32[1024,256]{1,0:T(8,128)S(1)}, f32[1024,256]{1,0:T(8,128)}, u32[]{:S(2)}) copy-start(f32[1024,256]{1,0:T(8,128)} %get-tuple-element.137.next_ref) | copy-start | bytes 3145732
  115.4 20.8 %all-to-all-start.7 = ((bf16[64,8,384]{2,1,0:T(8,128)(2,1)}), bf16[64,8,384]{2,1,0:T(8,128)(2,1)S(1)}, u32[]{:S(2)}, u32[]{:S(2)}) async-start(bf16[64,8,384]{2,1,0:T(8,128)(2,1)} %combine.1), calls=%async_computation.7 | async-start | bytes 786432 | tf_op jit(solution)/shard_map/all_to_all | solution.py:685
  121.6 5.9 %collective-permute-start.3 = (bf16[256,256]{1,0:T(8,128)(2,1)S(1)}, bf16[256,256]{1,0:T(8,128)(2,1)S(1)}, u32[]{:S(2)}, u32[]{:S(2)}) collective-permute-start(bf16[256,256]{1,0:T(8,128)(2,1)S(1)} %get-tuple-element.173.c0), channel_id=1, source_target_pairs={{0,1},{1,2},{2,3},{3,0},{4,5},{5,6},{6,7},{7,4},{8,9},{9,10},{10,1... | collective-permute-start | bytes 393224 | tf_op jit(solution)/shard_map/ppermute | solution.py:689
  122.7 8.0 %collective-permute-start.4 = (bf16[256,256]{1,0:T(8,128)(2,1)S(1)}, bf16[256,256]{1,0:T(8,128)(2,1)S(1)}, u32[]{:S(2)}, u32[]{:S(2)}) collective-permute-start(bf16[256,256]{1,0:T(8,128)(2,1)S(1)} %get-tuple-element.173.c0), channel_id=1, source_target_pairs={{0,2},{1,3},{2,0},{3,1},{4,6},{5,7},{6,4},{7,5},{8,10},{9,11},{10,... | collective-permute-start | bytes 393224 | tf_op jit(solution)/shard_map/ppermute | solution.py:689
  124.8 5.9 %collective-permute-start.5 = (bf16[256,256]{1,0:T(8,128)(2,1)S(1)}, bf16[256,256]{1,0:T(8,128)(2,1)S(1)}, u32[]{:S(2)}, u32[]{:S(2)}) collective-permute-start(bf16[256,256]{1,0:T(8,128)(2,1)S(1)} %get-tuple-element.173.c0), channel_id=1, source_target_pairs={{0,3},{1,0},{2,1},{3,2},{4,7},{5,4},{6,5},{7,6},{8,11},{9,8},{10,9... | collective-permute-start | bytes 393224 | tf_op jit(solution)/shard_map/ppermute | solution.py:689

commit v7 on v6

--- a/solution.py
+++ b/solution.py
@@ -48,9 +48,12 @@
     return pl.CostEstimate(flops=int(flops), bytes_accessed=int(nbytes), transcendentals=int(trans))
 
 
-def slots_kernel(peers, tiles_ref, count_ref, owner_hbm, target_hbm, source_hbm, relation_hbm, request_ref, ids_ref,
-                 owner_ref, target_ref, source_ref, relation_ref, sems):
-    pairs = ((owner_hbm, owner_ref), (target_hbm, target_ref), (source_hbm, source_ref), (relation_hbm, relation_ref))
+def slots_kernel(peers, tiles_hbm, count_hbm, owner_hbm, target_hbm, source_hbm, relation_hbm, request_ref, ids_ref,
+                 tiles_ref, count_ref, owner_ref, target_ref, source_ref, relation_ref, sems):
+    pairs = (
+        (owner_hbm, owner_ref), (source_hbm, source_ref), (tiles_hbm, tiles_ref), (count_hbm, count_ref),
+        (target_hbm, target_ref), (relation_hbm, relation_ref),
+    )
     copies = [pltpu.make_async_copy(a, b, sems.at[i]) for i, (a, b) in enumerate(pairs)]
     for copy in copies:
         copy.start()
@@ -62,7 +65,8 @@
     tile = lax.shift_right_logical(source_ref[...], 7)
     request, tops = [], []
     for hop in (1, 0):
-        live = (tile == tiles_ref[hop, 0]) | ((tile == tiles_ref[hop, 1]) & (count_ref[0, hop] > 1))
+        first, second = tiles_ref[hop:hop + 1, 0:1], tiles_ref[hop:hop + 1, 1:2]
+        live = (tile == first) | ((tile == second) & (count_ref[0:1, hop:hop + 1] > 1))
         own = jnp.where(live, hit, 0.0)
         own_low = own.astype(BF16)
         offset = jnp.zeros((peers, 1), F32)
@@ -107,7 +111,7 @@
         weight = jnp.where(lane == place + base, 32.0, 0.0) + jnp.where(
             lane == place + (base + 32), 1.0, 0.0
         )
-        columns.append(jnp.sum(spread * weight, axis=1, keepdims=True).astype(jnp.int32))
+        columns.append(dot_nn((spread * weight).astype(BF16), jnp.ones((128, 128), BF16)).astype(jnp.int32))
     return columns
 
 
@@ -122,10 +126,11 @@
 
 
 def onehot(column, width):
-    shape = (column.shape[0], width)
-    lane = lax.broadcasted_iota(jnp.int16, shape, 1)
-    hit = lane == jnp.broadcast_to(column, shape).astype(jnp.int16)
-    return jnp.where(hit, jnp.ones((), BF16), jnp.zeros((), BF16))
+    column = column.astype(jnp.int16)
+    lane = lax.broadcasted_iota(jnp.int16, column.shape, 1)
+    one, zero = jnp.ones((), BF16), jnp.zeros((), BF16)
+    parts = [jnp.where(lane == column - t, one, zero) for t in range(0, width, TILE)]
+    return jnp.concatenate(parts, axis=1)
 
 
 def build_weights(layer, w_in_ref, w_bias_ref, w_out_ref, wx_ref, wu_ref, wb_ref):
@@ -211,13 +216,18 @@
 
 def first_kernel(blocks, agg_hbm, state_hbm, up_hbm, w_in_ref, w_bias_ref, w_out_ref,
                  next_hbm, grad_agg, grad_hbm, sums_hbm, wx, wu, wb, acc_in, acc_out, sums_ref,
-                 agg_buf, state_buf, up_buf, next_buf, sems, out_sems):
+                 agg_buf, state_buf, up_buf, next_buf, sems, out_sems, sums_sem):
     rows = agg_hbm.shape[0] // blocks
 
     def copies(step):
         part = pl.ds(pl.multiple_of(step * rows, rows), rows)
         pairs = ((agg_hbm, agg_buf), (state_hbm, state_buf), (up_hbm, up_buf))
         return [pltpu.make_async_copy(a.at[part], b.at[part], sems.at[step, i]) for i, (a, b) in enumerate(pairs)]
+
+    def results(step):
+        part = pl.ds(pl.multiple_of(step * rows, rows), rows)
+        pairs = ((next_buf, next_hbm), (grad_agg, grad_hbm))
+        return [pltpu.make_async_copy(a.at[part], b.at[part], out_sems.at[step, i]) for i, (a, b) in enumerate(pairs)]
 
     for step in range(blocks):
         for copy in copies(step):
@@ -233,14 +243,16 @@
         up_low = up_buf[part, :]
         dense_step(step, agg_buf.at[part], state_buf.at[part], up_low.astype(F32), up_low, wx, wu, wb,
                    acc_in, acc_out, grad_agg, next_buf.at[part])
+        for copy in results(step):
+            copy.start()
 
     store_sums(acc_in, acc_out, sums_ref)
-    pairs = ((next_buf, next_hbm), (grad_agg, grad_hbm), (sums_ref, sums_hbm))
-    copies = [pltpu.make_async_copy(a, b, out_sems.at[i]) for i, (a, b) in enumerate(pairs)]
-    for copy in copies:
-        copy.start()
-    for copy in copies:
-        copy.wait()
+    last = pltpu.make_async_copy(sums_ref, sums_hbm, sums_sem)
+    last.start()
+    for step in range(blocks):
+        for copy in results(step):
+            copy.wait()
+    last.wait()
 
 
 def first_pass(agg, state, up, w_in, w_bias, w_out):
@@ -259,7 +271,8 @@
         scratch_shapes=scratch(WEIGHT_SHAPES + SUM_SHAPES)
         + [pltpu.VMEM((SUM_ROWS, WIDE), F32)]
         + [pltpu.VMEM((rows, feat), BF16)] * 3
-        + [pltpu.VMEM((rows, feat), F32), pltpu.SemaphoreType.DMA((blocks, 3)), pltpu.SemaphoreType.DMA((3,))],
+        + [pltpu.VMEM((rows, feat), F32), pltpu.SemaphoreType.DMA((blocks, 3))]
+        + [pltpu.SemaphoreType.DMA((blocks, 2)), pltpu.SemaphoreType.DMA],
         compiler_params=params(),
         cost_estimate=cost(5.4e9, 4 << 20, 2 << 20),
         name="first",
@@ -344,7 +357,7 @@
 
 
 def as_row(column):
-    return jnp.broadcast_to(column.astype(F32), (column.shape[0], TILE)).T[0:8].astype(jnp.int32)
+    return column.astype(F32).T[0:8].astype(jnp.int32)
 
 
 def onehot_rows(row, width):
@@ -696,13 +709,15 @@
     weights = (update_in, update_bias, jnp.swapaxes(update_out, 1, 2))
     request, ids = pl.pallas_call(
         functools.partial(slots_kernel, peers),
-        in_specs=[SMEM] * 2 + [HBM] * 4,
+        in_specs=[HBM] * 6,
         out_specs=[VMEM] * 2,
         out_shape=[
             jax.ShapeDtypeStruct((peers, 1, 128), F32),
             jax.ShapeDtypeStruct((2, peers, 128), F32),
         ],
-        scratch_shapes=[pltpu.VMEM((1, edges), jnp.int32)] * 4 + [pltpu.SemaphoreType.DMA((4,))],
+        scratch_shapes=[pltpu.VMEM(frontier_tiles.shape, jnp.int32), pltpu.VMEM(count.shape, jnp.int32)]
+        + [pltpu.VMEM((1, edges), jnp.int32)] * 4
+        + [pltpu.SemaphoreType.DMA((6,))],
         compiler_params=params(8 << 20),
         cost_estimate=cost(1e8, 1 << 20),
         name="slots",

time: 138 us -> 137 us (level)
  no operation moved by 1% of the time
where the time goes in v7:
time: 137 us; the launch traced here: 136 us
  blocking collectives  44.7 us (33%)
  starting transfers between devices  38.4 us (28%)
  Pallas kernels  34.2 us (25%)
  waiting for transfers between devices  16.2 us (12%)
  between operations  2.15 us (2%)
    all_to_all x2, blocking collectives, exchange(): lax.all_to_all(chunks, 'ent', split_axis=0, concat_axis=0, tiled=True)  44.7 us
    all_to_all x3, starting transfers between devices, exchange(): lax.all_to_all(chunks, 'ent', split_axis=0, concat_axis=0, tiled=True)  28.9 us
    all_to_all x3, waiting for transfers between devices, exchange(): lax.all_to_all(chunks, 'ent', split_axis=0, concat_axis=0, tiled=True)  10 us
    pallas_call x1, Pallas kernels, rest_pass(): pl.pallas_call(functools.partial(rest_kernel, capacity), grid=(rows // bl...  9.87 us
    ppermute x6, starting transfers between devices, over_rel(): lax.ppermute(part, 'rel', [(i, (i + k) % group_size) for i in range(group...  9.5 us
    pallas_call x1, Pallas kernels, first_pass(): pl.pallas_call(functools.partial(first_kernel, blocks), in_specs=[HBM, HB...  7.98 us
    ppermute x6, waiting for transfers between devices, over_rel(): lax.ppermute(part, 'rel', [(i, (i + k) % group_size) for i in range(group...  6.21 us
    pallas_call x1, Pallas kernels, tables_one(): pl.pallas_call(functools.partial(tables_one_kernel, capacity), grid_spec=...  3.53 us
  transfers between devices with their start and end apart: 9, of which 6 were waited for; matrix products, arithmetic and copies ran while one was open for 0% of the time, Pallas kernels for 18%

profile of v7, /device:TPU:1, one launch (start us, length us, event | category | flops | bytes accessed | tf_op | source)
XLA Modules:
  0.0 136.4 jit_solution(4315461026589906186)
XLA Ops:
  0.6 2.1 %slots.1 = (f32[64,1,128]{2,1,0:T(1,128)}, f32[2,64,128]{2,1,0:T(8,128)S(1)}) custom-call(s32[2,2]{1,0:T(2,128)} %tiles_ref.9, s32[1,2]{1,0:T(1,128)} %bitcast.34, s32[1,1024]{1,0:T(1,128)} %bitcast.43, s32[1,1024]{1,0:T(1,128)} %bitcast.44, s32[1,1024]{1,0:T(1,128)} %bitcast.45, s32[1,1024]{1,0:T(1,128)} %bitcast.46), custom_call_target="tpu_custom_call" | custom-call | flops 100000000 | bytes 1048576 | tf_op jit(solution)/shard_map/slots/pallas_call | solution.py:710
  2.7 13.1 %all-to-all-start.3 = ((f32[64,1,128]{2,1,0:T(1,128)}), f32[64,1,128]{2,1,0:T(1,128)S(1)}, u32[]{:S(2)}, u32[]{:S(2)}) async-start(f32[64,1,128]{2,1,0:T(1,128)} %get-tuple-element.136), calls=%async_computation.3 | async-start | bytes 65536 | tf_op jit(solution)/shard_map/all_to_all | solution.py:698
  15.9 8.0 %first.1 = (f32[1024,256]{1,0:T(8,128)}, bf16[1024,256]{1,0:T(8,128)(2,1)S(1)}, bf16[1024,256]{1,0:T(8,128)(2,1)}, f32[104,256]{1,0:T(8,128)}) custom-call(bf16[1024,256]{1,0:T(8,128)(2,1)} %agg_hbm.1, bf16[1024,256]{1,0:T(8,128)(2,1)} %one_b.1, bf16[1024,256]{1,0:T(8,128)(2,1)} %up_hbm.1, bf16[2,64,256]{2,1,0:T(8,128)(2,1)S(1)} %copy-done.4, ...), custom_call_target="tpu_custom_call" | custom-call | flops 5400000000 | bytes 4194304 | tf_op jit(solution)/shard_map/first/pallas_call | solution.py:261
  23.9 1.2 all-to-all-done.3.asked_ref
  25.1 1.9 %pick.5 = (bf16[1024,256]{1,0:T(8,128)(2,1)}, s32[1]{0:T(128)}, s32[1]{0:T(128)}) custom-call(f32[64,1,128]{2,1,0:T(1,128)S(1)} %all-to-all-done.3.asked_ref, bf16[1024,256]{1,0:T(8,128)(2,1)S(1)} %get-tuple-element.138.grad_agg), custom_call_target="tpu_custom_call" | custom-call | flops 800000000 | bytes 1048576 | tf_op jit(solution)/shard_map/pick/pallas_call | solution.py:292
  27.0 9.2 %all-to-all-start.4 = ((bf16[64,16,256]{2,1,0:T(8,128)(2,1)}), bf16[64,16,256]{2,1,0:T(8,128)(2,1)S(1)}, u32[]{:S(2)}, u32[]{:S(2)}) async-start(bf16[64,16,256]{2,1,0:T(8,128)(2,1)} %bitcast.13), calls=%async_computation.4 | async-start | bytes 1048576 | tf_op jit(solution)/shard_map/all_to_all | solution.py:698
  37.0 2.0 %tables_two.1 = (bf16[1024,256]{1,0:T(8,128)(2,1)S(1)}, s32[4,8,1024]{2,1,0:T(8,128)S(1)}) custom-call(s32[2,2]{1,0:T(2,128)S(1)} %copy-done.10, s32[1,2]{1,0:T(1,128)S(1)} %bitcast.35, f32[2,64,128]{2,1,0:T(8,128)S(1)} %get-tuple-element.141.ids_ref, bf16[328,256]{1,0:T(8,128)(2,1)S(1)} %copy-done.13), custom_call_target="tpu_custom_call" | custom-call | flops 1000000000 | bytes 2097152 | tf_op jit(solution)/shard_map/tables_two/pallas_call | solution.py:387
  39.0 9.9 %rest.1 = (f32[1024,256]{1,0:T(8,128)}, bf16[1024,256]{1,0:T(8,128)(2,1)}, f32[104,256]{1,0:T(8,128)}, bf16[1024,256]{1,0:T(8,128)(2,1)}, bf16[1024,256]{1,0:T(8,128)(2,1)}) custom-call(s32[2,2]{1,0:T(2,128)S(1)} %copy-done.10, s32[1,2]{1,0:T(1,128)S(1)} %bitcast.36, bf16[1024,256]{1,0:T(8,128)(2,1)} %agg_b.1, bf16[1024,256]{1,0:T(8,128)(2,1)} %state_b.1, ...), custom_call_target="tpu_custom_call" | custom-call | flops 5400000000 | bytes 4194304 | tf_op jit(solution)/shard_map/rest/pallas_call | solution.py:338
  48.8 4.7 %all-to-all-done.4 = bf16[64,16,256]{2,1,0:T(8,128)(2,1)S(1)} async-done(((bf16[64,16,256]{2,1,0:T(8,128)(2,1)}), bf16[64,16,256]{2,1,0:T(8,128)(2,1)S(1)}, u32[]{:S(2)}, u32[]{:S(2)}) %all-to-all-start.4) | async-done | bytes 524320 | tf_op jit(solution)/shard_map/all_to_all | solution.py:698
  54.6 1.4 %collective-permute-start = (bf16[256,256]{1,0:T(8,128)(2,1)S(1)}, bf16[256,256]{1,0:T(8,128)(2,1)S(1)}, u32[]{:S(2)}, u32[]{:S(2)}) collective-permute-start(bf16[256,256]{1,0:T(8,128)(2,1)S(1)} %get-tuple-element.183.c0), channel_id=1, source_target_pairs={{0,1},{1,2},{2,3},{3,0},{4,5},{5,6},{6,7},{7,4},{8,9},{9,10},{10,1... | collective-permute-start | bytes 393224 | tf_op jit(solution)/shard_map/ppermute | solution.py:702
  56.0 2.6 %collective-permute-start.1 = (bf16[256,256]{1,0:T(8,128)(2,1)S(1)}, bf16[256,256]{1,0:T(8,128)(2,1)S(1)}, u32[]{:S(2)}, u32[]{:S(2)}) collective-permute-start(bf16[256,256]{1,0:T(8,128)(2,1)S(1)} %get-tuple-element.183.c0), channel_id=1, source_target_pairs={{0,2},{1,3},{2,0},{3,1},{4,6},{5,7},{6,4},{7,5},{8,10},{9,11},{10,... | collective-permute-start | bytes 393224 | tf_op jit(solution)/shard_map/ppermute | solution.py:702
  58.6 1.1 collective-permute-start.2
  59.7 3.5 %tables_one.1 = (bf16[1024,256]{1,0:T(8,128)(2,1)S(1)}, bf16[1024,256]{1,0:T(8,128)(2,1)S(1)}, f32[384,256]{1,0:T(8,128)S(1)}) custom-call(s32[2,2]{1,0:T(2,128)S(1)} %copy-done.10, s32[1,2]{1,0:T(1,128)S(1)} %bitcast.38, f32[2,64,128]{2,1,0:T(8,128)S(1)} %get-tuple-element.141.ids_ref, s32[4,8,1024]{2,1,0:T(8,128)S(1)} %get-tuple-element.149.rows_ref, ...), custom_call_target="tpu_custom_call" | custom-call | flops 2000000000 | bytes 4194304 | tf_op jit(solution)/shard_map/tables_one/pallas_call | solution.py:421
  63.2 1.6 %collective-permute-done.1.c2 = bf16[256,256]{1,0:T(8,128)(2,1)S(1)} collective-permute-done((bf16[256,256]{1,0:T(8,128)(2,1)S(1)}, bf16[256,256]{1,0:T(8,128)(2,1)S(1)}, u32[]{:S(2)}, u32[]{:S(2)}) %collective-permute-start.1) | collective-permute-done | bytes 131104 | tf_op jit(solution)/shard_map/ppermute | solution.py:702
  64.8 3.0 %live.1 = (bf16[1024,256]{1,0:T(8,128)(2,1)S(1)}, f32[256,256]{1,0:T(8,128)S(1)}, f32[104,256]{1,0:T(8,128)S(1)}, bf16[256,256]{1,0:T(8,128)(2,1)}) custom-call(s32[2,2]{1,0:T(2,128)S(1)} %copy-done.10, s32[1,2]{1,0:T(1,128)S(1)} %bitcast.39, bf16[1024,256]{1,0:T(8,128)(2,1)S(1)} %copy-done.3, bf16[1024,256]{1,0:T(8,128)(2,1)S(1)} %copy-done.3, ...), custom_call_target="tpu_custom_call" | custom-call | flops 1600000000 | bytes 4194304 | tf_op jit(solution)/shard_map/live/pallas_call | solution.py:521
  67.8 23.9 %all_to_all.37 = bf16[64,16,256]{2,1,0:T(8,128)(2,1)S(1)} all-to-all(bf16[64,16,256]{2,1,0:T(8,128)(2,1)S(1)} %bitcast.26), channel_id=1, replica_groups=mesh['ent'=64,'rel'=4] {'ent'}, dimensions={0} | all-to-all | bytes 1048576 | tf_op jit(solution)/shard_map/all_to_all | solution.py:698
  92.9 20.8 %all_to_all.38.in_ref = bf16[64,8,384]{2,1,0:T(8,128)(2,1)S(1)} all-to-all(bf16[64,8,384]{2,1,0:T(8,128)(2,1)S(1)} %bitcast.33), channel_id=1, replica_groups=mesh['ent'=64,'rel'=4] {'ent'}, dimensions={0} | all-to-all | bytes 786432 | tf_op jit(solution)/shard_map/all_to_all | solution.py:698
  114.5 6.5 %all-to-all-start.7 = ((bf16[64,8,384]{2,1,0:T(8,128)(2,1)}), bf16[64,8,384]{2,1,0:T(8,128)(2,1)S(1)}, u32[]{:S(2)}, u32[]{:S(2)}) async-start(bf16[64,8,384]{2,1,0:T(8,128)(2,1)} %combine.1), calls=%async_computation.7 | async-start | bytes 786432 | tf_op jit(solution)/shard_map/all_to_all | solution.py:698
  122.1 2.1 %collective-permute-start.4 = (bf16[256,256]{1,0:T(8,128)(2,1)S(1)}, bf16[256,256]{1,0:T(8,128)(2,1)S(1)}, u32[]{:S(2)}, u32[]{:S(2)}) collective-permute-start(bf16[256,256]{1,0:T(8,128)(2,1)S(1)} %get-tuple-element.173.c0), channel_id=1, source_target_pairs={{0,2},{1,3},{2,0},{3,1},{4,6},{5,7},{6,4},{7,5},{8,10},{9,11},{10,... | collective-permute-start | bytes 393224 | tf_op jit(solution)/shard_map/ppermute | solution.py:702
  124.2 1.3 collective-permute-start.5
  125.5 1.5 %collective-permute-done.3.c1 = bf16[256,256]{1,0:T(8,128)(2,1)S(1)} collective-permute-done((bf16[256,256]{1,0:T(8,128)(2,1)S(1)}, bf16[256,256]{1,0:T(8,128)(2,1)S(1)}, u32[]{:S(2)}, u32[]{:S(2)}) %collective-permute-start.3) | collective-permute-done | bytes 131104 | tf_op jit(solution)/shard_map/ppermute | solution.py:702
  126.9 3.2 %collective-permute-done.4.c2 = bf16[256,256]{1,0:T(8,128)(2,1)S(1)} collective-permute-done((bf16[256,256]{1,0:T(8,128)(2,1)S(1)}, bf16[256,256]{1,0:T(8,128)(2,1)S(1)}, u32[]{:S(2)}, u32[]{:S(2)}) %collective-permute-start.4) | collective-permute-done | bytes 131104 | tf_op jit(solution)/shard_map/ppermute | solution.py:702
  130.1 1.4 %final.1 = bf16[256,256]{1,0:T(8,128)(2,1)} custom-call(s32[2,2]{1,0:T(2,128)S(1)} %copy-done.10, s32[1,2]{1,0:T(1,128)S(1)} %bitcast.41, s32[1]{0:T(128)} %bitcast.7.quarter_ref, f32[1024,256]{1,0:T(8,128)S(1)} %copy-done, f32[256,256]{1,0:T(8,128)S(1)} %get-tuple-element.158.live_ref, bf16[256,256]{1,0:T(8,128)(2,1)S(1)} %get-tuple-element.173.c0, ...), custom_call_target="tpu_custom_call" | custom-call | flops 1000000 | bytes 1048576 | tf_op jit(solution)/shard_map/final/pallas_call | solution.py:667
  131.5 4.0 %all-to-all-done.7 = bf16[64,8,384]{2,1,0:T(8,128)(2,1)S(1)} async-done(((bf16[64,8,384]{2,1,0:T(8,128)(2,1)}), bf16[64,8,384]{2,1,0:T(8,128)(2,1)S(1)}, u32[]{:S(2)}, u32[]{:S(2)}) %all-to-all-start.7) | async-done | bytes 393248 | tf_op jit(solution)/shard_map/all_to_all | solution.py:698
  (41 shorter events, 4.3 us)
Async XLA Ops:
  0.6 15.2 %copy-start.5 = (bf16[2,256,32]{1,2,0:T(8,128)(2,1)S(1)}, bf16[2,256,32]{1,2,0:T(8,128)(2,1)}, u32[]{:S(2)}) copy-start(bf16[2,256,32]{1,2,0:T(8,128)(2,1)} %param.29) | copy-start | bytes 98308
  2.7 57.0 %copy-start.15 = (f32[2,64,128]{2,1,0:T(8,128)}, f32[2,64,128]{2,1,0:T(8,128)S(1)}, u32[]{:S(2)}) copy-start(f32[2,64,128]{2,1,0:T(8,128)S(1)} %get-tuple-element.141.ids_ref) | copy-start | bytes 196612
  2.7 13.2 %copy-start.4 = (bf16[2,64,256]{2,1,0:T(8,128)(2,1)S(1)}, bf16[2,64,256]{2,1,0:T(8,128)(2,1)}, u32[]{:S(2)}) copy-start(bf16[2,64,256]{2,1,0:T(8,128)(2,1)} %w_in_ref.5) | copy-start | bytes 196612
  2.7 13.2 %copy-start.6 = (f32[2,256]{1,0:T(2,128)S(1)}, f32[2,256]{1,0:T(2,128)}, u32[]{:S(2)}) copy-start(f32[2,256]{1,0:T(2,128)} %w_bias_ref.5) | copy-start | bytes 6148
  2.7 22.4 %all-to-all-start.3 = ((f32[64,1,128]{2,1,0:T(1,128)}), f32[64,1,128]{2,1,0:T(1,128)S(1)}, u32[]{:S(2)}, u32[]{:S(2)}) async-start(f32[64,1,128]{2,1,0:T(1,128)} %get-tuple-element.136), calls=%async_computation.3 | async-start | bytes 65536 | tf_op jit(solution)/shard_map/all_to_all | solution.py:698
  27.0 9.3 %copy-start.13 = (bf16[328,256]{1,0:T(8,128)(2,1)S(1)}, bf16[328,256]{1,0:T(8,128)(2,1)}, u32[]{:S(2)}) copy-start(bf16[328,256]{1,0:T(8,128)(2,1)} %table_ref.3) | copy-start | bytes 503812
  27.0 26.5 %all-to-all-start.4 = ((bf16[64,16,256]{2,1,0:T(8,128)(2,1)}), bf16[64,16,256]{2,1,0:T(8,128)(2,1)S(1)}, u32[]{:S(2)}, u32[]{:S(2)}) async-start(bf16[64,16,256]{2,1,0:T(8,128)(2,1)} %bitcast.13), calls=%async_computation.4 | async-start | bytes 1048576 | tf_op jit(solution)/shard_map/all_to_all | solution.py:698
  36.3 0.7 copy-start.10
  36.3 0.7 copy-start.11
  54.5 5.2 %copy-start.12 = (bf16[1024,256]{1,0:T(8,128)(2,1)S(1)}, bf16[1024,256]{1,0:T(8,128)(2,1)}, u32[]{:S(2)}) copy-start(bf16[1024,256]{1,0:T(8,128)(2,1)} %state_b.1) | copy-start | bytes 1572868
  54.6 10.2 %copy-start.3 = (bf16[1024,256]{1,0:T(8,128)(2,1)S(1)}, bf16[1024,256]{1,0:T(8,128)(2,1)}, u32[]{:S(2)}) copy-start(bf16[1024,256]{1,0:T(8,128)(2,1)} %agg_b.1) | copy-start | bytes 1572868
  54.6 10.2 %copy-start.7 = (f32[1024,256]{1,0:T(8,128)S(1)}, f32[1024,256]{1,0:T(8,128)}, u32[]{:S(2)}) copy-start(f32[1024,256]{1,0:T(8,128)} %get-tuple-element.135.up_ref.up_a.up_b) | copy-start | bytes 3145732
  54.6 10.2 %copy-start.8 = (bf16[1024,256]{1,0:T(8,128)(2,1)S(1)}, bf16[1024,256]{1,0:T(8,128)(2,1)}, u32[]{:S(2)}) copy-start(bf16[1024,256]{1,0:T(8,128)(2,1)} %get-tuple-element.157.rest_ref) | copy-start | bytes 1572868
  54.6 10.2 %copy-start.9 = (bf16[1024,256]{1,0:T(8,128)(2,1)S(1)}, bf16[1024,256]{1,0:T(8,128)(2,1)}, u32[]{:S(2)}) copy-start(bf16[1024,256]{1,0:T(8,128)(2,1)} %get-tuple-element.156.live_ref) | copy-start | bytes 1572868
  54.6 8.6 %collective-permute-start = (bf16[256,256]{1,0:T(8,128)(2,1)S(1)}, bf16[256,256]{1,0:T(8,128)(2,1)S(1)}, u32[]{:S(2)}, u32[]{:S(2)}) collective-permute-start(bf16[256,256]{1,0:T(8,128)(2,1)S(1)} %get-tuple-element.183.c0), channel_id=1, source_target_pairs={{0,1},{1,2},{2,3},{3,0},{4,5},{5,6},{6,7},{7,4},{8,9},{9,10},{10,1... | collective-permute-start | bytes 393224 | tf_op jit(solution)/shard_map/ppermute | solution.py:702
  56.0 8.8 %collective-permute-start.1 = (bf16[256,256]{1,0:T(8,128)(2,1)S(1)}, bf16[256,256]{1,0:T(8,128)(2,1)S(1)}, u32[]{:S(2)}, u32[]{:S(2)}) collective-permute-start(bf16[256,256]{1,0:T(8,128)(2,1)S(1)} %get-tuple-element.183.c0), channel_id=1, source_target_pairs={{0,2},{1,3},{2,0},{3,1},{4,6},{5,7},{6,4},{7,5},{8,10},{9,11},{10,... | collective-permute-start | bytes 393224 | tf_op jit(solution)/shard_map/ppermute | solution.py:702
  58.6 6.2 %collective-permute-start.2 = (bf16[256,256]{1,0:T(8,128)(2,1)S(1)}, bf16[256,256]{1,0:T(8,128)(2,1)S(1)}, u32[]{:S(2)}, u32[]{:S(2)}) collective-permute-start(bf16[256,256]{1,0:T(8,128)(2,1)S(1)} %get-tuple-element.183.c0), channel_id=1, source_target_pairs={{0,3},{1,0},{2,1},{3,2},{4,7},{5,4},{6,5},{7,6},{8,11},{9,8},{10,9... | collective-permute-start | bytes 393224 | tf_op jit(solution)/shard_map/ppermute | solution.py:702
  67.8 24.5 %copy-start.1 = (f32[104,256]{1,0:T(8,128)S(1)}, f32[104,256]{1,0:T(8,128)}, u32[]{:S(2)}) copy-start(f32[104,256]{1,0:T(8,128)} %get-tuple-element.166.w2_ref) | copy-start | bytes 319492
  67.8 24.5 %copy-start.2 = (f32[104,256]{1,0:T(8,128)S(1)}, f32[104,256]{1,0:T(8,128)}, u32[]{:S(2)}) copy-start(f32[104,256]{1,0:T(8,128)} %get-tuple-element.167.w1a_ref) | copy-start | bytes 319492
  92.9 37.2 %copy-start = (f32[1024,256]{1,0:T(8,128)S(1)}, f32[1024,256]{1,0:T(8,128)}, u32[]{:S(2)}) copy-start(f32[1024,256]{1,0:T(8,128)} %get-tuple-element.137.next_ref) | copy-start | bytes 3145732
  114.5 21.1 %all-to-all-start.7 = ((bf16[64,8,384]{2,1,0:T(8,128)(2,1)}), bf16[64,8,384]{2,1,0:T(8,128)(2,1)S(1)}, u32[]{:S(2)}, u32[]{:S(2)}) async-start(bf16[64,8,384]{2,1,0:T(8,128)(2,1)} %combine.1), calls=%async_computation.7 | async-start | bytes 786432 | tf_op jit(solution)/shard_map/all_to_all | solution.py:698
  121.0 5.9 %collective-permute-start.3 = (bf16[256,256]{1,0:T(8,128)(2,1)S(1)}, bf16[256,256]{1,0:T(8,128)(2,1)S(1)}, u32[]{:S(2)}, u32[]{:S(2)}) collective-permute-start(bf16[256,256]{1,0:T(8,128)(2,1)S(1)} %get-tuple-element.173.c0), channel_id=1, source_target_pairs={{0,1},{1,2},{2,3},{3,0},{4,5},{5,6},{6,7},{7,4},{8,9},{9,10},{10,1... | collective-permute-start | bytes 393224 | tf_op jit(solution)/shard_map/ppermute | solution.py:702
  122.1 8.1 %collective-permute-start.4 = (bf16[256,256]{1,0:T(8,128)(2,1)S(1)}, bf16[256,256]{1,0:T(8,128)(2,1)S(1)}, u32[]{:S(2)}, u32[]{:S(2)}) collective-permute-start(bf16[256,256]{1,0:T(8,128)(2,1)S(1)} %get-tuple-element.173.c0), channel_id=1, source_target_pairs={{0,2},{1,3},{2,0},{3,1},{4,6},{5,7},{6,4},{7,5},{8,10},{9,11},{10,... | collective-permute-start | bytes 393224 | tf_op jit(solution)/shard_map/ppermute | solution.py:702
  124.2 5.9 %collective-permute-start.5 = (bf16[256,256]{1,0:T(8,128)(2,1)S(1)}, bf16[256,256]{1,0:T(8,128)(2,1)S(1)}, u32[]{:S(2)}, u32[]{:S(2)}) collective-permute-start(bf16[256,256]{1,0:T(8,128)(2,1)S(1)} %get-tuple-element.173.c0), channel_id=1, source_target_pairs={{0,3},{1,0},{2,1},{3,2},{4,7},{5,4},{6,5},{7,6},{8,11},{9,8},{10,9... | collective-permute-start | bytes 393224 | tf_op jit(solution)/shard_map/ppermute | solution.py:702

commit v8 on v7

--- a/solution.py
+++ b/solution.py
@@ -279,12 +279,22 @@
     )(in_hbm(agg), in_hbm(state), in_hbm(up), w_in, w_bias, w_out)
 
 
-def pick_kernel(capacity, skip, base, asked_ref, grad_agg, picked_ref, two_ref, any_ref):
+def pick_kernel(capacity, skip, base, asked_ref, grad_agg, picked_hbm, two_ref, any_ref, picked_ref, sems):
     two, one = jnp.max(asked_ref[:, 0, 31:32]), jnp.max(asked_ref[:, 0, 95:96])
     two_ref[0] = (two > capacity).astype(jnp.int32)
     any_ref[0] = (jnp.maximum(two, one) > capacity).astype(jnp.int32)
     asked = slot_columns(asked_ref[:, 0, :], capacity, (base,), skip)[0]
-    pick_rows(asked, grad_agg, picked_ref)
+    chunks = sems.shape[0]
+    step = picked_ref.shape[0] // chunks
+    copies = []
+    for c in range(chunks):
+        part = pl.ds(c * step, step)
+        select = onehot(asked[c * step:(c + 1) * step], grad_agg.shape[0])
+        picked_ref[part, :] = dot_nn(select, grad_agg[...]).astype(BF16)
+        copies.append(pltpu.make_async_copy(picked_ref.at[part], picked_hbm.at[part], sems.at[c]))
+        copies[-1].start()
+    for copy in copies:
+        copy.wait()
 
 
 def pick(capacity, skip, base, asked, grad_agg):
@@ -292,12 +302,13 @@
     return pl.pallas_call(
         functools.partial(pick_kernel, capacity, skip, base),
         in_specs=[VMEM, VMEM],
-        out_specs=[VMEM, SMEM, SMEM],
+        out_specs=[HBM, SMEM, SMEM],
         out_shape=[
-            jax.ShapeDtypeStruct((slots, feat), BF16),
+            pltpu.HBM((slots, feat), BF16),
             jax.ShapeDtypeStruct((1,), jnp.int32),
             jax.ShapeDtypeStruct((1,), jnp.int32),
         ],
+        scratch_shapes=[pltpu.VMEM((slots, feat), BF16), pltpu.SemaphoreType.DMA((4,))],
         compiler_params=params(12 << 20),
         cost_estimate=cost(8e8, 1 << 20),
         name="pick",
@@ -353,7 +364,7 @@
         compiler_params=params(),
         cost_estimate=cost(5.4e9, 4 << 20, 2 << 20),
         name="rest",
-    )(tiles, count, in_hbm(agg), in_hbm(state), in_hbm(up), w_in, w_bias, w_out, asked)
+    )(in_hbm(tiles), in_hbm(count), in_hbm(agg), in_hbm(state), in_hbm(up), w_in, w_bias, w_out, asked)
 
 
 def as_row(column):
@@ -395,7 +406,7 @@
         compiler_params=params(),
         cost_estimate=cost(1e9, 2 << 20),
         name="tables_two",
-    )(tiles, count, ids, table)
+    )(in_hbm(tiles), in_hbm(count), ids, table)
 
 
 def tables_one_kernel(capacity, tiles_ref, count_ref, ids_ref, rows_ref, table_ref, answer_ref,
@@ -435,7 +446,7 @@
         compiler_params=params(),
         cost_estimate=cost(2e9, 4 << 20),
         name="tables_one",
-    )(tiles, count, ids, rows, table, answer, state_one, state_one, state_zero, state_zero)
+    )(in_hbm(tiles), in_hbm(count), ids, rows, table, answer, state_one, state_one, state_zero, state_zero)
 
 
 def extra_kernel(hop, capacity, skip, tiles_ref, count_ref, ids_ref, table_ref, answer_ref, state_a, state_b,
@@ -469,7 +480,7 @@
         compiler_params=params(),
         cost_estimate=cost(1e9, 2 << 20),
         name="extra",
-    )(tiles, count, ids, table, answer, state, state, part)
+    )(in_hbm(tiles), in_hbm(count), ids, table, answer, state, state, part)
 
 
 def contribution_kernel(answer_ref, t_ref, rows_ref, out_ref):
@@ -537,7 +548,7 @@
         compiler_params=params(),
         cost_estimate=cost(1.6e9, 4 << 20, 1 << 19),
         name="live",
-    )(tiles, count, agg, agg, state, state, up, up, *parts, *weights, live, rest)
+    )(in_hbm(tiles), in_hbm(count), agg, agg, state, state, up, up, *parts, *weights, live, rest)
 
 
 def late_kernel(capacity, skip, tiles_ref, count_ref, asked_ref, rest_ref, live_ref, picked_ref):
@@ -557,7 +568,7 @@
         compiler_params=params(),
         cost_estimate=cost(8e8, 1 << 20),
         name="late_pick",
-    )(tiles, count, asked, rest, live)
+    )(in_hbm(tiles), in_hbm(count), asked, rest, live)
 
 
 GAP = SUM_ROWS
@@ -677,7 +688,7 @@
         compiler_params=params(),
         cost_estimate=cost(1e6, 1 << 20),
         name="final",
-    )(tiles, count, quarter_id, after, live, *parts)
+    )(in_hbm(tiles), in_hbm(count), quarter_id, after, live, *parts)
 
 
 def shards(state_zero, state_one, aggregate_one, aggregate_two, cotangent, relation_table, update_in, update_bias,
@@ -726,7 +737,8 @@
 
     upstream_one, grad_agg, grad_kept, sums_two = first_pass(aggregate_two, state_one, cotangent, *weights)
     picked_two, more_two, more_any = pick(regular, 0, 0, asked, grad_agg)
-    more_two, more_any = more_two[0], more_any[0]
+    more_two, more_any = lax.optimization_barrier((more_two[0], more_any[0]))
+    more_two, more_any = more_two > 0, more_any > 0
     answered_two = exchange(picked_two.reshape(peers, regular, feat)).reshape(slots, feat)
     after, rest, sums_rest, live, grad_rest = rest_pass(
         regular, frontier_tiles, count, aggregate_one, state_zero, upstream_one, *weights, asked
@@ -744,7 +756,7 @@
         )
 
     part = contribution(answered_two, edge_table, rows)
-    part = lax.switch(more_two, (lambda part: part, lambda part: over_two(part)[0]), part)
+    part = lax.cond(more_two, lambda part: over_two(part)[0], lambda part: part, part)
     parts = over_rel(part)
     table_one, states_one, relation_two = tables_one(
         regular, frontier_tiles, count, ids, rows, relation_table, answered_two, state_one, state_zero
@@ -772,7 +784,7 @@
         total = packed[:used, :feat].astype(F32) + (first + second)
         return part, packed.at[:used, :feat].set(total.astype(BF16))
 
-    part, packed = lax.switch(more_any, (lambda part, packed: (part, packed), over_any), part, packed)
+    part, packed = lax.cond(more_any, over_any, lambda part, packed: (part, packed), part, packed)
     parts = over_rel(part)
     scale_weights = 1.0 / math.sqrt(block_rows * peers * QUERIES)
     scale_relations = math.sqrt(groups * group_size / (edges * peers * group_size))

time: 137 us -> 137 us (level)
  no operation moved by 1% of the time
where the time goes in v8:
time: 137 us; the launch traced here: 136 us
  blocking collectives  45 us (33%)
  starting transfers between devices  38.3 us (28%)
  Pallas kernels  35.1 us (26%)
  waiting for transfers between devices  15.2 us (11%)
  between operations  2.18 us (2%)
    all_to_all x2, blocking collectives, exchange(): lax.all_to_all(chunks, 'ent', split_axis=0, concat_axis=0, tiled=True)  45 us
    all_to_all x3, starting transfers between devices, exchange(): lax.all_to_all(chunks, 'ent', split_axis=0, concat_axis=0, tiled=True)  28.8 us
    pallas_call x1, Pallas kernels, rest_pass(): pl.pallas_call(functools.partial(rest_kernel, capacity), grid=(rows // bl...  9.89 us
    ppermute x6, starting transfers between devices, over_rel(): lax.ppermute(part, 'rel', [(i, (i + k) % group_size) for i in range(group...  9.5 us
    all_to_all x3, waiting for transfers between devices, exchange(): lax.all_to_all(chunks, 'ent', split_axis=0, concat_axis=0, tiled=True)  9.16 us
    pallas_call x1, Pallas kernels, first_pass(): pl.pallas_call(functools.partial(first_kernel, blocks), in_specs=[HBM, HB...  7.9 us
    ppermute x6, waiting for transfers between devices, over_rel(): lax.ppermute(part, 'rel', [(i, (i + k) % group_size) for i in range(group...  6.07 us
    pallas_call x1, Pallas kernels, tables_one(): pl.pallas_call(functools.partial(tables_one_kernel, capacity), grid_spec=...  3.68 us
  transfers between devices with their start and end apart: 9, of which 6 were waited for; matrix products, arithmetic and copies ran while one was open for 0% of the time, Pallas kernels for 18%

profile of v8, /device:TPU:1, one launch (start us, length us, event | category | flops | bytes accessed | tf_op | source)
XLA Modules:
  0.0 136.0 jit_solution(1201976197470753375)
XLA Ops:
  0.6 2.1 %slots.1 = (f32[64,1,128]{2,1,0:T(1,128)}, f32[2,64,128]{2,1,0:T(8,128)S(1)}) custom-call(s32[2,2]{1,0:T(2,128)} %tiles_ref.9, s32[1,2]{1,0:T(1,128)} %bitcast.37, s32[1,1024]{1,0:T(1,128)} %bitcast.46, s32[1,1024]{1,0:T(1,128)} %bitcast.47, s32[1,1024]{1,0:T(1,128)} %bitcast.48, s32[1,1024]{1,0:T(1,128)} %bitcast.49), custom_call_target="tpu_custom_call" | custom-call | flops 100000000 | bytes 1048576 | tf_op jit(solution)/shard_map/slots/pallas_call | solution.py:721
  2.7 13.1 %all-to-all-start.3 = ((f32[64,1,128]{2,1,0:T(1,128)}), f32[64,1,128]{2,1,0:T(1,128)S(1)}, u32[]{:S(2)}, u32[]{:S(2)}) async-start(f32[64,1,128]{2,1,0:T(1,128)} %get-tuple-element.138), calls=%async_computation.3 | async-start | bytes 65536 | tf_op jit(solution)/shard_map/all_to_all | solution.py:709
  15.9 7.9 %first.1 = (f32[1024,256]{1,0:T(8,128)}, bf16[1024,256]{1,0:T(8,128)(2,1)S(1)}, bf16[1024,256]{1,0:T(8,128)(2,1)}, f32[104,256]{1,0:T(8,128)}) custom-call(bf16[1024,256]{1,0:T(8,128)(2,1)} %agg_hbm.1, bf16[1024,256]{1,0:T(8,128)(2,1)} %one_b.1, bf16[1024,256]{1,0:T(8,128)(2,1)} %up_hbm.1, bf16[2,64,256]{2,1,0:T(8,128)(2,1)S(1)} %copy-done.4, ...), custom_call_target="tpu_custom_call" | custom-call | flops 5400000000 | bytes 4194304 | tf_op jit(solution)/shard_map/first/pallas_call | solution.py:261
  23.8 1.3 all-to-all-done.3.asked_ref
  25.1 2.3 %pick.5 = (bf16[1024,256]{1,0:T(8,128)(2,1)}, s32[1]{0:T(128)}, s32[1]{0:T(128)}) custom-call(f32[64,1,128]{2,1,0:T(1,128)S(1)} %all-to-all-done.3.asked_ref, bf16[1024,256]{1,0:T(8,128)(2,1)S(1)} %get-tuple-element.140.grad_agg), custom_call_target="tpu_custom_call" | custom-call | flops 800000000 | bytes 1048576 | tf_op jit(solution)/shard_map/pick/pallas_call | solution.py:302
  27.5 9.2 %all-to-all-start.4 = ((bf16[64,16,256]{2,1,0:T(8,128)(2,1)}), bf16[64,16,256]{2,1,0:T(8,128)(2,1)S(1)}, u32[]{:S(2)}, u32[]{:S(2)}) async-start(bf16[64,16,256]{2,1,0:T(8,128)(2,1)} %bitcast.34), calls=%async_computation.4 | async-start | bytes 1048576 | tf_op jit(solution)/shard_map/all_to_all | solution.py:709
  36.7 2.1 %tables_two.1 = (bf16[1024,256]{1,0:T(8,128)(2,1)S(1)}, s32[4,8,1024]{2,1,0:T(8,128)S(1)}) custom-call(s32[2,2]{1,0:T(2,128)} %tiles_ref.9, s32[1,2]{1,0:T(1,128)} %bitcast.38, f32[2,64,128]{2,1,0:T(8,128)S(1)} %get-tuple-element.143.ids_ref, bf16[328,256]{1,0:T(8,128)(2,1)S(1)} %copy-done.11), custom_call_target="tpu_custom_call" | custom-call | flops 1000000000 | bytes 2097152 | tf_op jit(solution)/shard_map/tables_two/pallas_call | solution.py:398
  40.1 9.9 %rest.1 = (f32[1024,256]{1,0:T(8,128)}, bf16[1024,256]{1,0:T(8,128)(2,1)}, f32[104,256]{1,0:T(8,128)}, bf16[1024,256]{1,0:T(8,128)(2,1)}, bf16[1024,256]{1,0:T(8,128)(2,1)}) custom-call(s32[2,2]{1,0:T(2,128)} %tiles_ref.9, s32[1,2]{1,0:T(1,128)} %bitcast.39, bf16[1024,256]{1,0:T(8,128)(2,1)} %agg_b.1, bf16[1024,256]{1,0:T(8,128)(2,1)} %state_b.1, ...), custom_call_target="tpu_custom_call" | custom-call | flops 5400000000 | bytes 4194304 | tf_op jit(solution)/shard_map/rest/pallas_call | solution.py:349
  50.0 4.0 %all-to-all-done.4 = bf16[64,16,256]{2,1,0:T(8,128)(2,1)S(1)} async-done(((bf16[64,16,256]{2,1,0:T(8,128)(2,1)}), bf16[64,16,256]{2,1,0:T(8,128)(2,1)S(1)}, u32[]{:S(2)}, u32[]{:S(2)}) %all-to-all-start.4) | async-done | bytes 524320 | tf_op jit(solution)/shard_map/all_to_all | solution.py:709
  54.3 1.4 %collective-permute-start = (bf16[256,256]{1,0:T(8,128)(2,1)S(1)}, bf16[256,256]{1,0:T(8,128)(2,1)S(1)}, u32[]{:S(2)}, u32[]{:S(2)}) collective-permute-start(bf16[256,256]{1,0:T(8,128)(2,1)S(1)} %get-tuple-element.187.c0), channel_id=1, source_target_pairs={{0,1},{1,2},{2,3},{3,0},{4,5},{5,6},{6,7},{7,4},{8,9},{9,10},{10,1... | collective-permute-start | bytes 393224 | tf_op jit(solution)/shard_map/ppermute | solution.py:713
  55.7 2.6 %collective-permute-start.1 = (bf16[256,256]{1,0:T(8,128)(2,1)S(1)}, bf16[256,256]{1,0:T(8,128)(2,1)S(1)}, u32[]{:S(2)}, u32[]{:S(2)}) collective-permute-start(bf16[256,256]{1,0:T(8,128)(2,1)S(1)} %get-tuple-element.187.c0), channel_id=1, source_target_pairs={{0,2},{1,3},{2,0},{3,1},{4,6},{5,7},{6,4},{7,5},{8,10},{9,11},{10,... | collective-permute-start | bytes 393224 | tf_op jit(solution)/shard_map/ppermute | solution.py:713
  58.3 1.1 collective-permute-start.2
  59.4 3.7 %tables_one.1 = (bf16[1024,256]{1,0:T(8,128)(2,1)S(1)}, bf16[1024,256]{1,0:T(8,128)(2,1)S(1)}, f32[384,256]{1,0:T(8,128)S(1)}) custom-call(s32[2,2]{1,0:T(2,128)} %tiles_ref.9, s32[1,2]{1,0:T(1,128)} %bitcast.41, f32[2,64,128]{2,1,0:T(8,128)S(1)} %get-tuple-element.143.ids_ref, s32[4,8,1024]{2,1,0:T(8,128)S(1)} %get-tuple-element.153.rows_ref, ...), custom_call_target="tpu_custom_call" | custom-call | flops 2000000000 | bytes 4194304 | tf_op jit(solution)/shard_map/tables_one/pallas_call | solution.py:432
  63.1 1.4 %collective-permute-done.1.c2 = bf16[256,256]{1,0:T(8,128)(2,1)S(1)} collective-permute-done((bf16[256,256]{1,0:T(8,128)(2,1)S(1)}, bf16[256,256]{1,0:T(8,128)(2,1)S(1)}, u32[]{:S(2)}, u32[]{:S(2)}) %collective-permute-start.1) | collective-permute-done | bytes 131104 | tf_op jit(solution)/shard_map/ppermute | solution.py:713
  64.5 3.1 %live.1 = (bf16[1024,256]{1,0:T(8,128)(2,1)S(1)}, f32[256,256]{1,0:T(8,128)S(1)}, f32[104,256]{1,0:T(8,128)S(1)}, bf16[256,256]{1,0:T(8,128)(2,1)}) custom-call(s32[2,2]{1,0:T(2,128)} %tiles_ref.9, s32[1,2]{1,0:T(1,128)} %bitcast.42, bf16[1024,256]{1,0:T(8,128)(2,1)S(1)} %copy-done.3, bf16[1024,256]{1,0:T(8,128)(2,1)S(1)} %copy-done.3, ...), custom_call_target="tpu_custom_call" | custom-call | flops 1600000000 | bytes 4194304 | tf_op jit(solution)/shard_map/live/pallas_call | solution.py:532
  67.6 24.3 %all_to_all.37 = bf16[64,16,256]{2,1,0:T(8,128)(2,1)S(1)} all-to-all(bf16[64,16,256]{2,1,0:T(8,128)(2,1)S(1)} %bitcast.26), channel_id=1, replica_groups=mesh['ent'=64,'rel'=4] {'ent'}, dimensions={0} | all-to-all | bytes 1048576 | tf_op jit(solution)/shard_map/all_to_all | solution.py:709
  92.5 20.8 %all_to_all.38.in_ref = bf16[64,8,384]{2,1,0:T(8,128)(2,1)S(1)} all-to-all(bf16[64,8,384]{2,1,0:T(8,128)(2,1)S(1)} %bitcast.33), channel_id=1, replica_groups=mesh['ent'=64,'rel'=4] {'ent'}, dimensions={0} | all-to-all | bytes 786432 | tf_op jit(solution)/shard_map/all_to_all | solution.py:709
  114.1 6.5 %all-to-all-start.7 = ((bf16[64,8,384]{2,1,0:T(8,128)(2,1)}), bf16[64,8,384]{2,1,0:T(8,128)(2,1)S(1)}, u32[]{:S(2)}, u32[]{:S(2)}) async-start(bf16[64,8,384]{2,1,0:T(8,128)(2,1)} %combine.1), calls=%async_computation.7 | async-start | bytes 786432 | tf_op jit(solution)/shard_map/all_to_all | solution.py:709
  121.7 2.1 %collective-permute-start.4 = (bf16[256,256]{1,0:T(8,128)(2,1)S(1)}, bf16[256,256]{1,0:T(8,128)(2,1)S(1)}, u32[]{:S(2)}, u32[]{:S(2)}) collective-permute-start(bf16[256,256]{1,0:T(8,128)(2,1)S(1)} %get-tuple-element.177.c0), channel_id=1, source_target_pairs={{0,2},{1,3},{2,0},{3,1},{4,6},{5,7},{6,4},{7,5},{8,10},{9,11},{10,... | collective-permute-start | bytes 393224 | tf_op jit(solution)/shard_map/ppermute | solution.py:713
  123.8 1.3 collective-permute-start.5
  125.1 1.5 %collective-permute-done.3.c1 = bf16[256,256]{1,0:T(8,128)(2,1)S(1)} collective-permute-done((bf16[256,256]{1,0:T(8,128)(2,1)S(1)}, bf16[256,256]{1,0:T(8,128)(2,1)S(1)}, u32[]{:S(2)}, u32[]{:S(2)}) %collective-permute-start.3) | collective-permute-done | bytes 131104 | tf_op jit(solution)/shard_map/ppermute | solution.py:713
  126.5 3.2 %collective-permute-done.4.c2 = bf16[256,256]{1,0:T(8,128)(2,1)S(1)} collective-permute-done((bf16[256,256]{1,0:T(8,128)(2,1)S(1)}, bf16[256,256]{1,0:T(8,128)(2,1)S(1)}, u32[]{:S(2)}, u32[]{:S(2)}) %collective-permute-start.4) | collective-permute-done | bytes 131104 | tf_op jit(solution)/shard_map/ppermute | solution.py:713
  129.7 1.6 %final.1 = bf16[256,256]{1,0:T(8,128)(2,1)} custom-call(s32[2,2]{1,0:T(2,128)} %tiles_ref.9, s32[1,2]{1,0:T(1,128)} %bitcast.44, s32[1]{0:T(128)} %bitcast.7.quarter_ref, f32[1024,256]{1,0:T(8,128)S(1)} %copy-done, f32[256,256]{1,0:T(8,128)S(1)} %get-tuple-element.162.live_ref, bf16[256,256]{1,0:T(8,128)(2,1)S(1)} %get-tuple-element.177.c0, ...), custom_call_target="tpu_custom_call" | custom-call | flops 1000000 | bytes 1048576 | tf_op jit(solution)/shard_map/final/pallas_call | solution.py:678
  131.3 3.9 %all-to-all-done.7 = bf16[64,8,384]{2,1,0:T(8,128)(2,1)S(1)} async-done(((bf16[64,8,384]{2,1,0:T(8,128)(2,1)}), bf16[64,8,384]{2,1,0:T(8,128)(2,1)S(1)}, u32[]{:S(2)}, u32[]{:S(2)}) %all-to-all-start.7) | async-done | bytes 393248 | tf_op jit(solution)/shard_map/all_to_all | solution.py:709
  (37 shorter events, 3.7 us)
Async XLA Ops:
  0.6 15.2 %copy-start.5 = (bf16[2,256,32]{1,2,0:T(8,128)(2,1)S(1)}, bf16[2,256,32]{1,2,0:T(8,128)(2,1)}, u32[]{:S(2)}) copy-start(bf16[2,256,32]{1,2,0:T(8,128)(2,1)} %param.29) | copy-start | bytes 98308
  2.7 56.7 %copy-start.13 = (f32[2,64,128]{2,1,0:T(8,128)}, f32[2,64,128]{2,1,0:T(8,128)S(1)}, u32[]{:S(2)}) copy-start(f32[2,64,128]{2,1,0:T(8,128)S(1)} %get-tuple-element.143.ids_ref) | copy-start | bytes 196612
  2.7 13.2 %copy-start.4 = (bf16[2,64,256]{2,1,0:T(8,128)(2,1)S(1)}, bf16[2,64,256]{2,1,0:T(8,128)(2,1)}, u32[]{:S(2)}) copy-start(bf16[2,64,256]{2,1,0:T(8,128)(2,1)} %w_in_ref.5) | copy-start | bytes 196612
  2.7 13.2 %copy-start.6 = (f32[2,256]{1,0:T(2,128)S(1)}, f32[2,256]{1,0:T(2,128)}, u32[]{:S(2)}) copy-start(f32[2,256]{1,0:T(2,128)} %w_bias_ref.5) | copy-start | bytes 6148
  2.7 22.4 %all-to-all-start.3 = ((f32[64,1,128]{2,1,0:T(1,128)}), f32[64,1,128]{2,1,0:T(1,128)S(1)}, u32[]{:S(2)}, u32[]{:S(2)}) async-start(f32[64,1,128]{2,1,0:T(1,128)} %get-tuple-element.138), calls=%async_computation.3 | async-start | bytes 65536 | tf_op jit(solution)/shard_map/all_to_all | solution.py:709
  27.4 9.2 %copy-start.11 = (bf16[328,256]{1,0:T(8,128)(2,1)S(1)}, bf16[328,256]{1,0:T(8,128)(2,1)}, u32[]{:S(2)}) copy-start(bf16[328,256]{1,0:T(8,128)(2,1)} %table_ref.3) | copy-start | bytes 503812
  27.5 26.5 %all-to-all-start.4 = ((bf16[64,16,256]{2,1,0:T(8,128)(2,1)}), bf16[64,16,256]{2,1,0:T(8,128)(2,1)S(1)}, u32[]{:S(2)}, u32[]{:S(2)}) async-start(bf16[64,16,256]{2,1,0:T(8,128)(2,1)} %bitcast.34), calls=%async_computation.4 | async-start | bytes 1048576 | tf_op jit(solution)/shard_map/all_to_all | solution.py:709
  54.2 5.1 %copy-start.10 = (bf16[1024,256]{1,0:T(8,128)(2,1)S(1)}, bf16[1024,256]{1,0:T(8,128)(2,1)}, u32[]{:S(2)}) copy-start(bf16[1024,256]{1,0:T(8,128)(2,1)} %state_b.1) | copy-start | bytes 1572868
  54.3 10.2 %copy-start.3 = (bf16[1024,256]{1,0:T(8,128)(2,1)S(1)}, bf16[1024,256]{1,0:T(8,128)(2,1)}, u32[]{:S(2)}) copy-start(bf16[1024,256]{1,0:T(8,128)(2,1)} %agg_b.1) | copy-start | bytes 1572868
  54.3 10.2 %copy-start.7 = (f32[1024,256]{1,0:T(8,128)S(1)}, f32[1024,256]{1,0:T(8,128)}, u32[]{:S(2)}) copy-start(f32[1024,256]{1,0:T(8,128)} %get-tuple-element.137.up_ref.up_a.up_b) | copy-start | bytes 3145732
  54.3 10.2 %copy-start.8 = (bf16[1024,256]{1,0:T(8,128)(2,1)S(1)}, bf16[1024,256]{1,0:T(8,128)(2,1)}, u32[]{:S(2)}) copy-start(bf16[1024,256]{1,0:T(8,128)(2,1)} %get-tuple-element.161.rest_ref) | copy-start | bytes 1572868
  54.3 10.2 %copy-start.9 = (bf16[1024,256]{1,0:T(8,128)(2,1)S(1)}, bf16[1024,256]{1,0:T(8,128)(2,1)}, u32[]{:S(2)}) copy-start(bf16[1024,256]{1,0:T(8,128)(2,1)} %get-tuple-element.160.live_ref) | copy-start | bytes 1572868
  54.3 8.8 %collective-permute-start = (bf16[256,256]{1,0:T(8,128)(2,1)S(1)}, bf16[256,256]{1,0:T(8,128)(2,1)S(1)}, u32[]{:S(2)}, u32[]{:S(2)}) collective-permute-start(bf16[256,256]{1,0:T(8,128)(2,1)S(1)} %get-tuple-element.187.c0), channel_id=1, source_target_pairs={{0,1},{1,2},{2,3},{3,0},{4,5},{5,6},{6,7},{7,4},{8,9},{9,10},{10,1... | collective-permute-start | bytes 393224 | tf_op jit(solution)/shard_map/ppermute | solution.py:713
  55.7 8.8 %collective-permute-start.1 = (bf16[256,256]{1,0:T(8,128)(2,1)S(1)}, bf16[256,256]{1,0:T(8,128)(2,1)S(1)}, u32[]{:S(2)}, u32[]{:S(2)}) collective-permute-start(bf16[256,256]{1,0:T(8,128)(2,1)S(1)} %get-tuple-element.187.c0), channel_id=1, source_target_pairs={{0,2},{1,3},{2,0},{3,1},{4,6},{5,7},{6,4},{7,5},{8,10},{9,11},{10,... | collective-permute-start | bytes 393224 | tf_op jit(solution)/shard_map/ppermute | solution.py:713
  58.3 6.2 %collective-permute-start.2 = (bf16[256,256]{1,0:T(8,128)(2,1)S(1)}, bf16[256,256]{1,0:T(8,128)(2,1)S(1)}, u32[]{:S(2)}, u32[]{:S(2)}) collective-permute-start(bf16[256,256]{1,0:T(8,128)(2,1)S(1)} %get-tuple-element.187.c0), channel_id=1, source_target_pairs={{0,3},{1,0},{2,1},{3,2},{4,7},{5,4},{6,5},{7,6},{8,11},{9,8},{10,9... | collective-permute-start | bytes 393224 | tf_op jit(solution)/shard_map/ppermute | solution.py:713
  67.6 24.3 %copy-start.1 = (f32[104,256]{1,0:T(8,128)S(1)}, f32[104,256]{1,0:T(8,128)}, u32[]{:S(2)}) copy-start(f32[104,256]{1,0:T(8,128)} %get-tuple-element.170.w2_ref) | copy-start | bytes 319492
  67.6 24.3 %copy-start.2 = (f32[104,256]{1,0:T(8,128)S(1)}, f32[104,256]{1,0:T(8,128)}, u32[]{:S(2)}) copy-start(f32[104,256]{1,0:T(8,128)} %get-tuple-element.171.w1a_ref) | copy-start | bytes 319492
  92.5 37.2 %copy-start = (f32[1024,256]{1,0:T(8,128)S(1)}, f32[1024,256]{1,0:T(8,128)}, u32[]{:S(2)}) copy-start(f32[1024,256]{1,0:T(8,128)} %get-tuple-element.139.next_ref) | copy-start | bytes 3145732
  114.1 21.1 %all-to-all-start.7 = ((bf16[64,8,384]{2,1,0:T(8,128)(2,1)}), bf16[64,8,384]{2,1,0:T(8,128)(2,1)S(1)}, u32[]{:S(2)}, u32[]{:S(2)}) async-start(bf16[64,8,384]{2,1,0:T(8,128)(2,1)} %combine.1), calls=%async_computation.7 | async-start | bytes 786432 | tf_op jit(solution)/shard_map/all_to_all | solution.py:709
  120.6 5.9 %collective-permute-start.3 = (bf16[256,256]{1,0:T(8,128)(2,1)S(1)}, bf16[256,256]{1,0:T(8,128)(2,1)S(1)}, u32[]{:S(2)}, u32[]{:S(2)}) collective-permute-start(bf16[256,256]{1,0:T(8,128)(2,1)S(1)} %get-tuple-element.177.c0), channel_id=1, source_target_pairs={{0,1},{1,2},{2,3},{3,0},{4,5},{5,6},{6,7},{7,4},{8,9},{9,10},{10,1... | collective-permute-start | bytes 393224 | tf_op jit(solution)/shard_map/ppermute | solution.py:713
  121.7 8.1 %collective-permute-start.4 = (bf16[256,256]{1,0:T(8,128)(2,1)S(1)}, bf16[256,256]{1,0:T(8,128)(2,1)S(1)}, u32[]{:S(2)}, u32[]{:S(2)}) collective-permute-start(bf16[256,256]{1,0:T(8,128)(2,1)S(1)} %get-tuple-element.177.c0), channel_id=1, source_target_pairs={{0,2},{1,3},{2,0},{3,1},{4,6},{5,7},{6,4},{7,5},{8,10},{9,11},{10,... | collective-permute-start | bytes 393224 | tf_op jit(solution)/shard_map/ppermute | solution.py:713
  123.8 5.9 %collective-permute-start.5 = (bf16[256,256]{1,0:T(8,128)(2,1)S(1)}, bf16[256,256]{1,0:T(8,128)(2,1)S(1)}, u32[]{:S(2)}, u32[]{:S(2)}) collective-permute-start(bf16[256,256]{1,0:T(8,128)(2,1)S(1)} %get-tuple-element.177.c0), channel_id=1, source_target_pairs={{0,3},{1,0},{2,1},{3,2},{4,7},{5,4},{6,5},{7,6},{8,11},{9,8},{10,9... | collective-permute-start | bytes 393224 | tf_op jit(solution)/shard_map/ppermute | solution.py:713

commit v9 on v7

--- a/solution.py
+++ b/solution.py
@@ -279,10 +279,9 @@
     )(in_hbm(agg), in_hbm(state), in_hbm(up), w_in, w_bias, w_out)
 
 
-def pick_kernel(capacity, skip, base, asked_ref, grad_agg, picked_ref, two_ref, any_ref):
+def pick_kernel(capacity, skip, base, asked_ref, grad_agg, picked_ref, over_ref):
     two, one = jnp.max(asked_ref[:, 0, 31:32]), jnp.max(asked_ref[:, 0, 95:96])
-    two_ref[0] = (two > capacity).astype(jnp.int32)
-    any_ref[0] = (jnp.maximum(two, one) > capacity).astype(jnp.int32)
+    over_ref[0] = (two > capacity).astype(jnp.int32) + (jnp.maximum(two, one) > capacity).astype(jnp.int32)
     asked = slot_columns(asked_ref[:, 0, :], capacity, (base,), skip)[0]
     pick_rows(asked, grad_agg, picked_ref)
 
@@ -292,10 +291,9 @@
     return pl.pallas_call(
         functools.partial(pick_kernel, capacity, skip, base),
         in_specs=[VMEM, VMEM],
-        out_specs=[VMEM, SMEM, SMEM],
+        out_specs=[VMEM, SMEM],
         out_shape=[
             jax.ShapeDtypeStruct((slots, feat), BF16),
-            jax.ShapeDtypeStruct((1,), jnp.int32),
             jax.ShapeDtypeStruct((1,), jnp.int32),
         ],
         compiler_params=params(12 << 20),
@@ -725,8 +723,9 @@
     asked = exchange(request)
 
     upstream_one, grad_agg, grad_kept, sums_two = first_pass(aggregate_two, state_one, cotangent, *weights)
-    picked_two, more_two, more_any = pick(regular, 0, 0, asked, grad_agg)
-    more_two, more_any = more_two[0], more_any[0]
+    picked_two, code = pick(regular, 0, 0, asked, grad_agg)
+    code = lax.optimization_barrier(lax.optimization_barrier(code[0]) + 1)
+    more_two, more_any = code > 2, code > 1
     answered_two = exchange(picked_two.reshape(peers, regular, feat)).reshape(slots, feat)
     after, rest, sums_rest, live, grad_rest = rest_pass(
         regular, frontier_tiles, count, aggregate_one, state_zero, upstream_one, *weights, asked
@@ -744,7 +743,7 @@
         )
 
     part = contribution(answered_two, edge_table, rows)
-    part = lax.switch(more_two, (lambda part: part, lambda part: over_two(part)[0]), part)
+    part = lax.cond(more_two, lambda part: over_two(part)[0], lambda part: part, part)
     parts = over_rel(part)
     table_one, states_one, relation_two = tables_one(
         regular, frontier_tiles, count, ids, rows, relation_table, answered_two, state_one, state_zero
@@ -772,7 +771,7 @@
         total = packed[:used, :feat].astype(F32) + (first + second)
         return part, packed.at[:used, :feat].set(total.astype(BF16))
 
-    part, packed = lax.switch(more_any, (lambda part, packed: (part, packed), over_any), part, packed)
+    part, packed = lax.cond(more_any, over_any, lambda part, packed: (part, packed), part, packed)
     parts = over_rel(part)
     scale_weights = 1.0 / math.sqrt(block_rows * peers * QUERIES)
     scale_relations = math.sqrt(groups * group_size / (edges * peers * group_size))

time: 137 us -> 136 us (level)
  no operation moved by 1% of the time
where the time goes in v9:
time: 136 us; the launch traced here: 135 us
  blocking collectives  44.9 us (33%)
  starting transfers between devices  38.4 us (28%)
  Pallas kernels  34.2 us (25%)
  waiting for transfers between devices  15.6 us (11%)
  between operations  1.56 us (1%)
    all_to_all x2, blocking collectives, exchange(): lax.all_to_all(chunks, 'ent', split_axis=0, concat_axis=0, tiled=True)  44.9 us
    all_to_all x3, starting transfers between devices, exchange(): lax.all_to_all(chunks, 'ent', split_axis=0, concat_axis=0, tiled=True)  28.9 us
    pallas_call x1, Pallas kernels, rest_pass(): pl.pallas_call(functools.partial(rest_kernel, capacity), grid=(rows // bl...  9.87 us
    ppermute x6, starting transfers between devices, over_rel(): lax.ppermute(part, 'rel', [(i, (i + k) % group_size) for i in range(group...  9.51 us
    all_to_all x3, waiting for transfers between devices, exchange(): lax.all_to_all(chunks, 'ent', split_axis=0, concat_axis=0, tiled=True)  9.35 us
    pallas_call x1, Pallas kernels, first_pass(): pl.pallas_call(functools.partial(first_kernel, blocks), in_specs=[HBM, HB...  7.98 us
    ppermute x6, waiting for transfers between devices, over_rel(): lax.ppermute(part, 'rel', [(i, (i + k) % group_size) for i in range(group...  6.21 us
    pallas_call x1, Pallas kernels, tables_one(): pl.pallas_call(functools.partial(tables_one_kernel, capacity), grid_spec=...  3.54 us
  transfers between devices with their start and end apart: 9, of which 6 were waited for; matrix products, arithmetic and copies ran while one was open for 0% of the time, Pallas kernels for 18%

profile of v9, /device:TPU:1, one launch (start us, length us, event | category | flops | bytes accessed | tf_op | source)
XLA Modules:
  0.0 135.4 jit_solution(7267108341192521884)
XLA Ops:
  0.6 2.1 %slots.1 = (f32[64,1,128]{2,1,0:T(1,128)}, f32[2,64,128]{2,1,0:T(8,128)S(1)}) custom-call(s32[2,2]{1,0:T(2,128)} %tiles_ref.9, s32[1,2]{1,0:T(1,128)} %bitcast.33, s32[1,1024]{1,0:T(1,128)} %bitcast.42, s32[1,1024]{1,0:T(1,128)} %bitcast.43, s32[1,1024]{1,0:T(1,128)} %bitcast.44, s32[1,1024]{1,0:T(1,128)} %bitcast.45), custom_call_target="tpu_custom_call" | custom-call | flops 100000000 | bytes 1048576 | tf_op jit(solution)/shard_map/slots/pallas_call | solution.py:708
  2.7 13.1 %all-to-all-start.3 = ((f32[64,1,128]{2,1,0:T(1,128)}), f32[64,1,128]{2,1,0:T(1,128)S(1)}, u32[]{:S(2)}, u32[]{:S(2)}) async-start(f32[64,1,128]{2,1,0:T(1,128)} %get-tuple-element.135), calls=%async_computation.3 | async-start | bytes 65536 | tf_op jit(solution)/shard_map/all_to_all | solution.py:696
  15.9 8.0 %first.1 = (f32[1024,256]{1,0:T(8,128)}, bf16[1024,256]{1,0:T(8,128)(2,1)S(1)}, bf16[1024,256]{1,0:T(8,128)(2,1)}, f32[104,256]{1,0:T(8,128)}) custom-call(bf16[1024,256]{1,0:T(8,128)(2,1)} %agg_hbm.1, bf16[1024,256]{1,0:T(8,128)(2,1)} %one_b.1, bf16[1024,256]{1,0:T(8,128)(2,1)} %up_hbm.1, bf16[2,64,256]{2,1,0:T(8,128)(2,1)S(1)} %copy-done.4, ...), custom_call_target="tpu_custom_call" | custom-call | flops 5400000000 | bytes 4194304 | tf_op jit(solution)/shard_map/first/pallas_call | solution.py:261
  23.9 1.2 all-to-all-done.3.asked_ref
  25.1 1.9 %pick.5 = (bf16[1024,256]{1,0:T(8,128)(2,1)}, s32[1]{0:T(128)}) custom-call(f32[64,1,128]{2,1,0:T(1,128)S(1)} %all-to-all-done.3.asked_ref, bf16[1024,256]{1,0:T(8,128)(2,1)S(1)} %get-tuple-element.137.grad_agg), custom_call_target="tpu_custom_call" | custom-call | flops 800000000 | bytes 1048576 | tf_op jit(solution)/shard_map/pick/pallas_call | solution.py:291
  27.0 9.2 %all-to-all-start.4 = ((bf16[64,16,256]{2,1,0:T(8,128)(2,1)}), bf16[64,16,256]{2,1,0:T(8,128)(2,1)S(1)}, u32[]{:S(2)}, u32[]{:S(2)}) async-start(bf16[64,16,256]{2,1,0:T(8,128)(2,1)} %bitcast.13), calls=%async_computation.4 | async-start | bytes 1048576 | tf_op jit(solution)/shard_map/all_to_all | solution.py:696
  37.0 2.0 %tables_two.1 = (bf16[1024,256]{1,0:T(8,128)(2,1)S(1)}, s32[4,8,1024]{2,1,0:T(8,128)S(1)}) custom-call(s32[2,2]{1,0:T(2,128)S(1)} %copy-done.10, s32[1,2]{1,0:T(1,128)S(1)} %bitcast.34, f32[2,64,128]{2,1,0:T(8,128)S(1)} %get-tuple-element.140.ids_ref, bf16[328,256]{1,0:T(8,128)(2,1)S(1)} %copy-done.13), custom_call_target="tpu_custom_call" | custom-call | flops 1000000000 | bytes 2097152 | tf_op jit(solution)/shard_map/tables_two/pallas_call | solution.py:385
  39.6 9.9 %rest.1 = (f32[1024,256]{1,0:T(8,128)}, bf16[1024,256]{1,0:T(8,128)(2,1)}, f32[104,256]{1,0:T(8,128)}, bf16[1024,256]{1,0:T(8,128)(2,1)}, bf16[1024,256]{1,0:T(8,128)(2,1)}) custom-call(s32[2,2]{1,0:T(2,128)S(1)} %copy-done.10, s32[1,2]{1,0:T(1,128)S(1)} %bitcast.35, bf16[1024,256]{1,0:T(8,128)(2,1)} %agg_b.1, bf16[1024,256]{1,0:T(8,128)(2,1)} %state_b.1, ...), custom_call_target="tpu_custom_call" | custom-call | flops 5400000000 | bytes 4194304 | tf_op jit(solution)/shard_map/rest/pallas_call | solution.py:336
  49.5 4.1 %all-to-all-done.4 = bf16[64,16,256]{2,1,0:T(8,128)(2,1)S(1)} async-done(((bf16[64,16,256]{2,1,0:T(8,128)(2,1)}), bf16[64,16,256]{2,1,0:T(8,128)(2,1)S(1)}, u32[]{:S(2)}, u32[]{:S(2)}) %all-to-all-start.4) | async-done | bytes 524320 | tf_op jit(solution)/shard_map/all_to_all | solution.py:696
  54.0 1.4 %collective-permute-start = (bf16[256,256]{1,0:T(8,128)(2,1)S(1)}, bf16[256,256]{1,0:T(8,128)(2,1)S(1)}, u32[]{:S(2)}, u32[]{:S(2)}) collective-permute-start(bf16[256,256]{1,0:T(8,128)(2,1)S(1)} %get-tuple-element.181.c0), channel_id=1, source_target_pairs={{0,1},{1,2},{2,3},{3,0},{4,5},{5,6},{6,7},{7,4},{8,9},{9,10},{10,1... | collective-permute-start | bytes 393224 | tf_op jit(solution)/shard_map/ppermute | solution.py:700
  55.3 2.6 %collective-permute-start.1 = (bf16[256,256]{1,0:T(8,128)(2,1)S(1)}, bf16[256,256]{1,0:T(8,128)(2,1)S(1)}, u32[]{:S(2)}, u32[]{:S(2)}) collective-permute-start(bf16[256,256]{1,0:T(8,128)(2,1)S(1)} %get-tuple-element.181.c0), channel_id=1, source_target_pairs={{0,2},{1,3},{2,0},{3,1},{4,6},{5,7},{6,4},{7,5},{8,10},{9,11},{10,... | collective-permute-start | bytes 393224 | tf_op jit(solution)/shard_map/ppermute | solution.py:700
  58.0 1.1 collective-permute-start.2
  59.0 3.5 %tables_one.1 = (bf16[1024,256]{1,0:T(8,128)(2,1)S(1)}, bf16[1024,256]{1,0:T(8,128)(2,1)S(1)}, f32[384,256]{1,0:T(8,128)S(1)}) custom-call(s32[2,2]{1,0:T(2,128)S(1)} %copy-done.10, s32[1,2]{1,0:T(1,128)S(1)} %bitcast.37, f32[2,64,128]{2,1,0:T(8,128)S(1)} %get-tuple-element.140.ids_ref, s32[4,8,1024]{2,1,0:T(8,128)S(1)} %get-tuple-element.147.rows_ref, ...), custom_call_target="tpu_custom_call" | custom-call | flops 2000000000 | bytes 4194304 | tf_op jit(solution)/shard_map/tables_one/pallas_call | solution.py:419
  62.6 1.6 %collective-permute-done.1.c2 = bf16[256,256]{1,0:T(8,128)(2,1)S(1)} collective-permute-done((bf16[256,256]{1,0:T(8,128)(2,1)S(1)}, bf16[256,256]{1,0:T(8,128)(2,1)S(1)}, u32[]{:S(2)}, u32[]{:S(2)}) %collective-permute-start.1) | collective-permute-done | bytes 131104 | tf_op jit(solution)/shard_map/ppermute | solution.py:700
  64.2 3.0 %live.1 = (bf16[1024,256]{1,0:T(8,128)(2,1)S(1)}, f32[256,256]{1,0:T(8,128)S(1)}, f32[104,256]{1,0:T(8,128)S(1)}, bf16[256,256]{1,0:T(8,128)(2,1)}) custom-call(s32[2,2]{1,0:T(2,128)S(1)} %copy-done.10, s32[1,2]{1,0:T(1,128)S(1)} %bitcast.38, bf16[1024,256]{1,0:T(8,128)(2,1)S(1)} %copy-done.3, bf16[1024,256]{1,0:T(8,128)(2,1)S(1)} %copy-done.3, ...), custom_call_target="tpu_custom_call" | custom-call | flops 1600000000 | bytes 4194304 | tf_op jit(solution)/shard_map/live/pallas_call | solution.py:519
  67.1 24.1 %all_to_all.37 = bf16[64,16,256]{2,1,0:T(8,128)(2,1)S(1)} all-to-all(bf16[64,16,256]{2,1,0:T(8,128)(2,1)S(1)} %bitcast.25), channel_id=1, replica_groups=mesh['ent'=64,'rel'=4] {'ent'}, dimensions={0} | all-to-all | bytes 1048576 | tf_op jit(solution)/shard_map/all_to_all | solution.py:696
  91.9 20.8 %all_to_all.38.in_ref = bf16[64,8,384]{2,1,0:T(8,128)(2,1)S(1)} all-to-all(bf16[64,8,384]{2,1,0:T(8,128)(2,1)S(1)} %bitcast.32), channel_id=1, replica_groups=mesh['ent'=64,'rel'=4] {'ent'}, dimensions={0} | all-to-all | bytes 786432 | tf_op jit(solution)/shard_map/all_to_all | solution.py:696
  113.5 6.5 %all-to-all-start.7 = ((bf16[64,8,384]{2,1,0:T(8,128)(2,1)}), bf16[64,8,384]{2,1,0:T(8,128)(2,1)S(1)}, u32[]{:S(2)}, u32[]{:S(2)}) async-start(bf16[64,8,384]{2,1,0:T(8,128)(2,1)} %combine.1), calls=%async_computation.7 | async-start | bytes 786432 | tf_op jit(solution)/shard_map/all_to_all | solution.py:696
  121.0 2.1 %collective-permute-start.4 = (bf16[256,256]{1,0:T(8,128)(2,1)S(1)}, bf16[256,256]{1,0:T(8,128)(2,1)S(1)}, u32[]{:S(2)}, u32[]{:S(2)}) collective-permute-start(bf16[256,256]{1,0:T(8,128)(2,1)S(1)} %get-tuple-element.171.c0), channel_id=1, source_target_pairs={{0,2},{1,3},{2,0},{3,1},{4,6},{5,7},{6,4},{7,5},{8,10},{9,11},{10,... | collective-permute-start | bytes 393224 | tf_op jit(solution)/shard_map/ppermute | solution.py:700
  123.1 1.3 collective-permute-start.5
  124.4 1.5 %collective-permute-done.3.c1 = bf16[256,256]{1,0:T(8,128)(2,1)S(1)} collective-permute-done((bf16[256,256]{1,0:T(8,128)(2,1)S(1)}, bf16[256,256]{1,0:T(8,128)(2,1)S(1)}, u32[]{:S(2)}, u32[]{:S(2)}) %collective-permute-start.3) | collective-permute-done | bytes 131104 | tf_op jit(solution)/shard_map/ppermute | solution.py:700
  125.9 3.2 %collective-permute-done.4.c2 = bf16[256,256]{1,0:T(8,128)(2,1)S(1)} collective-permute-done((bf16[256,256]{1,0:T(8,128)(2,1)S(1)}, bf16[256,256]{1,0:T(8,128)(2,1)S(1)}, u32[]{:S(2)}, u32[]{:S(2)}) %collective-permute-start.4) | collective-permute-done | bytes 131104 | tf_op jit(solution)/shard_map/ppermute | solution.py:700
  129.1 1.4 %final.1 = bf16[256,256]{1,0:T(8,128)(2,1)} custom-call(s32[2,2]{1,0:T(2,128)S(1)} %copy-done.10, s32[1,2]{1,0:T(1,128)S(1)} %bitcast.40, s32[1]{0:T(128)} %bitcast.7.quarter_ref, f32[1024,256]{1,0:T(8,128)S(1)} %copy-done, f32[256,256]{1,0:T(8,128)S(1)} %get-tuple-element.156.live_ref, bf16[256,256]{1,0:T(8,128)(2,1)S(1)} %get-tuple-element.171.c0, ...), custom_call_target="tpu_custom_call" | custom-call | flops 1000000 | bytes 1048576 | tf_op jit(solution)/shard_map/final/pallas_call | solution.py:665
  130.5 4.0 %all-to-all-done.7 = bf16[64,8,384]{2,1,0:T(8,128)(2,1)S(1)} async-done(((bf16[64,8,384]{2,1,0:T(8,128)(2,1)}), bf16[64,8,384]{2,1,0:T(8,128)(2,1)S(1)}, u32[]{:S(2)}, u32[]{:S(2)}) %all-to-all-start.7) | async-done | bytes 393248 | tf_op jit(solution)/shard_map/all_to_all | solution.py:696
  (41 shorter events, 4.3 us)
Async XLA Ops:
  0.6 15.2 %copy-start.5 = (bf16[2,256,32]{1,2,0:T(8,128)(2,1)S(1)}, bf16[2,256,32]{1,2,0:T(8,128)(2,1)}, u32[]{:S(2)}) copy-start(bf16[2,256,32]{1,2,0:T(8,128)(2,1)} %param.29) | copy-start | bytes 98308
  2.7 56.3 %copy-start.15 = (f32[2,64,128]{2,1,0:T(8,128)}, f32[2,64,128]{2,1,0:T(8,128)S(1)}, u32[]{:S(2)}) copy-start(f32[2,64,128]{2,1,0:T(8,128)S(1)} %get-tuple-element.140.ids_ref) | copy-start | bytes 196612
  2.7 13.2 %copy-start.4 = (bf16[2,64,256]{2,1,0:T(8,128)(2,1)S(1)}, bf16[2,64,256]{2,1,0:T(8,128)(2,1)}, u32[]{:S(2)}) copy-start(bf16[2,64,256]{2,1,0:T(8,128)(2,1)} %w_in_ref.5) | copy-start | bytes 196612
  2.7 13.2 %copy-start.6 = (f32[2,256]{1,0:T(2,128)S(1)}, f32[2,256]{1,0:T(2,128)}, u32[]{:S(2)}) copy-start(f32[2,256]{1,0:T(2,128)} %w_bias_ref.5) | copy-start | bytes 6148
  2.7 22.4 %all-to-all-start.3 = ((f32[64,1,128]{2,1,0:T(1,128)}), f32[64,1,128]{2,1,0:T(1,128)S(1)}, u32[]{:S(2)}, u32[]{:S(2)}) async-start(f32[64,1,128]{2,1,0:T(1,128)} %get-tuple-element.135), calls=%async_computation.3 | async-start | bytes 65536 | tf_op jit(solution)/shard_map/all_to_all | solution.py:696
  27.0 9.3 %copy-start.13 = (bf16[328,256]{1,0:T(8,128)(2,1)S(1)}, bf16[328,256]{1,0:T(8,128)(2,1)}, u32[]{:S(2)}) copy-start(bf16[328,256]{1,0:T(8,128)(2,1)} %table_ref.3) | copy-start | bytes 503812
  27.0 26.5 %all-to-all-start.4 = ((bf16[64,16,256]{2,1,0:T(8,128)(2,1)}), bf16[64,16,256]{2,1,0:T(8,128)(2,1)S(1)}, u32[]{:S(2)}, u32[]{:S(2)}) async-start(bf16[64,16,256]{2,1,0:T(8,128)(2,1)} %bitcast.13), calls=%async_computation.4 | async-start | bytes 1048576 | tf_op jit(solution)/shard_map/all_to_all | solution.py:696
  36.3 0.7 copy-start.10
  36.3 0.7 copy-start.11
  53.9 5.2 %copy-start.12 = (bf16[1024,256]{1,0:T(8,128)(2,1)S(1)}, bf16[1024,256]{1,0:T(8,128)(2,1)}, u32[]{:S(2)}) copy-start(bf16[1024,256]{1,0:T(8,128)(2,1)} %state_b.1) | copy-start | bytes 1572868
  53.9 10.2 %copy-start.3 = (bf16[1024,256]{1,0:T(8,128)(2,1)S(1)}, bf16[1024,256]{1,0:T(8,128)(2,1)}, u32[]{:S(2)}) copy-start(bf16[1024,256]{1,0:T(8,128)(2,1)} %agg_b.1) | copy-start | bytes 1572868
  53.9 10.2 %copy-start.7 = (f32[1024,256]{1,0:T(8,128)S(1)}, f32[1024,256]{1,0:T(8,128)}, u32[]{:S(2)}) copy-start(f32[1024,256]{1,0:T(8,128)} %get-tuple-element.134.up_ref.up_a.up_b) | copy-start | bytes 3145732
  53.9 10.2 %copy-start.8 = (bf16[1024,256]{1,0:T(8,128)(2,1)S(1)}, bf16[1024,256]{1,0:T(8,128)(2,1)}, u32[]{:S(2)}) copy-start(bf16[1024,256]{1,0:T(8,128)(2,1)} %get-tuple-element.155.rest_ref) | copy-start | bytes 1572868
  53.9 10.2 %copy-start.9 = (bf16[1024,256]{1,0:T(8,128)(2,1)S(1)}, bf16[1024,256]{1,0:T(8,128)(2,1)}, u32[]{:S(2)}) copy-start(bf16[1024,256]{1,0:T(8,128)(2,1)} %get-tuple-element.154.live_ref) | copy-start | bytes 1572868
  54.0 8.6 %collective-permute-start = (bf16[256,256]{1,0:T(8,128)(2,1)S(1)}, bf16[256,256]{1,0:T(8,128)(2,1)S(1)}, u32[]{:S(2)}, u32[]{:S(2)}) collective-permute-start(bf16[256,256]{1,0:T(8,128)(2,1)S(1)} %get-tuple-element.181.c0), channel_id=1, source_target_pairs={{0,1},{1,2},{2,3},{3,0},{4,5},{5,6},{6,7},{7,4},{8,9},{9,10},{10,1... | collective-permute-start | bytes 393224 | tf_op jit(solution)/shard_map/ppermute | solution.py:700
  55.3 8.8 %collective-permute-start.1 = (bf16[256,256]{1,0:T(8,128)(2,1)S(1)}, bf16[256,256]{1,0:T(8,128)(2,1)S(1)}, u32[]{:S(2)}, u32[]{:S(2)}) collective-permute-start(bf16[256,256]{1,0:T(8,128)(2,1)S(1)} %get-tuple-element.181.c0), channel_id=1, source_target_pairs={{0,2},{1,3},{2,0},{3,1},{4,6},{5,7},{6,4},{7,5},{8,10},{9,11},{10,... | collective-permute-start | bytes 393224 | tf_op jit(solution)/shard_map/ppermute | solution.py:700
  58.0 6.2 %collective-permute-start.2 = (bf16[256,256]{1,0:T(8,128)(2,1)S(1)}, bf16[256,256]{1,0:T(8,128)(2,1)S(1)}, u32[]{:S(2)}, u32[]{:S(2)}) collective-permute-start(bf16[256,256]{1,0:T(8,128)(2,1)S(1)} %get-tuple-element.181.c0), channel_id=1, source_target_pairs={{0,3},{1,0},{2,1},{3,2},{4,7},{5,4},{6,5},{7,6},{8,11},{9,8},{10,9... | collective-permute-start | bytes 393224 | tf_op jit(solution)/shard_map/ppermute | solution.py:700
  67.1 24.1 %copy-start.1 = (f32[104,256]{1,0:T(8,128)S(1)}, f32[104,256]{1,0:T(8,128)}, u32[]{:S(2)}) copy-start(f32[104,256]{1,0:T(8,128)} %get-tuple-element.164.w2_ref) | copy-start | bytes 319492
  67.1 24.1 %copy-start.2 = (f32[104,256]{1,0:T(8,128)S(1)}, f32[104,256]{1,0:T(8,128)}, u32[]{:S(2)}) copy-start(f32[104,256]{1,0:T(8,128)} %get-tuple-element.165.w1a_ref) | copy-start | bytes 319492
  91.8 37.2 %copy-start = (f32[1024,256]{1,0:T(8,128)S(1)}, f32[1024,256]{1,0:T(8,128)}, u32[]{:S(2)}) copy-start(f32[1024,256]{1,0:T(8,128)} %get-tuple-element.136.next_ref) | copy-start | bytes 3145732
  113.5 21.1 %all-to-all-start.7 = ((bf16[64,8,384]{2,1,0:T(8,128)(2,1)}), bf16[64,8,384]{2,1,0:T(8,128)(2,1)S(1)}, u32[]{:S(2)}, u32[]{:S(2)}) async-start(bf16[64,8,384]{2,1,0:T(8,128)(2,1)} %combine.1), calls=%async_computation.7 | async-start | bytes 786432 | tf_op jit(solution)/shard_map/all_to_all | solution.py:696
  120.0 5.9 %collective-permute-start.3 = (bf16[256,256]{1,0:T(8,128)(2,1)S(1)}, bf16[256,256]{1,0:T(8,128)(2,1)S(1)}, u32[]{:S(2)}, u32[]{:S(2)}) collective-permute-start(bf16[256,256]{1,0:T(8,128)(2,1)S(1)} %get-tuple-element.171.c0), channel_id=1, source_target_pairs={{0,1},{1,2},{2,3},{3,0},{4,5},{5,6},{6,7},{7,4},{8,9},{9,10},{10,1... | collective-permute-start | bytes 393224 | tf_op jit(solution)/shard_map/ppermute | solution.py:700
  121.0 8.1 %collective-permute-start.4 = (bf16[256,256]{1,0:T(8,128)(2,1)S(1)}, bf16[256,256]{1,0:T(8,128)(2,1)S(1)}, u32[]{:S(2)}, u32[]{:S(2)}) collective-permute-start(bf16[256,256]{1,0:T(8,128)(2,1)S(1)} %get-tuple-element.171.c0), channel_id=1, source_target_pairs={{0,2},{1,3},{2,0},{3,1},{4,6},{5,7},{6,4},{7,5},{8,10},{9,11},{10,... | collective-permute-start | bytes 393224 | tf_op jit(solution)/shard_map/ppermute | solution.py:700
  123.1 5.9 %collective-permute-start.5 = (bf16[256,256]{1,0:T(8,128)(2,1)S(1)}, bf16[256,256]{1,0:T(8,128)(2,1)S(1)}, u32[]{:S(2)}, u32[]{:S(2)}) collective-permute-start(bf16[256,256]{1,0:T(8,128)(2,1)S(1)} %get-tuple-element.171.c0), channel_id=1, source_target_pairs={{0,3},{1,0},{2,1},{3,2},{4,7},{5,4},{6,5},{7,6},{8,11},{9,8},{10,9... | collective-permute-start | bytes 393224 | tf_op jit(solution)/shard_map/ppermute | solution.py:700
